TPU v7x, 256 devices: a whole 4x4x8 slice. The times are simulated.
256 devices in a mesh: dp: 4 (over y), seq: 64 (over z, x, core).
Axes of the slice: x: 4, y: 4, z: 8, core: 2. Of those that a mesh axis runs over, the one named last changes fastest.
Arguments:
- queries: bfloat16 [4, 8192, 1024], P('dp', 'seq'), may hold values from -6 to 6
- keys: bfloat16 [4, 8192, 1024], P('dp', 'seq'), may hold values from -6 to 6
- values: bfloat16 [4, 8192, 1024], P('dp', 'seq'), may hold values from -6 to 6
- gates: bfloat16 [4, 8192, 1024], P('dp', 'seq'), may hold values from -6 to 6
- cotangent: bfloat16 [4, 8192, 1024], P('dp', 'seq'), may hold values from -16 to 16
- segment: int32 [4, 8192], P('dp'), may hold values from 0 to 31, never falling along the last dimension, each value on 1 to 1024 neighbouring positions
- w_out: bfloat16 [1024, 1024], replicated, may hold values from -0.1875 to 0.1875
Outputs:
- output: bfloat16 [4, 8192, 1024], P('dp', 'seq')
- grad_queries: bfloat16 [4, 8192, 1024], P('dp', 'seq')
- grad_keys: bfloat16 [4, 8192, 1024], P('dp', 'seq')
- grad_values: bfloat16 [4, 8192, 1024], P('dp', 'seq')
- grad_gates: bfloat16 [4, 8192, 1024], P('dp', 'seq')
- grad_w_out: float32 [1024, 1024], P(('dp', 'seq'))
Inputs may be any that keep to these rules, and one draw needn't show every extreme that they name: `segment`: within each replica the user numbers never fall along the tokens; every user has 1 to 1024 tokens, and one user has exactly 1024.
All inputs are finite; a program needn't handle non-finite values.
Results may differ from a plain program's by a relative error of at most 0.0058.
Values may be sent and summed in bfloat16 or wider, within the bound.
No kernel may reach another device: no remote copies, remote signals or barrier semaphores. Data moves between devices by JAX's collectives and lax.ppermute only.
A program may use at most 128 MiB of HBM per device.

v0:
```python
import math

import jax
import jax.numpy as jnp
from jax import lax
from jax.sharding import PartitionSpec as P

HEADS = 8
HOPS = 8


EPS = 1e-05


def from_behind(block, axis, distance):
    devices = range(lax.axis_size(axis))
    route = [(i - distance, i) for i in devices if i - distance in devices]
    return lax.ppermute(block, axis, route)


def silu_slope(scores):
    sigmoid_value = jax.nn.sigmoid(scores)
    return sigmoid_value * (1.0 + scores * (1.0 - sigmoid_value))


def block_pass(query_rows, gate_rows, cotan_rows, w_out, key_rows, value_rows, allowed):
    row_count, features = query_rows.shape
    head_size = features // HEADS
    score_scale = 1.0 / math.sqrt(head_size)
    query_heads = query_rows.reshape(row_count, HEADS, head_size)
    key_heads = key_rows.reshape(-1, HEADS, head_size)
    value_heads = value_rows.reshape(-1, HEADS, head_size)
    scores = (
        jnp.einsum("qhd,khd->hqk", query_heads, key_heads, preferred_element_type=jnp.float32)
        * score_scale
    )
    weights = jnp.where(allowed[None], jax.nn.silu(scores), 0.0).astype(jnp.bfloat16)
    mixed = jnp.einsum(
        "hqk,khd->qhd", weights, value_heads, preferred_element_type=jnp.float32
    ).reshape(row_count, features)
    row_mean = jnp.mean(mixed, axis=-1, keepdims=True)
    centred = mixed - row_mean
    inverse = lax.rsqrt(jnp.mean(centred * centred, axis=-1, keepdims=True) + EPS)
    normed = centred * inverse
    gate_float = gate_rows.astype(jnp.float32)
    gated = (normed * gate_float).astype(jnp.bfloat16)
    output_rows = jnp.dot(gated, w_out, preferred_element_type=jnp.float32).astype(jnp.bfloat16)
    dgated = jnp.einsum("rc,wc->rw", cotan_rows, w_out, preferred_element_type=jnp.float32)
    grad_gate_rows = (dgated * normed).astype(jnp.bfloat16)
    dnormed = dgated * gate_float
    dmixed = inverse * (
        dnormed
        - jnp.mean(dnormed, axis=-1, keepdims=True)
        - normed * jnp.mean(dnormed * normed, axis=-1, keepdims=True)
    )
    dmixed_heads = dmixed.astype(jnp.bfloat16).reshape(row_count, HEADS, head_size)
    dweights = jnp.einsum(
        "qhd,khd->hqk", dmixed_heads, value_heads, preferred_element_type=jnp.float32
    )
    dscores = jnp.where(allowed[None], dweights * silu_slope(scores) * score_scale, 0.0).astype(
        jnp.bfloat16
    )
    dvalue_rows = jnp.einsum(
        "hqk,qhd->khd", weights, dmixed_heads, preferred_element_type=jnp.float32
    ).reshape(-1, features)
    dquery_rows = jnp.einsum(
        "hqk,khd->qhd", dscores, key_heads, preferred_element_type=jnp.float32
    ).reshape(row_count, features)
    dkey_rows = jnp.einsum(
        "hqk,qhd->khd", dscores, query_heads, preferred_element_type=jnp.float32
    ).reshape(-1, features)
    weight_part = jnp.einsum("rw,rc->wc", gated, cotan_rows, preferred_element_type=jnp.float32)
    return (
        output_rows,
        dquery_rows.astype(jnp.bfloat16),
        grad_gate_rows,
        dkey_rows,
        dvalue_rows,
        weight_part,
    )


def shards(queries, keys, values, gates, cotangent, segment, w_out):
    query_rows = queries[0]
    gate_rows = gates[0]
    cotan_rows = cotangent[0]
    segment_ids = segment[0]
    row_count, features = query_rows.shape
    reach_rows = HOPS * row_count
    key_count = reach_rows + row_count
    device_index = lax.axis_index("seq")
    first_row = device_index * row_count
    own_block = jnp.stack([keys[0], values[0]])
    arrived = [own_block]
    moving = own_block
    for distance in range(1, HOPS + 1):
        moving = from_behind(moving, "seq", 1)
        arrived.append(moving)
    ordered = arrived[::-1]
    key_rows = jnp.concatenate([block[0] for block in ordered])
    value_rows = jnp.concatenate([block[1] for block in ordered])
    segment_padded = jnp.concatenate([jnp.full((reach_rows,), -1, jnp.int32), segment_ids])
    key_segment = lax.dynamic_slice_in_dim(segment_padded, first_row, key_count)
    query_segment = lax.dynamic_slice_in_dim(segment_ids, first_row, row_count)
    query_place = first_row + jnp.arange(row_count, dtype=jnp.int32)
    key_place = first_row - reach_rows + jnp.arange(key_count, dtype=jnp.int32)
    allowed = (query_segment[:, None] == key_segment[None, :]) & (
        key_place[None, :] <= query_place[:, None]
    )
    output_rows, dquery_rows, grad_gate_rows, dkey_rows, dvalue_rows, weight_part = block_pass(
        query_rows, gate_rows, cotan_rows, w_out, key_rows, value_rows, allowed
    )
    grads_all = jnp.stack([dkey_rows, dvalue_rows])

    def share_of(distance):
        return grads_all[:, (HOPS - distance) * row_count : (HOPS - distance + 1) * row_count]

    summed = share_of(HOPS)
    for distance in range(HOPS - 1, -1, -1):
        summed = from_behind(summed, "seq", -1) + share_of(distance)
    weight_grad = lax.psum_scatter(weight_part, ("dp", "seq"), scatter_dimension=0, tiled=True)
    return (
        output_rows[None],
        dquery_rows[None],
        summed[0].astype(jnp.bfloat16)[None],
        summed[1].astype(jnp.bfloat16)[None],
        grad_gate_rows[None],
        weight_grad,
    )


def solution(mesh):
    placed = (
        P("dp", "seq", None),
        P("dp", "seq", None),
        P("dp", "seq", None),
        P("dp", "seq", None),
        P("dp", "seq", None),
        P("dp", None),
        P(),
    )
    return jax.shard_map(
        shards,
        mesh=mesh,
        in_specs=placed,
        out_specs=(
            P("dp", "seq", None),
            P("dp", "seq", None),
            P("dp", "seq", None),
            P("dp", "seq", None),
            P("dp", "seq", None),
            P(("dp", "seq"), None),
        ),
        check_vma=False,
    )
```

profile of v0, /device:TPU:128, one launch (start us, length us, event | category | flops | bytes accessed | tf_op | source)
XLA Modules:
  0.0 574.3 jit_solution(16594147862181866420)
XLA Ops:
  11.6 11.9 %collective-permute-done = bf16[2,128,1024]{1,2,0:T(8,128)(2,1)S(1)} collective-permute-done((bf16[2,128,1024]{1,2,0:T(8,128)(2,1)S(1)}, bf16[2,128,1024]{1,2,0:T(8,128)(2,1)S(1)}, u32[]{:S(2)}, u32[]{:S(2)}) %collective-permute-start) | collective-permute-done | bytes 524320 | tf_op jit(solution)/shard_map/ppermute | solution.py:18
  25.4 11.9 %collective-permute-done.1 = bf16[2,128,1024]{1,2,0:T(8,128)(2,1)S(1)} collective-permute-done((bf16[2,128,1024]{1,2,0:T(8,128)(2,1)S(1)}, bf16[2,128,1024]{1,2,0:T(8,128)(2,1)S(1)}, u32[]{:S(2)}, u32[]{:S(2)}) %collective-permute-start.1) | collective-permute-done | bytes 524320 | tf_op jit(solution)/shard_map/ppermute | solution.py:18
  40.0 11.9 %collective-permute-done.2 = bf16[2,128,1024]{1,2,0:T(8,128)(2,1)S(1)} collective-permute-done((bf16[2,128,1024]{1,2,0:T(8,128)(2,1)S(1)}, bf16[2,128,1024]{1,2,0:T(8,128)(2,1)S(1)}, u32[]{:S(2)}, u32[]{:S(2)}) %collective-permute-start.2) | collective-permute-done | bytes 524320 | tf_op jit(solution)/shard_map/ppermute | solution.py:18
  54.6 11.9 %collective-permute-done.3 = bf16[2,128,1024]{1,2,0:T(8,128)(2,1)S(1)} collective-permute-done((bf16[2,128,1024]{1,2,0:T(8,128)(2,1)S(1)}, bf16[2,128,1024]{1,2,0:T(8,128)(2,1)S(1)}, u32[]{:S(2)}, u32[]{:S(2)}) %collective-permute-start.3) | collective-permute-done | bytes 524320 | tf_op jit(solution)/shard_map/ppermute | solution.py:18
  69.9 10.5 %collective-permute-done.4 = bf16[2,128,1024]{1,2,0:T(8,128)(2,1)} collective-permute-done((bf16[2,128,1024]{1,2,0:T(8,128)(2,1)S(1)}, bf16[2,128,1024]{1,2,0:T(8,128)(2,1)}, u32[]{:S(2)}, u32[]{:S(2)}) %collective-permute-start.4) | collective-permute-done | bytes 524320 | tf_op jit(solution)/shard_map/ppermute | solution.py:18
  85.1 9.5 %collective-permute-done.5 = bf16[2,128,1024]{1,2,0:T(8,128)(2,1)} collective-permute-done((bf16[2,128,1024]{1,2,0:T(8,128)(2,1)}, bf16[2,128,1024]{1,2,0:T(8,128)(2,1)}, u32[]{:S(2)}, u32[]{:S(2)}) %collective-permute-start.5) | collective-permute-done | bytes 524320 | tf_op jit(solution)/shard_map/ppermute | solution.py:18
  132.9 4.1 fusion.6
  142.5 4.9 fusion.50
  147.4 2.8 fusion.9
  150.2 3.0 fusion.49
  153.3 6.1 %copy.92 = f32[1,1152,1024]{2,1,0:T(8,128)} copy(f32[1,1152,1024]{1,2,0:T(8,128)} %bitcast.111) | data formatting | bytes 9437184 | tf_op jit(solution)/shard_map/stack;reshape | solution.py:113
  159.3 6.2 %copy.93 = f32[1,1152,1024]{2,1,0:T(8,128)} copy(f32[1,1152,1024]{1,2,0:T(8,128)} %bitcast.110) | data formatting | bytes 9437184 | tf_op jit(solution)/shard_map/stack;reshape | solution.py:113
  167.0 6.1 %collective-permute-start.8 = (f32[2,128,1024]{2,1,0:T(8,128)S(1)}, f32[2,128,1024]{2,1,0:T(8,128)S(1)}, u32[]{:S(2)}, u32[]{:S(2)}) collective-permute-start(f32[2,128,1024]{2,1,0:T(8,128)S(1)} %fusion.13), channel_id=1, source_target_pairs={{1,0},{2,1},{3,2},{4,3},{5,4},{6,5},{7,6},{8,7},{9,8},{10,9},{11,1... | collective-permute-start | bytes 3145736 | tf_op jit(solution)/shard_map/ppermute | solution.py:18
  173.1 12.3 %collective-permute-done.8 = f32[2,128,1024]{2,1,0:T(8,128)S(1)} collective-permute-done((f32[2,128,1024]{2,1,0:T(8,128)S(1)}, f32[2,128,1024]{2,1,0:T(8,128)S(1)}, u32[]{:S(2)}, u32[]{:S(2)}) %collective-permute-start.8) | collective-permute-done | bytes 1048608 | tf_op jit(solution)/shard_map/ppermute | solution.py:18
  185.6 7.1 %collective-permute-start.9 = (f32[2,128,1024]{2,1,0:T(8,128)S(1)}, f32[2,128,1024]{2,1,0:T(8,128)S(1)}, u32[]{:S(2)}, u32[]{:S(2)}) collective-permute-start(f32[2,128,1024]{2,1,0:T(8,128)S(1)} %fusion.15), channel_id=1, source_target_pairs={{1,0},{2,1},{3,2},{4,3},{5,4},{6,5},{7,6},{8,7},{9,8},{10,9},{11,1... | collective-permute-start | bytes 3145736 | tf_op jit(solution)/shard_map/ppermute | solution.py:18
  192.7 12.3 %collective-permute-done.9 = f32[2,128,1024]{2,1,0:T(8,128)S(1)} collective-permute-done((f32[2,128,1024]{2,1,0:T(8,128)S(1)}, f32[2,128,1024]{2,1,0:T(8,128)S(1)}, u32[]{:S(2)}, u32[]{:S(2)}) %collective-permute-start.9) | collective-permute-done | bytes 1048608 | tf_op jit(solution)/shard_map/ppermute | solution.py:18
  205.2 7.1 %collective-permute-start.10 = (f32[2,128,1024]{2,1,0:T(8,128)S(1)}, f32[2,128,1024]{2,1,0:T(8,128)S(1)}, u32[]{:S(2)}, u32[]{:S(2)}) collective-permute-start(f32[2,128,1024]{2,1,0:T(8,128)S(1)} %fusion.17), channel_id=1, source_target_pairs={{1,0},{2,1},{3,2},{4,3},{5,4},{6,5},{7,6},{8,7},{9,8},{10,9},{11,1... | collective-permute-start | bytes 3145736 | tf_op jit(solution)/shard_map/ppermute | solution.py:18
  212.4 12.3 %collective-permute-done.10 = f32[2,128,1024]{2,1,0:T(8,128)S(1)} collective-permute-done((f32[2,128,1024]{2,1,0:T(8,128)S(1)}, f32[2,128,1024]{2,1,0:T(8,128)S(1)}, u32[]{:S(2)}, u32[]{:S(2)}) %collective-permute-start.10) | collective-permute-done | bytes 1048608 | tf_op jit(solution)/shard_map/ppermute | solution.py:18
  224.8 7.1 %collective-permute-start.11 = (f32[2,128,1024]{2,1,0:T(8,128)S(1)}, f32[2,128,1024]{2,1,0:T(8,128)S(1)}, u32[]{:S(2)}, u32[]{:S(2)}) collective-permute-start(f32[2,128,1024]{2,1,0:T(8,128)S(1)} %fusion.19), channel_id=1, source_target_pairs={{1,0},{2,1},{3,2},{4,3},{5,4},{6,5},{7,6},{8,7},{9,8},{10,9},{11,1... | collective-permute-start | bytes 3145736 | tf_op jit(solution)/shard_map/ppermute | solution.py:18
  232.0 12.3 %collective-permute-done.11 = f32[2,128,1024]{2,1,0:T(8,128)S(1)} collective-permute-done((f32[2,128,1024]{2,1,0:T(8,128)S(1)}, f32[2,128,1024]{2,1,0:T(8,128)S(1)}, u32[]{:S(2)}, u32[]{:S(2)}) %collective-permute-start.11) | collective-permute-done | bytes 1048608 | tf_op jit(solution)/shard_map/ppermute | solution.py:18
  244.5 7.1 %collective-permute-start.12 = (f32[2,128,1024]{2,1,0:T(8,128)S(1)}, f32[2,128,1024]{2,1,0:T(8,128)S(1)}, u32[]{:S(2)}, u32[]{:S(2)}) collective-permute-start(f32[2,128,1024]{2,1,0:T(8,128)S(1)} %fusion.21), channel_id=1, source_target_pairs={{1,0},{2,1},{3,2},{4,3},{5,4},{6,5},{7,6},{8,7},{9,8},{10,9},{11,1... | collective-permute-start | bytes 3145736 | tf_op jit(solution)/shard_map/ppermute | solution.py:18
  251.6 12.3 %collective-permute-done.12 = f32[2,128,1024]{2,1,0:T(8,128)S(1)} collective-permute-done((f32[2,128,1024]{2,1,0:T(8,128)S(1)}, f32[2,128,1024]{2,1,0:T(8,128)S(1)}, u32[]{:S(2)}, u32[]{:S(2)}) %collective-permute-start.12) | collective-permute-done | bytes 1048608 | tf_op jit(solution)/shard_map/ppermute | solution.py:18
  265.0 7.3 %collective-permute-start.13 = (f32[2,128,1024]{2,1,0:T(8,128)}, f32[2,128,1024]{2,1,0:T(8,128)}, u32[]{:S(2)}, u32[]{:S(2)}) collective-permute-start(f32[2,128,1024]{2,1,0:T(8,128)} %fusion.23), channel_id=1, source_target_pairs={{1,0},{2,1},{3,2},{4,3},{5,4},{6,5},{7,6},{8,7},{9,8},{10,9},{11,1... | collective-permute-start | bytes 3145736 | tf_op jit(solution)/shard_map/ppermute | solution.py:18
  273.7 11.1 %collective-permute-done.13 = f32[2,128,1024]{2,1,0:T(8,128)} collective-permute-done((f32[2,128,1024]{2,1,0:T(8,128)}, f32[2,128,1024]{2,1,0:T(8,128)}, u32[]{:S(2)}, u32[]{:S(2)}) %collective-permute-start.13) | collective-permute-done | bytes 1048608 | tf_op jit(solution)/shard_map/ppermute | solution.py:18
  284.8 2.7 fusion.25
  287.4 7.1 %collective-permute-start.14 = (f32[2,128,1024]{2,1,0:T(8,128)}, f32[2,128,1024]{2,1,0:T(8,128)}, u32[]{:S(2)}, u32[]{:S(2)}) collective-permute-start(f32[2,128,1024]{2,1,0:T(8,128)} %fusion.25), channel_id=1, source_target_pairs={{1,0},{2,1},{3,2},{4,3},{5,4},{6,5},{7,6},{8,7},{9,8},{10,9},{11,1... | collective-permute-start | bytes 3145736 | tf_op jit(solution)/shard_map/ppermute | solution.py:18
  294.6 2.6 fusion.31
  297.2 9.9 %collective-permute-done.14 = f32[2,128,1024]{2,1,0:T(8,128)} collective-permute-done((f32[2,128,1024]{2,1,0:T(8,128)}, f32[2,128,1024]{2,1,0:T(8,128)}, u32[]{:S(2)}, u32[]{:S(2)}) %collective-permute-start.14) | collective-permute-done | bytes 1048608 | tf_op jit(solution)/shard_map/ppermute | solution.py:18
  307.2 2.8 fusion.12
  310.0 7.2 %collective-permute-start.15 = (f32[2,128,1024]{2,1,0:T(8,128)}, f32[2,128,1024]{2,1,0:T(8,128)}, u32[]{:S(2)}, u32[]{:S(2)}) collective-permute-start(f32[2,128,1024]{2,1,0:T(8,128)} %fusion.12), channel_id=1, source_target_pairs={{1,0},{2,1},{3,2},{4,3},{5,4},{6,5},{7,6},{8,7},{9,8},{10,9},{11,1... | collective-permute-start | bytes 3145736 | tf_op jit(solution)/shard_map/ppermute | solution.py:18
  317.2 3.3 convolution_convert_fusion.1
  322.5 241.0 %all-reduce.4.cloned.1.call-done = f32[1024,1024]{1,0:T(8,128)} async-done(((f32[1024,1024]{1,0:T(8,128)}), f32[1024,1024]{1,0:T(8,128)}) %all-reduce.4.cloned.1.call-update) | async-done | bytes 4194320
  (148 shorter events, 73.5 us)
Async XLA Ops:
  7.2 132.2 %copy-start = (bf16[1024,1024]{1,0:T(8,128)(2,1)S(1)}, bf16[1024,1024]{1,0:T(8,128)(2,1)}, u32[]{:S(2)}) copy-start(bf16[1024,1024]{1,0:T(8,128)(2,1)} %param.13) | copy-start | bytes 6291460
  7.2 62.6 %copy-start.25 = (s32[1,8192]{1,0:T(1,128)S(1)}, s32[1,8192]{1,0:T(1,128)}, u32[]{:S(2)}) copy-start(s32[1,8192]{1,0:T(1,128)} %param.12) | copy-start | bytes 98308
  7.2 556.4 %all-reduce.4.cloned.1.call-start = ((), (), s32[]{:S(2)}) async-start(), calls=%async_computation | async-start | bytes 8388608
  9.7 13.8 %collective-permute-start = (bf16[2,128,1024]{1,2,0:T(8,128)(2,1)S(1)}, bf16[2,128,1024]{1,2,0:T(8,128)(2,1)S(1)}, u32[]{:S(2)}, u32[]{:S(2)}) collective-permute-start(bf16[2,128,1024]{1,2,0:T(8,128)(2,1)S(1)} %pad_maximum_fusion.1), channel_id=1, source_target_pairs={{0,1},{1,2},{2,3},{3,4},{4,5},{5,6},{6,7},{7,8},{8,9},{9,10},{10,1... | collective-permute-start | bytes 1572872 | tf_op jit(solution)/shard_map/ppermute | solution.py:18
  23.5 13.8 %collective-permute-start.1 = (bf16[2,128,1024]{1,2,0:T(8,128)(2,1)S(1)}, bf16[2,128,1024]{1,2,0:T(8,128)(2,1)S(1)}, u32[]{:S(2)}, u32[]{:S(2)}) collective-permute-start(bf16[2,128,1024]{1,2,0:T(8,128)(2,1)S(1)} %collective-permute-done), channel_id=1, source_target_pairs={{0,1},{1,2},{2,3},{3,4},{4,5},{5,6},{6,7},{7,8},{8,9},{9,10},{10,1... | collective-permute-start | bytes 1572872 | tf_op jit(solution)/shard_map/ppermute | solution.py:18
  38.1 13.8 %collective-permute-start.2 = (bf16[2,128,1024]{1,2,0:T(8,128)(2,1)S(1)}, bf16[2,128,1024]{1,2,0:T(8,128)(2,1)S(1)}, u32[]{:S(2)}, u32[]{:S(2)}) collective-permute-start(bf16[2,128,1024]{1,2,0:T(8,128)(2,1)S(1)} %collective-permute-done.1), channel_id=1, source_target_pairs={{0,1},{1,2},{2,3},{3,4},{4,5},{5,6},{6,7},{7,8},{8,9},{9,10},{10,1... | collective-permute-start | bytes 1572872 | tf_op jit(solution)/shard_map/ppermute | solution.py:18
  52.7 13.8 %collective-permute-start.3 = (bf16[2,128,1024]{1,2,0:T(8,128)(2,1)S(1)}, bf16[2,128,1024]{1,2,0:T(8,128)(2,1)S(1)}, u32[]{:S(2)}, u32[]{:S(2)}) collective-permute-start(bf16[2,128,1024]{1,2,0:T(8,128)(2,1)S(1)} %collective-permute-done.2), channel_id=1, source_target_pairs={{0,1},{1,2},{2,3},{3,4},{4,5},{5,6},{6,7},{7,8},{8,9},{9,10},{10,1... | collective-permute-start | bytes 1572872 | tf_op jit(solution)/shard_map/ppermute | solution.py:18
  66.5 15.8 %copy-start.23 = (bf16[2,128,1024]{1,2,0:T(8,128)(2,1)}, bf16[2,128,1024]{1,2,0:T(8,128)(2,1)S(1)}, u32[]{:S(2)}) copy-start(bf16[2,128,1024]{1,2,0:T(8,128)(2,1)S(1)} %collective-permute-done.3) | copy-start | bytes 1572868
  66.5 13.9 %collective-permute-start.4 = (bf16[2,128,1024]{1,2,0:T(8,128)(2,1)S(1)}, bf16[2,128,1024]{1,2,0:T(8,128)(2,1)}, u32[]{:S(2)}, u32[]{:S(2)}) collective-permute-start(bf16[2,128,1024]{1,2,0:T(8,128)(2,1)S(1)} %collective-permute-done.3), channel_id=1, source_target_pairs={{0,1},{1,2},{2,3},{3,4},{4,5},{5,6},{6,7},{7,8},{8,9},{9,10},{10,1... | collective-permute-start | bytes 1572872 | tf_op jit(solution)/shard_map/ppermute | solution.py:18
  69.8 63.2 %copy-start.10 = (bf16[1,128,1024]{1,2,0:T(8,128)(2,1)}, bf16[1,128,1024]{1,2,0:T(8,128)(2,1)S(1)}, u32[]{:S(2)}) copy-start(bf16[1,128,1024]{1,2,0:T(8,128)(2,1)S(1)} %copy.103) | copy-start | bytes 786436
  80.4 14.1 %collective-permute-start.5 = (bf16[2,128,1024]{1,2,0:T(8,128)(2,1)}, bf16[2,128,1024]{1,2,0:T(8,128)(2,1)}, u32[]{:S(2)}, u32[]{:S(2)}) collective-permute-start(bf16[2,128,1024]{1,2,0:T(8,128)(2,1)} %collective-permute-done.4), channel_id=1, source_target_pairs={{0,1},{1,2},{2,3},{3,4},{4,5},{5,6},{6,7},{7,8},{8,9},{9,10},{10,1... | collective-permute-start | bytes 1572872 | tf_op jit(solution)/shard_map/ppermute | solution.py:18
  94.6 14.1 %collective-permute-start.6 = (bf16[2,128,1024]{1,2,0:T(8,128)(2,1)}, bf16[2,128,1024]{1,2,0:T(8,128)(2,1)}, u32[]{:S(2)}, u32[]{:S(2)}) collective-permute-start(bf16[2,128,1024]{1,2,0:T(8,128)(2,1)} %collective-permute-done.5), channel_id=1, source_target_pairs={{0,1},{1,2},{2,3},{3,4},{4,5},{5,6},{6,7},{7,8},{8,9},{9,10},{10,1... | collective-permute-start | bytes 1572872 | tf_op jit(solution)/shard_map/ppermute | solution.py:18
  108.7 14.1 %collective-permute-start.7 = (bf16[2,128,1024]{1,2,0:T(8,128)(2,1)}, bf16[2,128,1024]{1,2,0:T(8,128)(2,1)}, u32[]{:S(2)}, u32[]{:S(2)}) collective-permute-start(bf16[2,128,1024]{1,2,0:T(8,128)(2,1)} %collective-permute-done.6), channel_id=1, source_target_pairs={{0,1},{1,2},{2,3},{3,4},{4,5},{5,6},{6,7},{7,8},{8,9},{9,10},{10,1... | collective-permute-start | bytes 1572872 | tf_op jit(solution)/shard_map/ppermute | solution.py:18
  126.5 5.3 copy-start.20
  126.5 5.4 copy-start.19
  126.5 5.5 copy-start.18
  126.5 5.6 copy-start.17
  142.5 4.9 copy-start.8
  159.3 26.1 %slice-start = ((s8[4718592]{0:T(1024)(128)(4,1)}), s8[524288]{0:T(1024)(128)(4,1)S(1)}, s32[]{:S(2)}) async-start(s8[4718592]{0:T(1024)(128)(4,1)} %bitcast.108), calls=%async_computation.1 | async-start | bytes 1048576
  165.5 19.9 %slice-start.1 = ((s8[4718592]{0:T(1024)(128)(4,1)}), s8[4194304]{0:T(1024)(128)(4,1)S(1)}, s32[]{:S(2)}) async-start(s8[4718592]{0:T(1024)(128)(4,1)} %bitcast.108), calls=%async_computation.2 | async-start | bytes 8388608
  165.5 19.9 %copy-start.1 = (f32[1,1152,1024]{2,1,0:T(8,128)S(1)}, f32[1,1152,1024]{2,1,0:T(8,128)}, u32[]{:S(2)}) copy-start(f32[1,1152,1024]{2,1,0:T(8,128)} %copy.93) | copy-start | bytes 14155780
  167.0 18.4 %collective-permute-start.8 = (f32[2,128,1024]{2,1,0:T(8,128)S(1)}, f32[2,128,1024]{2,1,0:T(8,128)S(1)}, u32[]{:S(2)}, u32[]{:S(2)}) collective-permute-start(f32[2,128,1024]{2,1,0:T(8,128)S(1)} %fusion.13), channel_id=1, source_target_pairs={{1,0},{2,1},{3,2},{4,3},{5,4},{6,5},{7,6},{8,7},{9,8},{10,9},{11,1... | collective-permute-start | bytes 3145736 | tf_op jit(solution)/shard_map/ppermute | solution.py:18
  185.6 19.4 %collective-permute-start.9 = (f32[2,128,1024]{2,1,0:T(8,128)S(1)}, f32[2,128,1024]{2,1,0:T(8,128)S(1)}, u32[]{:S(2)}, u32[]{:S(2)}) collective-permute-start(f32[2,128,1024]{2,1,0:T(8,128)S(1)} %fusion.15), channel_id=1, source_target_pairs={{1,0},{2,1},{3,2},{4,3},{5,4},{6,5},{7,6},{8,7},{9,8},{10,9},{11,1... | collective-permute-start | bytes 3145736 | tf_op jit(solution)/shard_map/ppermute | solution.py:18
  205.2 19.4 %collective-permute-start.10 = (f32[2,128,1024]{2,1,0:T(8,128)S(1)}, f32[2,128,1024]{2,1,0:T(8,128)S(1)}, u32[]{:S(2)}, u32[]{:S(2)}) collective-permute-start(f32[2,128,1024]{2,1,0:T(8,128)S(1)} %fusion.17), channel_id=1, source_target_pairs={{1,0},{2,1},{3,2},{4,3},{5,4},{6,5},{7,6},{8,7},{9,8},{10,9},{11,1... | collective-permute-start | bytes 3145736 | tf_op jit(solution)/shard_map/ppermute | solution.py:18
  224.8 19.4 %collective-permute-start.11 = (f32[2,128,1024]{2,1,0:T(8,128)S(1)}, f32[2,128,1024]{2,1,0:T(8,128)S(1)}, u32[]{:S(2)}, u32[]{:S(2)}) collective-permute-start(f32[2,128,1024]{2,1,0:T(8,128)S(1)} %fusion.19), channel_id=1, source_target_pairs={{1,0},{2,1},{3,2},{4,3},{5,4},{6,5},{7,6},{8,7},{9,8},{10,9},{11,1... | collective-permute-start | bytes 3145736 | tf_op jit(solution)/shard_map/ppermute | solution.py:18
  244.5 28.1 %copy-start.28 = (f32[128]{0:T(128)S(1)}, f32[128]{0:T(128)}, u32[]{:S(2)}) copy-start(f32[128]{0:T(128)} %copy-done.26) | copy-start | bytes 1540
  244.5 28.0 %copy-start.30 = (f32[128]{0:T(128)S(1)}, f32[128]{0:T(128)}, u32[]{:S(2)}) copy-start(f32[128]{0:T(128)} %add_rsqrt_fusion) | copy-start | bytes 1540
  244.5 19.4 %collective-permute-start.12 = (f32[2,128,1024]{2,1,0:T(8,128)S(1)}, f32[2,128,1024]{2,1,0:T(8,128)S(1)}, u32[]{:S(2)}, u32[]{:S(2)}) collective-permute-start(f32[2,128,1024]{2,1,0:T(8,128)S(1)} %fusion.21), channel_id=1, source_target_pairs={{1,0},{2,1},{3,2},{4,3},{5,4},{6,5},{7,6},{8,7},{9,8},{10,9},{11,1... | collective-permute-start | bytes 3145736 | tf_op jit(solution)/shard_map/ppermute | solution.py:18
  265.0 19.7 %collective-permute-start.13 = (f32[2,128,1024]{2,1,0:T(8,128)}, f32[2,128,1024]{2,1,0:T(8,128)}, u32[]{:S(2)}, u32[]{:S(2)}) collective-permute-start(f32[2,128,1024]{2,1,0:T(8,128)} %fusion.23), channel_id=1, source_target_pairs={{1,0},{2,1},{3,2},{4,3},{5,4},{6,5},{7,6},{8,7},{9,8},{10,9},{11,1... | collective-permute-start | bytes 3145736 | tf_op jit(solution)/shard_map/ppermute | solution.py:18
  273.7 20.9 %copy-start.9 = (bf16[1,128,1024]{2,1,0:T(8,128)(2,1)S(1)}, bf16[1,128,1024]{2,1,0:T(8,128)(2,1)}, u32[]{:S(2)}) copy-start(bf16[1,128,1024]{2,1,0:T(8,128)(2,1)} %param.11) | copy-start | bytes 786436
  287.4 19.7 %collective-permute-start.14 = (f32[2,128,1024]{2,1,0:T(8,128)}, f32[2,128,1024]{2,1,0:T(8,128)}, u32[]{:S(2)}, u32[]{:S(2)}) collective-permute-start(f32[2,128,1024]{2,1,0:T(8,128)} %fusion.25), channel_id=1, source_target_pairs={{1,0},{2,1},{3,2},{4,3},{5,4},{6,5},{7,6},{8,7},{9,8},{10,9},{11,1... | collective-permute-start | bytes 3145736 | tf_op jit(solution)/shard_map/ppermute | solution.py:18
  310.0 255.0 %collective-permute-start.15 = (f32[2,128,1024]{2,1,0:T(8,128)}, f32[2,128,1024]{2,1,0:T(8,128)}, u32[]{:S(2)}, u32[]{:S(2)}) collective-permute-start(f32[2,128,1024]{2,1,0:T(8,128)} %fusion.12), channel_id=1, source_target_pairs={{1,0},{2,1},{3,2},{4,3},{5,4},{6,5},{7,6},{8,7},{9,8},{10,9},{11,1... | collective-permute-start | bytes 3145736 | tf_op jit(solution)/shard_map/ppermute | solution.py:18
  (19 other events, 48.1 us)
Sparse Core Ops, SparseCore 0:
  297.4 266.1 all-reduce.3
where the time goes:
time: 579 us; the launch traced here: 574 us
  waiting for transfers between devices  394 us (68%)
  starting transfers between devices  71.8 us (12%)
  local copies, waits for them, and re-layouts  54.7 us (9%)
  matrix products  24.7 us (4%)
  between operations  14.8 us (3%)
  other arithmetic  14 us (2%)
    unnamed x2, waiting for transfers between devices  241 us
    ppermute x16, waiting for transfers between devices, from_behind(): return lax.ppermute(block, axis, route)  153 us
    ppermute x16, starting transfers between devices, from_behind(): return lax.ppermute(block, axis, route)  71.8 us
    slice x8, local copies, waits for them, and re-layouts, shards(): key_rows = jnp.concatenate([block[0] for block in ordered])  14.7 us
    unnamed x88, local copies, waits for them, and re-layouts  13 us
    concatenate x10, local copies, waits for them, and re-layouts, shards(): key_rows = jnp.concatenate([block[0] for block in ordered])  12.3 us
    another operation x2, local copies, waits for them, and re-layouts, shards(): grads_all = jnp.stack([dkey_rows, dvalue_rows])  12.2 us
  transfers between devices with their start and end apart: 17, of which 16 were waited for; matrix products, arithmetic and copies ran while one was open for 7% of the time, Pallas kernels for 0%

commit v1 on v0

v1 whole, which is shorter than its diff:
```python
import functools
import math

import jax
import jax.numpy as jnp
from jax import lax
from jax.experimental import pallas as pl
from jax.experimental.pallas import tpu as pltpu
from jax.sharding import Mesh
from jax.sharding import PartitionSpec as P

HEADS = 8
EPS = 1e-05
USERS = 32
TOK = 128
PLANE = 1024
TILE = 256
TILES = PLANE // TILE
SCALE = 1.0 / math.sqrt(128.0)
F32 = jnp.float32
BF16 = jnp.bfloat16
PLANE_AXES = ("x", "c")
VMEM_LIMIT = 48 * 1024 * 1024

NN = (((1,), (0,)), ((), ()))
NT = (((1,), (1,)), ((), ()))
TN = (((0,), (0,)), ((), ()))


def dot(a, b, dims=NN):
    return lax.dot_general(a, b, dims, preferred_element_type=F32)


def flip(block):
    return block.astype(F32).T.astype(BF16)


def call(body, outs, flops, moved, scratch=(), smem=0, ins=0):
    vmem = pl.BlockSpec(memory_space=pltpu.VMEM)
    specs = [pl.BlockSpec(memory_space=pltpu.SMEM)] * smem + [vmem] * (ins - smem)
    many = isinstance(outs, (list, tuple))
    return pl.pallas_call(
        body,
        out_shape=outs,
        in_specs=specs,
        out_specs=[vmem] * len(outs) if many else vmem,
        scratch_shapes=list(scratch),
        compiler_params=pltpu.CompilerParams(vmem_limit_bytes=VMEM_LIMIT),
        cost_estimate=pl.CostEstimate(flops=flops, bytes_accessed=moved, transcendentals=0),
    )


def shape(dims, dtype):
    return jax.ShapeDtypeStruct(dims, dtype)


def pack_body(q_ref, k_ref, v_ref, out_ref):
    for h in range(HEADS):
        cols = slice(h * TOK, (h + 1) * TOK)
        out_ref[h, 0:128, :] = q_ref[:, cols]
        out_ref[h, 128:256, :] = k_ref[:, cols]
        out_ref[h, 256:384, :] = v_ref[:, cols]


def dgated_body(cot_ref, gate_ref, w_ref, out_ref):
    cot = cot_ref[...]
    for h in range(HEADS):
        cols = slice(h * TOK, (h + 1) * TOK)
        out_ref[h, 0:128, :] = flip(gate_ref[:, cols])
        out_ref[h, 128:256, :] = dot(w_ref[cols, :], cot, NT).astype(BF16)


def tile_of(ref, j, rows):
    return ref[pl.ds(2 * j, 2), rows, :].reshape(TILE, 128)


def tile_mask(start_ref, i, first_key):
    start = jnp.concatenate([start_ref[2 * i : 2 * i + 1, :], start_ref[2 * i + 1 : 2 * i + 2, :]], axis=1)
    key_place = first_key + lax.broadcasted_iota(jnp.int32, (TILE, TILE), 0)
    query_place = i * TILE + lax.broadcasted_iota(jnp.int32, (TILE, TILE), 1)
    return (key_place >= start) & (key_place <= query_place)


def sigmoid(s):
    return 1.0 / (1.0 + jnp.exp(-s))


def forward_tiles(i, low, high, first, keys_ref, key_rows, start_ref, qt, vt_ref, total):
    def step(j, acc):
        s = dot(tile_of(keys_ref, j, key_rows), qt) * SCALE
        mask = tile_mask(start_ref, i, first + j * TILE)
        w = jnp.where(mask, s * sigmoid(s), 0.0).astype(BF16)
        return acc + dot(vt_ref[j], w)

    return lax.fori_loop(low, high, step, total)


def fwd_own_body(low_ref, recv_ref, start_ref, mixt_ref, qt_ref, vt_ref):
    for t in range(HEADS):
        qt_ref[:, t * TOK : (t + 1) * TOK] = flip(recv_ref[t, 0:128, :])
        vt_ref[t // 2, :, (t % 2) * TOK : (t % 2 + 1) * TOK] = flip(recv_ref[t, 256:384, :])
    for i in range(TILES):
        cols = slice(i * TILE, (i + 1) * TILE)
        low = jnp.maximum(low_ref[i] - TILES, 0)
        mixt_ref[:, cols] = forward_tiles(
            i, low, i + 1, 0, recv_ref, slice(128, 256), start_ref, qt_ref[:, cols], vt_ref, jnp.zeros((128, TILE), F32)
        )


def fwd_halo_body(low_ref, halo_ref, start_ref, qt_ref, part_ref, gd_ref, mixt_ref, stats_ref, vt_ref):
    for t in range(HEADS):
        vt_ref[t // 2, :, (t % 2) * TOK : (t % 2 + 1) * TOK] = flip(halo_ref[t, 128:256, :])
    for i in range(TILES):
        cols = slice(i * TILE, (i + 1) * TILE)
        mixt_ref[:, cols] = forward_tiles(
            i, low_ref[i], TILES, -PLANE, halo_ref, slice(0, 128), start_ref, qt_ref[:, cols], vt_ref, part_ref[:, cols]
        )
    for b in range(HEADS):
        mix = mixt_ref[:, b * TOK : (b + 1) * TOK]
        dn = gd_ref[b, 0:128, :].astype(F32) * gd_ref[b, 128:256, :].astype(F32)
        mean = jnp.sum(mix, axis=0, keepdims=True) * (1.0 / 128.0)
        centred = mix - mean
        rows = (
            mean,
            jnp.sum(centred * centred, axis=0, keepdims=True),
            jnp.sum(dn, axis=0, keepdims=True),
            jnp.sum(dn * centred, axis=0, keepdims=True),
        )
        for k, row in enumerate(rows):
            stats_ref[0, 8 * k + b : 8 * k + b + 1, :] = row
    for d in range(1, HEADS):
        stats_ref[d] = stats_ref[0]


def finish_body(mixt_ref, gd_ref, stats_ref, gated_ref, gg_ref, dmix_ref):
    means = [stats_ref[h, 0:8, :] for h in range(HEADS)]
    mean = sum(means) * (1.0 / HEADS)
    square = sum(stats_ref[h, 8:16, :] for h in range(HEADS))
    square = square + 128.0 * sum((m - mean) * (m - mean) for m in means)
    inverse = lax.rsqrt(square * (1.0 / 1024.0) + EPS)
    dmean = sum(stats_ref[h, 16:24, :] for h in range(HEADS)) * (1.0 / 1024.0)
    cross = sum(stats_ref[h, 24:32, :] + (means[h] - mean) * stats_ref[h, 16:24, :] for h in range(HEADS))
    dcross = cross * inverse * (1.0 / 1024.0)
    for b in range(HEADS):
        cols = slice(b * TOK, (b + 1) * TOK)
        one = slice(b, b + 1)
        inv = inverse[one, :]
        normed = (mixt_ref[:, cols] - mean[one, :]) * inv
        gate = gd_ref[b, 0:128, :].astype(F32)
        dgated = gd_ref[b, 128:256, :].astype(F32)
        gated_ref[:, cols] = (normed * gate).astype(BF16)
        gg_ref[:, cols] = (normed * dgated).astype(BF16)
        dmix_ref[:, cols] = (inv * (dgated * gate - dmean[one, :] - normed * dcross[one, :])).astype(BF16)


def weight_body(gated_ref, cot_ref, out_ref):
    total = dot(gated_ref[:, 0:TOK], cot_ref[0])
    for b in range(1, HEADS):
        total = total + dot(gated_ref[:, b * TOK : (b + 1) * TOK], cot_ref[b])
    out_ref[...] = total.astype(BF16)


def backward_tiles(i, low, high, first, keys_ref, key_rows, value_rows, start_ref, qt, q, dmt, kt_ref, dk_ref, dv_ref, total):
    def step(j, acc):
        s = dot(tile_of(keys_ref, j, key_rows), qt) * SCALE
        mask = tile_mask(start_ref, i, first + j * TILE)
        sig = sigmoid(s)
        w = jnp.where(mask, s * sig, 0.0).astype(BF16)
        dw = dot(tile_of(keys_ref, j, value_rows), dmt)
        ds = jnp.where(mask, dw * (sig * (1.0 + s * (1.0 - sig))) * SCALE, 0.0).astype(BF16)
        dv_ref[j] += dot(w, dmt, NT)
        dk_ref[j] += dot(ds, q)
        return acc + dot(kt_ref[j], ds)

    return lax.fori_loop(low, high, step, total)


def bwd_halo_body(low_ref, halo_ref, recv_ref, start_ref, qt_ref, dmix_ref, dqt_ref, out_ref, kt_ref, dk_ref, dv_ref):
    for t in range(HEADS):
        kt_ref[t // 2, :, (t % 2) * TOK : (t % 2 + 1) * TOK] = flip(halo_ref[t, 0:128, :])
    dk_ref[...] = jnp.zeros_like(dk_ref)
    dv_ref[...] = jnp.zeros_like(dv_ref)
    for i in range(TILES):
        cols = slice(i * TILE, (i + 1) * TILE)
        dqt_ref[:, cols] = backward_tiles(
            i, low_ref[i], TILES, -PLANE, halo_ref, slice(0, 128), slice(128, 256), start_ref, qt_ref[:, cols],
            tile_of(recv_ref, i, slice(0, 128)), dmix_ref[:, cols], kt_ref, dk_ref, dv_ref, jnp.zeros((128, TILE), F32),
        )
    for j in range(TILES):
        out_ref[2 * j : 2 * j + 2, 0:128, :] = dk_ref[j].astype(BF16).reshape(2, 128, 128)
        out_ref[2 * j : 2 * j + 2, 128:256, :] = dv_ref[j].astype(BF16).reshape(2, 128, 128)


def bwd_own_body(low_ref, recv_ref, start_ref, qt_ref, dmix_ref, part_ref, dq_ref, dk_ref, dv_ref, kt_ref):
    for t in range(HEADS):
        kt_ref[t // 2, :, (t % 2) * TOK : (t % 2 + 1) * TOK] = flip(recv_ref[t, 128:256, :])
    dk_ref[...] = jnp.zeros_like(dk_ref)
    dv_ref[...] = jnp.zeros_like(dv_ref)
    for i in range(TILES):
        cols = slice(i * TILE, (i + 1) * TILE)
        low = jnp.maximum(low_ref[i] - TILES, 0)
        dqt = backward_tiles(
            i, low, i + 1, 0, recv_ref, slice(128, 256), slice(256, 384), start_ref, qt_ref[:, cols],
            tile_of(recv_ref, i, slice(0, 128)), dmix_ref[:, cols], kt_ref, dk_ref, dv_ref, part_ref[:, cols],
        )
        dq_ref[i] = dqt.T.astype(BF16)


def gather_body(gated_ref, gg_ref, dq_ref, dk_ref, dv_ref, next_ref, out_ref):
    for b in range(HEADS):
        cols = slice(b * TOK, (b + 1) * TOK)
        rows = slice((b % 2) * TOK, (b % 2 + 1) * TOK)
        out_ref[b, 0:128, :] = gated_ref[:, cols]
        out_ref[b, 128:256, :] = gg_ref[:, cols]
        out_ref[b, 256:384, :] = dq_ref[b // 2, rows, :]
        out_ref[b, 384:512, :] = (dk_ref[b // 2, rows, :] + next_ref[b, 0:128, :].astype(F32)).astype(BF16)
        out_ref[b, 512:640, :] = (dv_ref[b // 2, rows, :] + next_ref[b, 128:256, :].astype(F32)).astype(BF16)


def final_body(recv_ref, w_ref, out_ref, dq_ref, dk_ref, dv_ref, gg_ref):
    total = jnp.zeros((TOK, 1024), F32)
    for h in range(HEADS):
        cols = slice(h * TOK, (h + 1) * TOK)
        total = total + dot(flip(recv_ref[h, 0:128, :]), w_ref[cols, :])
        gg_ref[:, cols] = flip(recv_ref[h, 128:256, :])
        dq_ref[:, cols] = recv_ref[h, 256:384, :]
        dk_ref[:, cols] = recv_ref[h, 384:512, :]
        dv_ref[:, cols] = recv_ref[h, 512:640, :]
    out_ref[...] = total.astype(BF16)


def plane_exchange(blocks):
    return lax.all_to_all(blocks, PLANE_AXES, 0, 0, tiled=True)


def shards(sizes, queries, keys, values, gates, cotangent, segment, w_out):
    dp, planes = sizes
    q, k, v, gate, cot, seg = (a[0] for a in (queries, keys, values, gates, cotangent, segment))
    cot_plane = lax.all_gather(cot, PLANE_AXES)

    packed = call(pack_body, shape((8, 384, 128), BF16), 1 << 16, 3 << 19, ins=3)(q, k, v)
    recv = plane_exchange(packed)

    place = lax.axis_index("z") * PLANE
    users = jnp.arange(USERS, dtype=jnp.int32)[:, None]
    first = jnp.sum((seg[None, :] < users).astype(jnp.int32), axis=1)
    mine = lax.dynamic_slice_in_dim(seg, place, PLANE)
    start = jnp.sum(jnp.where(mine[None, :] == users, first[:, None], 0), axis=0) - place
    low = (start[::TILE] + PLANE) // TILE
    start = start.reshape(8, 128)

    gd = call(dgated_body, shape((8, 256, 128), BF16), 1 << 28, 3 << 20, ins=3)(cot, gate, w_out)
    gd_recv = plane_exchange(gd)

    halo = lax.ppermute(recv[:, 128:384], "z", [(i, i + 1) for i in range(planes - 1)])
    vt = pltpu.VMEM((TILES, 128, TILE), BF16)
    acc = pltpu.VMEM((TILES, TILE, 128), F32)
    part, qt = call(
        fwd_own_body, [shape((128, PLANE), F32), shape((128, PLANE), BF16)], 1 << 29, 1 << 21, [vt], smem=1, ins=3
    )(low, recv, start)
    mixt, stats = call(
        fwd_halo_body, [shape((128, PLANE), F32), shape((8, 32, 128), F32)], 1 << 28, 1 << 21, [vt], smem=1, ins=6
    )(low, halo, start, qt, part, gd_recv)
    stats = plane_exchange(stats)
    gated, gg, dmix = call(finish_body, [shape((128, PLANE), BF16)] * 3, 1 << 22, 1 << 21, ins=3)(mixt, gd_recv, stats)

    partial = call(weight_body, shape((128, 1024), BF16), 1 << 28, 5 << 19, ins=2)(gated, cot_plane)
    shares = lax.all_to_all(partial, ("dp", "z"), 0, 0, tiled=True).reshape(dp * planes, 4, 1024)
    summed = jnp.sum(shares.astype(F32), axis=0)
    route = []
    for d in range(dp):
        for z in range(planes):
            for r in range(8):
                rows = 128 * r + 4 * (d * planes + z)
                route.append(((d * planes + z) * 8 + r, rows // 4))
    weight_grad = lax.ppermute(summed, ("dp", "z", "x", "c"), route)

    dqt, back = call(
        bwd_halo_body, [shape((128, PLANE), F32), shape((8, 256, 128), BF16)], 1 << 29, 1 << 21, [vt, acc, acc], smem=1, ins=6
    )(low, halo, recv, start, qt, dmix)
    back = lax.ppermute(back, "z", [(i, i - 1) for i in range(1, planes)])
    dq, dk, dv = call(
        bwd_own_body,
        [shape((TILES, TILE, 128), BF16), shape((TILES, TILE, 128), F32), shape((TILES, TILE, 128), F32)],
        1 << 30, 1 << 22, [vt], smem=1, ins=6,
    )(low, recv, start, qt, dmix, dqt)
    sent = call(gather_body, shape((8, 640, 128), BF16), 1 << 20, 1 << 22, ins=6)(gated, gg, dq, dk, dv, back)
    got = plane_exchange(sent)
    rows = shape((TOK, 1024), BF16)
    out, dq, dk, dv, gg = call(final_body, [rows] * 5, 1 << 28, 5 << 20, ins=2)(got, w_out)
    return out[None], dq[None], dk[None], dv[None], gg[None], weight_grad


def solution(mesh):
    dp, seq = mesh.shape["dp"], mesh.shape["seq"]
    planes = seq // 8
    grid = Mesh(mesh.devices.reshape(dp, planes, 4, 2), ("dp", "z", "x", "c"))
    tokens = P("dp", ("z", "x", "c"), None)
    return jax.shard_map(
        functools.partial(shards, (dp, planes)),
        mesh=grid,
        in_specs=(tokens,) * 5 + (P("dp", None), P()),
        out_specs=(tokens,) * 5 + (P(("dp", "z", "x", "c"), None),),
        check_vma=False,
    )
```

time: 579 us -> 140 us (0.24)
  the two profiles are of different devices: /device:TPU:128 before, /device:TPU:1 now
where the time goes in v1:
time: 140 us; the launch traced here: 139 us
  starting transfers between devices  47.2 us (34%)
  waiting for transfers between devices  29.1 us (21%)
  Pallas kernels  19.4 us (14%)
  local copies, waits for them, and re-layouts  17 us (12%)
  between operations  14.2 us (10%)
  blocking collectives  10.4 us (7%)
    all_to_all x3, waiting for transfers between devices, plane_exchange(): return lax.all_to_all(blocks, PLANE_AXES, 0, 0, tiled=True)  23.4 us
    all_to_all x1, starting transfers between devices, shards(): lax.all_to_all(partial, ('dp', 'z'), 0, 0, tiled=True)  19.2 us
    all_to_all x3, starting transfers between devices, plane_exchange(): return lax.all_to_all(blocks, PLANE_AXES, 0, 0, tiled=True)  18.5 us
    unnamed x49, local copies, waits for them, and re-layouts  15.2 us
    all_to_all x1, blocking collectives, plane_exchange(): return lax.all_to_all(blocks, PLANE_AXES, 0, 0, tiled=True)  10.4 us
    ppermute x1, starting transfers between devices, shards(): weight_grad = lax.ppermute(summed, ('dp', 'z', 'x', 'c'), route)  5.24 us
    ppermute x1, waiting for transfers between devices, shards(): lax.ppermute(recv[:, 128:384], 'z', [(i, i + 1) for i in range(planes - 1)])  4.99 us
    pallas_call x1, Pallas kernels, shards(): call(bwd_own_body, [shape((TILES, TILE, 128), BF16), shape((TILES, TILE,...  4.86 us
  transfers between devices with their start and end apart: 8, of which 4 were waited for; matrix products, arithmetic and copies ran while one was open for 2% of the time, Pallas kernels for 14%

profile of v1, /device:TPU:1, one launch (start us, length us, event | category | flops | bytes accessed | tf_op | source)
XLA Modules:
  0.0 138.7 jit_solution(8079170481503247840)
XLA Ops:
  7.9 1.0 copy-done.11
  8.9 0.9 copy-done.12
  9.9 0.9 copy-done.13
  10.8 1.0 shard_map.118
  11.8 6.8 %all-to-all-start = ((bf16[8,384,128]{2,1,0:T(8,128)(2,1)}), bf16[8,384,128]{2,1,0:T(8,128)(2,1)S(1)}, u32[]{:S(2)}, u32[]{:S(2)}) async-start(bf16[8,384,128]{2,1,0:T(8,128)(2,1)} %shard_map.118), calls=%async_computation | async-start | bytes 1572864 | tf_op jit(solution)/shard_map/all_to_all | solution.py:233
  20.5 11.1 %all-to-all-done.recv_ref = bf16[8,384,128]{2,1,0:T(8,128)(2,1)S(1)} async-done(((bf16[8,384,128]{2,1,0:T(8,128)(2,1)}), bf16[8,384,128]{2,1,0:T(8,128)(2,1)S(1)}, u32[]{:S(2)}, u32[]{:S(2)}) %all-to-all-start) | async-done | bytes 786464 | tf_op jit(solution)/shard_map/all_to_all | solution.py:233
  31.6 5.2 %all-to-all-start.1 = ((bf16[8,256,128]{2,1,0:T(8,128)(2,1)}), bf16[8,256,128]{2,1,0:T(8,128)(2,1)S(1)}, u32[]{:S(2)}, u32[]{:S(2)}) async-start(bf16[8,256,128]{2,1,0:T(8,128)(2,1)} %copy-done.2), calls=%async_computation.1 | async-start | bytes 1048576 | tf_op jit(solution)/shard_map/all_to_all | solution.py:233
  36.8 0.8 slice.8
  37.6 2.9 %collective-permute-start = (bf16[8,256,128]{2,1,0:T(8,128)(2,1)}, bf16[8,256,128]{2,1,0:T(8,128)(2,1)}, u32[]{:S(2)}, u32[]{:S(2)}) collective-permute-start(bf16[8,256,128]{2,1,0:T(8,128)(2,1)} %slice.8), channel_id=1, source_target_pairs={{0,8},{8,16},{16,24},{24,32},{32,40},{40,48},{48,56},{1,9},{9,17},... | collective-permute-start | bytes 1572872 | tf_op jit(solution)/shard_map/ppermute | solution.py:255
  40.7 4.0 %shard_map.119 = (f32[128,1024]{1,0:T(8,128)S(1)}, bf16[128,1024]{1,0:T(8,128)(2,1)S(1)}) custom-call(s32[4]{0:T(128)S(1)} %and_select_fusion.low_ref, bf16[8,384,128]{2,1,0:T(8,128)(2,1)S(1)} %all-to-all-done.recv_ref, s32[8,128]{1,0:T(8,128)S(1)} %fusion.start_ref), custom_call_target="tpu_custom_call" | custom-call | flops 536870912 | bytes 2097152 | tf_op jit(solution)/shard_map/pallas_call | solution.py:258
  44.6 0.8 copy-done.6
  46.3 5.0 %collective-permute-done.halo_ref = bf16[8,256,128]{2,1,0:T(8,128)(2,1)} collective-permute-done((bf16[8,256,128]{2,1,0:T(8,128)(2,1)}, bf16[8,256,128]{2,1,0:T(8,128)(2,1)}, u32[]{:S(2)}, u32[]{:S(2)}) %collective-permute-start) | collective-permute-done | bytes 524320 | tf_op jit(solution)/shard_map/ppermute | solution.py:255
  51.3 1.0 copy-done.7
  52.4 0.9 copy-done.15
  53.3 1.5 %shard_map.121 = (f32[128,1024]{1,0:T(8,128)S(1)}, f32[8,32,128]{2,1,0:T(8,128)S(1)}) custom-call(s32[4]{0:T(128)S(1)} %and_select_fusion.low_ref, bf16[8,256,128]{2,1,0:T(8,128)(2,1)} %collective-permute-done.halo_ref, s32[8,128]{1,0:T(8,128)S(1)} %fusion.start_ref, bf16[128,1024]{1,0:T(8,128)(2,1)S(1)} %copy-done.15, f32[128,1024]{1,0:T(8,128)S(1)} %copy-done.7, ...), custom_call_target="tpu_custom_call" | custom-call | flops 268435456 | bytes 2097152 | tf_op jit(solution)/shard_map/pallas_call | solution.py:261
  54.8 10.4 %all_to_all.29.stats_ref = f32[8,32,128]{2,1,0:T(8,128)S(1)} all-to-all(f32[8,32,128]{2,1,0:T(8,128)S(1)} %get-tuple-element.26), channel_id=1, replica_groups=mesh['dp'=4,'z'=8,'x'=4,'c'=2] {'x','c'}, dimensions={0} | all-to-all | bytes 262144 | tf_op jit(solution)/shard_map/all_to_all | solution.py:233
  66.9 2.3 %shard_map.123 = (f32[128,1024]{1,0:T(8,128)S(1)}, bf16[8,256,128]{2,1,0:T(8,128)(2,1)}) custom-call(s32[4]{0:T(128)S(1)} %and_select_fusion.low_ref, bf16[8,256,128]{2,1,0:T(8,128)(2,1)} %collective-permute-done.halo_ref, bf16[8,384,128]{2,1,0:T(8,128)(2,1)S(1)} %all-to-all-done.recv_ref, s32[8,128]{1,0:T(8,128)S(1)} %fusion.start_ref, ...), custom_call_target="tpu_custom_call" | custom-call | flops 536870912 | bytes 2097152 | tf_op jit(solution)/shard_map/pallas_call | solution.py:278
  69.2 0.8 copy-done.20
  70.0 1.3 collective-permute-start.1
  71.3 1.6 %copy-done.1 = bf16[8,128,1024]{2,1,0:T(8,128)(2,1)S(1)} copy-done((bf16[8,128,1024]{2,1,0:T(8,128)(2,1)S(1)}, bf16[8,128,1024]{2,1,0:T(8,128)(2,1)}, u32[]{:S(2)}) %copy-start.1) | copy-done | bytes 2097176
  73.6 0.8 all_to_all.22
  74.4 19.2 %all-to-all-start.4 = ((bf16[32,4,1024]{2,1,0:T(4,128)(2,1)}), bf16[32,4,1024]{2,1,0:T(4,128)(2,1)S(1)}, u32[]{:S(2)}, u32[]{:S(2)}) async-start(bf16[32,4,1024]{2,1,0:T(4,128)(2,1)} %all_to_all.22), calls=%async_computation.4 | async-start | bytes 524288 | tf_op jit(solution)/shard_map/all_to_all | solution.py:268
  93.6 1.0 copy-done.17
  94.6 0.9 copy-done.19
  95.6 1.0 copy-done.21
  96.6 4.9 %shard_map.124 = (bf16[4,256,128]{2,1,0:T(8,128)(2,1)S(1)}, f32[4,256,128]{2,1,0:T(8,128)S(1)}, f32[4,256,128]{2,1,0:T(8,128)S(1)}) custom-call(s32[4]{0:T(128)S(1)} %and_select_fusion.low_ref, bf16[8,384,128]{2,1,0:T(8,128)(2,1)S(1)} %all-to-all-done.recv_ref, s32[8,128]{1,0:T(8,128)S(1)} %fusion.start_ref, bf16[128,1024]{1,0:T(8,128)(2,1)S(1)} %copy-done.17, ...), custom_call_target="tpu_custom_call" | custom-call | flops 1073741824 | bytes 4194304 | tf_op jit(solution)/shard_map/pallas_call | solution.py:282
  101.5 2.3 %shard_map.125 = bf16[8,640,128]{2,1,0:T(8,128)(2,1)} custom-call(bf16[128,1024]{1,0:T(8,128)(2,1)S(1)} %copy-done.4, bf16[128,1024]{1,0:T(8,128)(2,1)S(1)} %copy-done.9, bf16[4,256,128]{2,1,0:T(8,128)(2,1)S(1)} %get-tuple-element.31.dq_ref, f32[4,256,128]{2,1,0:T(8,128)S(1)} %get-tuple-element.32.dk_ref, f32[4,256,128]{2,1,0:T(8,128)S(1)} %get-tuple-element.33.dv_ref, ...), custom_call_target="tpu_custom_call" | custom-call | flops 1048576 | bytes 4194304 | tf_op jit(solution)/shard_map/pallas_call | solution.py:287
  104.5 6.5 %all-to-all-start.3 = ((bf16[8,640,128]{2,1,0:T(8,128)(2,1)}), bf16[8,640,128]{2,1,0:T(8,128)(2,1)S(1)}, u32[]{:S(2)}, u32[]{:S(2)}) async-start(bf16[8,640,128]{2,1,0:T(8,128)(2,1)} %shard_map.125), calls=%async_computation.3 | async-start | bytes 2621440 | tf_op jit(solution)/shard_map/all_to_all | solution.py:233
  111.0 1.1 convert_reduce_fusion.1
  112.1 5.2 %collective-permute-start.2 = (f32[4,1024]{1,0:T(4,128)S(1)}, f32[4,1024]{1,0:T(4,128)S(1)}, u32[]{:S(2)}, u32[]{:S(2)}) collective-permute-start(f32[4,1024]{1,0:T(4,128)S(1)} %convert_reduce_fusion.1), channel_id=1, source_target_pairs={{0,0},{1,32},{2,64},{3,96},{4,128},{5,160},{6,192},{7,224},{8,1},{... | collective-permute-start | bytes 49160 | tf_op jit(solution)/shard_map/ppermute | solution.py:276
  117.4 12.1 %all-to-all-done.3.recv_ref = bf16[8,640,128]{2,1,0:T(8,128)(2,1)S(1)} async-done(((bf16[8,640,128]{2,1,0:T(8,128)(2,1)}), bf16[8,640,128]{2,1,0:T(8,128)(2,1)S(1)}, u32[]{:S(2)}, u32[]{:S(2)}) %all-to-all-start.3) | async-done | bytes 1310752 | tf_op jit(solution)/shard_map/all_to_all | solution.py:233
  129.5 1.8 %shard_map.126 = (bf16[128,1024]{1,0:T(8,128)(2,1)}, bf16[128,1024]{1,0:T(8,128)(2,1)}, bf16[128,1024]{1,0:T(8,128)(2,1)}, bf16[128,1024]{1,0:T(8,128)(2,1)}, bf16[128,1024]{1,0:T(8,128)(2,1)}) custom-call(bf16[8,640,128]{2,1,0:T(8,128)(2,1)S(1)} %all-to-all-done.3.recv_ref, bf16[1024,1024]{1,0:T(8,128)(2,1)S(1)} %copy-done), custom_call_target="tpu_custom_call" | custom-call | flops 268435456 | bytes 5242880 | tf_op jit(solution)/shard_map/pallas_call | solution.py:290
  (55 shorter events, 7.3 us)
Async XLA Ops:
  7.2 11.5 %copy-start.5 = (bf16[1,128,1024]{2,1,0:T(8,128)(2,1)S(1)}, bf16[1,128,1024]{2,1,0:T(8,128)(2,1)}, u32[]{:S(2)}) copy-start(bf16[1,128,1024]{2,1,0:T(8,128)(2,1)} %param.11) | copy-start | bytes 786436
  7.2 11.5 %copy-start.10 = (bf16[1,128,1024]{2,1,0:T(8,128)(2,1)S(1)}, bf16[1,128,1024]{2,1,0:T(8,128)(2,1)}, u32[]{:S(2)}) copy-start(bf16[1,128,1024]{2,1,0:T(8,128)(2,1)} %param.10) | copy-start | bytes 786436
  7.2 11.5 %copy-start = (bf16[1024,1024]{1,0:T(8,128)(2,1)S(1)}, bf16[1024,1024]{1,0:T(8,128)(2,1)}, u32[]{:S(2)}) copy-start(bf16[1024,1024]{1,0:T(8,128)(2,1)} %w_ref.3) | copy-start | bytes 6291460
  7.2 64.1 %all-gather.2.cloned.1.call-start = ((), (), s32[]{:S(2)}) async-start(), calls=%async_computation.5 | async-start | bytes 2359296 | tf_op jit(solution)/shard_map/all_gather | solution.py:239
  7.9 1.0 copy-start.11
  8.9 0.9 copy-start.12
  9.9 0.9 copy-start.13
  11.8 8.3 %copy-start.23 = (s32[1,8192]{1,0:T(1,128)S(1)}, s32[1,8192]{1,0:T(1,128)}, u32[]{:S(2)}) copy-start(s32[1,8192]{1,0:T(1,128)} %param.12) | copy-start | bytes 98308
  11.8 19.8 %all-to-all-start = ((bf16[8,384,128]{2,1,0:T(8,128)(2,1)}), bf16[8,384,128]{2,1,0:T(8,128)(2,1)S(1)}, u32[]{:S(2)}, u32[]{:S(2)}) async-start(bf16[8,384,128]{2,1,0:T(8,128)(2,1)} %shard_map.118), calls=%async_computation | async-start | bytes 1572864 | tf_op jit(solution)/shard_map/all_to_all | solution.py:233
  19.4 0.8 copy-start.2
  31.6 14.7 %all-to-all-start.1 = ((bf16[8,256,128]{2,1,0:T(8,128)(2,1)}), bf16[8,256,128]{2,1,0:T(8,128)(2,1)S(1)}, u32[]{:S(2)}, u32[]{:S(2)}) async-start(bf16[8,256,128]{2,1,0:T(8,128)(2,1)} %copy-done.2), calls=%async_computation.1 | async-start | bytes 1048576 | tf_op jit(solution)/shard_map/all_to_all | solution.py:233
  37.6 13.7 %collective-permute-start = (bf16[8,256,128]{2,1,0:T(8,128)(2,1)}, bf16[8,256,128]{2,1,0:T(8,128)(2,1)}, u32[]{:S(2)}, u32[]{:S(2)}) collective-permute-start(bf16[8,256,128]{2,1,0:T(8,128)(2,1)} %slice.8), channel_id=1, source_target_pairs={{0,8},{8,16},{16,24},{24,32},{32,40},{40,48},{48,56},{1,9},{9,17},... | collective-permute-start | bytes 1572872 | tf_op jit(solution)/shard_map/ppermute | solution.py:255
  44.6 0.8 copy-start.6
  45.4 0.7 copy-start.14
  51.3 1.0 copy-start.7
  52.4 0.9 copy-start.15
  53.3 13.6 %copy-start.16 = (bf16[128,1024]{1,0:T(8,128)(2,1)S(1)}, bf16[128,1024]{1,0:T(8,128)(2,1)}, u32[]{:S(2)}) copy-start(bf16[128,1024]{1,0:T(8,128)(2,1)} %copy-done.14) | copy-start | bytes 786436
  65.5 0.7 copy-start.3
  66.2 0.7 copy-start.8
  66.9 2.3 %copy-start.18 = (bf16[128,1024]{1,0:T(8,128)(2,1)}, bf16[128,1024]{1,0:T(8,128)(2,1)S(1)}, u32[]{:S(2)}) copy-start(bf16[128,1024]{1,0:T(8,128)(2,1)S(1)} %get-tuple-element.29.dmix_ref) | copy-start | bytes 786436
  66.9 4.4 %copy-start.4 = (bf16[128,1024]{1,0:T(8,128)(2,1)S(1)}, bf16[128,1024]{1,0:T(8,128)(2,1)}, u32[]{:S(2)}) copy-start(bf16[128,1024]{1,0:T(8,128)(2,1)} %copy-done.3) | copy-start | bytes 786436
  69.2 0.8 copy-start.20
  70.0 31.5 %collective-permute-start.1 = (bf16[8,256,128]{2,1,0:T(8,128)(2,1)}, bf16[8,256,128]{2,1,0:T(8,128)(2,1)}, u32[]{:S(2)}, u32[]{:S(2)}) collective-permute-start(bf16[8,256,128]{2,1,0:T(8,128)(2,1)} %get-tuple-element.34), channel_id=1, source_target_pairs={{8,0},{16,8},{24,16},{32,24},{40,32},{48,40},{56,48},{9,1},{17,9},... | collective-permute-start | bytes 1572872 | tf_op jit(solution)/shard_map/ppermute | solution.py:281
  71.3 1.6 %copy-start.1 = (bf16[8,128,1024]{2,1,0:T(8,128)(2,1)S(1)}, bf16[8,128,1024]{2,1,0:T(8,128)(2,1)}, u32[]{:S(2)}) copy-start(bf16[8,128,1024]{2,1,0:T(8,128)(2,1)} %all-gather.2.cloned.1.call-done.cot_ref) | copy-start | bytes 6291460
  74.4 29.4 %all-to-all-start.4 = ((bf16[32,4,1024]{2,1,0:T(4,128)(2,1)}), bf16[32,4,1024]{2,1,0:T(4,128)(2,1)S(1)}, u32[]{:S(2)}, u32[]{:S(2)}) async-start(bf16[32,4,1024]{2,1,0:T(4,128)(2,1)} %all_to_all.22), calls=%async_computation.4 | async-start | bytes 524288 | tf_op jit(solution)/shard_map/all_to_all | solution.py:268
  93.6 7.9 %copy-start.9 = (bf16[128,1024]{1,0:T(8,128)(2,1)S(1)}, bf16[128,1024]{1,0:T(8,128)(2,1)}, u32[]{:S(2)}) copy-start(bf16[128,1024]{1,0:T(8,128)(2,1)} %copy-done.8) | copy-start | bytes 786436
  93.6 1.0 copy-start.17
  94.6 0.9 copy-start.19
  95.6 1.0 copy-start.21
  103.8 0.7 copy-start.22
  104.5 25.0 %all-to-all-start.3 = ((bf16[8,640,128]{2,1,0:T(8,128)(2,1)}), bf16[8,640,128]{2,1,0:T(8,128)(2,1)S(1)}, u32[]{:S(2)}, u32[]{:S(2)}) async-start(bf16[8,640,128]{2,1,0:T(8,128)(2,1)} %shard_map.125), calls=%async_computation.3 | async-start | bytes 2621440 | tf_op jit(solution)/shard_map/all_to_all | solution.py:233
  112.1 19.2 %collective-permute-start.2 = (f32[4,1024]{1,0:T(4,128)S(1)}, f32[4,1024]{1,0:T(4,128)S(1)}, u32[]{:S(2)}, u32[]{:S(2)}) collective-permute-start(f32[4,1024]{1,0:T(4,128)S(1)} %convert_reduce_fusion.1), channel_id=1, source_target_pairs={{0,0},{1,32},{2,64},{3,96},{4,128},{5,160},{6,192},{7,224},{8,1},{... | collective-permute-start | bytes 49160 | tf_op jit(solution)/shard_map/ppermute | solution.py:276
Sparse Core Ops, SparseCore 0:
  9.9 34.7 all-gather.1

commit v2 on v1

--- a/solution.py
+++ b/solution.py
@@ -20,7 +20,8 @@
 F32 = jnp.float32
 BF16 = jnp.bfloat16
 PLANE_AXES = ("x", "c")
-VMEM_LIMIT = 48 * 1024 * 1024
+VMEM_LIMIT = 60 * 1024 * 1024
+ROOM = 62_300_000
 
 NN = (((1,), (0,)), ((), ()))
 NT = (((1,), (1,)), ((), ()))
@@ -35,31 +36,71 @@
     return block.astype(F32).T.astype(BF16)
 
 
-def call(body, outs, flops, moved, scratch=(), smem=0, ins=0):
-    vmem = pl.BlockSpec(memory_space=pltpu.VMEM)
-    specs = [pl.BlockSpec(memory_space=pltpu.SMEM)] * smem + [vmem] * (ins - smem)
+def call(body, places, outs, flops, scratch=(), limit=VMEM_LIMIT):
     many = isinstance(outs, (list, tuple))
-    return pl.pallas_call(
-        body,
-        out_shape=outs,
-        in_specs=specs,
-        out_specs=[vmem] * len(outs) if many else vmem,
-        scratch_shapes=list(scratch),
-        compiler_params=pltpu.CompilerParams(vmem_limit_bytes=VMEM_LIMIT),
-        cost_estimate=pl.CostEstimate(flops=flops, bytes_accessed=moved, transcendentals=0),
-    )
+    outs = list(outs) if many else [outs]
+    spaces = {"s": pltpu.SMEM, "v": pltpu.VMEM, "h": pltpu.HBM, "l": pltpu.HBM}
+
+    def build(*args):
+        staged = [n for n, place in enumerate(places) if place in "hl"]
+
+        def whole(*refs):
+            refs = list(refs)
+            given, refs = refs[: len(args)], refs[len(args) :]
+            results, refs = refs[: len(outs)], refs[len(outs) :]
+            held, refs = refs[: len(staged)], refs[len(staged) :]
+            made, refs = refs[: len(outs)], refs[len(outs) :]
+            sems, out_sems, extra = refs[0], refs[1], refs[2:]
+            now = []
+            for m, n in enumerate(staged):
+                copy = pltpu.make_async_copy(given[n], held[m], sems.at[m])
+                copy.start()
+                given[n] = held[m]
+                if places[n] == "l":
+                    given[n] = (held[m], copy)
+                else:
+                    now.append(copy)
+            for copy in now:
+                copy.wait()
+            body(*given, *made, *extra)
+            back = [pltpu.make_async_copy(src, dst, out_sems.at[m]) for m, (src, dst) in enumerate(zip(made, results))]
+            for copy in back:
+                copy.start()
+            for copy in back:
+                copy.wait()
+
+        moved = sum(a.size * a.dtype.itemsize for a in args) + sum(o.size * o.dtype.itemsize for o in outs)
+        got = pl.pallas_call(
+            whole,
+            out_shape=outs,
+            in_specs=[pl.BlockSpec(memory_space=spaces[place]) for place in places],
+            out_specs=[pl.BlockSpec(memory_space=pltpu.HBM)] * len(outs),
+            scratch_shapes=[pltpu.VMEM(args[n].shape, args[n].dtype) for n in staged]
+            + [pltpu.VMEM(o.shape, o.dtype) for o in outs]
+            + [pltpu.SemaphoreType.DMA((max(len(staged), 1),)), pltpu.SemaphoreType.DMA((len(outs),))]
+            + list(scratch),
+            compiler_params=pltpu.CompilerParams(vmem_limit_bytes=limit),
+            cost_estimate=pl.CostEstimate(flops=flops, bytes_accessed=moved, transcendentals=0),
+        )(*args)
+        return got if many else got[0]
+
+    return build
 
 
 def shape(dims, dtype):
     return jax.ShapeDtypeStruct(dims, dtype)
 
 
-def pack_body(q_ref, k_ref, v_ref, out_ref):
+def pack_body(q_ref, k_ref, v_ref, out_ref, sems):
+    copies = []
     for h in range(HEADS):
-        cols = slice(h * TOK, (h + 1) * TOK)
-        out_ref[h, 0:128, :] = q_ref[:, cols]
-        out_ref[h, 128:256, :] = k_ref[:, cols]
-        out_ref[h, 256:384, :] = v_ref[:, cols]
+        for n, ref in enumerate((q_ref, k_ref, v_ref)):
+            src = ref.at[:, h * TOK : (h + 1) * TOK]
+            copies.append(pltpu.make_async_copy(src, out_ref.at[h, n * TOK : (n + 1) * TOK, :], sems.at[n, h]))
+    for copy in copies:
+        copy.start()
+    for copy in copies:
+        copy.wait()
 
 
 def dgated_body(cot_ref, gate_ref, w_ref, out_ref):
@@ -132,7 +173,7 @@
         stats_ref[d] = stats_ref[0]
 
 
-def finish_body(mixt_ref, gd_ref, stats_ref, gated_ref, gg_ref, dmix_ref):
+def finish(mixt_ref, gd_ref, stats_ref, gated_ref, gg_ref, dmix_ref):
     means = [stats_ref[h, 0:8, :] for h in range(HEADS)]
     mean = sum(means) * (1.0 / HEADS)
     square = sum(stats_ref[h, 8:16, :] for h in range(HEADS))
@@ -153,7 +194,7 @@
         dmix_ref[:, cols] = (inv * (dgated * gate - dmean[one, :] - normed * dcross[one, :])).astype(BF16)
 
 
-def weight_body(gated_ref, cot_ref, out_ref):
+def weight_part(gated_ref, cot_ref, out_ref):
     total = dot(gated_ref[:, 0:TOK], cot_ref[0])
     for b in range(1, HEADS):
         total = total + dot(gated_ref[:, b * TOK : (b + 1) * TOK], cot_ref[b])
@@ -175,7 +216,11 @@
     return lax.fori_loop(low, high, step, total)
 
 
-def bwd_halo_body(low_ref, halo_ref, recv_ref, start_ref, qt_ref, dmix_ref, dqt_ref, out_ref, kt_ref, dk_ref, dv_ref):
+def middle_body(
+    low_ref, mixt_ref, gd_ref, stats_ref, halo_ref, recv_ref, start_ref, qt_ref, late,
+    gated_ref, gg_ref, dmix_ref, dqt_ref, out_ref, part_ref, kt_ref, dk_ref, dv_ref,
+):
+    finish(mixt_ref, gd_ref, stats_ref, gated_ref, gg_ref, dmix_ref)
     for t in range(HEADS):
         kt_ref[t // 2, :, (t % 2) * TOK : (t % 2 + 1) * TOK] = flip(halo_ref[t, 0:128, :])
     dk_ref[...] = jnp.zeros_like(dk_ref)
@@ -189,9 +234,15 @@
     for j in range(TILES):
         out_ref[2 * j : 2 * j + 2, 0:128, :] = dk_ref[j].astype(BF16).reshape(2, 128, 128)
         out_ref[2 * j : 2 * j + 2, 128:256, :] = dv_ref[j].astype(BF16).reshape(2, 128, 128)
-
-
-def bwd_own_body(low_ref, recv_ref, start_ref, qt_ref, dmix_ref, part_ref, dq_ref, dk_ref, dv_ref, kt_ref):
+    cot_ref, copy = late
+    copy.wait()
+    weight_part(gated_ref, cot_ref, part_ref)
+
+
+def bwd_own_body(low_ref, recv_ref, start_ref, qt_ref, dmix_ref, part_ref, gated_ref, gg_ref, late, out_ref, kt_ref, dk_ref, dv_ref):
+    for b in range(HEADS):
+        out_ref[b, 0:128, :] = gated_ref[:, b * TOK : (b + 1) * TOK]
+        out_ref[b, 128:256, :] = gg_ref[:, b * TOK : (b + 1) * TOK]
     for t in range(HEADS):
         kt_ref[t // 2, :, (t % 2) * TOK : (t % 2 + 1) * TOK] = flip(recv_ref[t, 128:256, :])
     dk_ref[...] = jnp.zeros_like(dk_ref)
@@ -203,29 +254,27 @@
             i, low, i + 1, 0, recv_ref, slice(128, 256), slice(256, 384), start_ref, qt_ref[:, cols],
             tile_of(recv_ref, i, slice(0, 128)), dmix_ref[:, cols], kt_ref, dk_ref, dv_ref, part_ref[:, cols],
         )
-        dq_ref[i] = dqt.T.astype(BF16)
-
-
-def gather_body(gated_ref, gg_ref, dq_ref, dk_ref, dv_ref, next_ref, out_ref):
+        out_ref[2 * i : 2 * i + 2, 256:384, :] = dqt.T.astype(BF16).reshape(2, 128, 128)
+    next_ref, copy = late
+    copy.wait()
     for b in range(HEADS):
-        cols = slice(b * TOK, (b + 1) * TOK)
         rows = slice((b % 2) * TOK, (b % 2 + 1) * TOK)
-        out_ref[b, 0:128, :] = gated_ref[:, cols]
-        out_ref[b, 128:256, :] = gg_ref[:, cols]
-        out_ref[b, 256:384, :] = dq_ref[b // 2, rows, :]
         out_ref[b, 384:512, :] = (dk_ref[b // 2, rows, :] + next_ref[b, 0:128, :].astype(F32)).astype(BF16)
         out_ref[b, 512:640, :] = (dv_ref[b // 2, rows, :] + next_ref[b, 128:256, :].astype(F32)).astype(BF16)
 
 
-def final_body(recv_ref, w_ref, out_ref, dq_ref, dk_ref, dv_ref, gg_ref):
-    total = jnp.zeros((TOK, 1024), F32)
+def final_body(recv_ref, late, out_ref, dq_ref, dk_ref, dv_ref, gg_ref):
+    w_ref, copy = late
     for h in range(HEADS):
         cols = slice(h * TOK, (h + 1) * TOK)
-        total = total + dot(flip(recv_ref[h, 0:128, :]), w_ref[cols, :])
         gg_ref[:, cols] = flip(recv_ref[h, 128:256, :])
         dq_ref[:, cols] = recv_ref[h, 256:384, :]
         dk_ref[:, cols] = recv_ref[h, 384:512, :]
         dv_ref[:, cols] = recv_ref[h, 512:640, :]
+    copy.wait()
+    total = dot(flip(recv_ref[0, 0:128, :]), w_ref[0:TOK, :])
+    for h in range(1, HEADS):
+        total = total + dot(flip(recv_ref[h, 0:128, :]), w_ref[h * TOK : (h + 1) * TOK, :])
     out_ref[...] = total.astype(BF16)
 
 
@@ -238,7 +287,15 @@
     q, k, v, gate, cot, seg = (a[0] for a in (queries, keys, values, gates, cotangent, segment))
     cot_plane = lax.all_gather(cot, PLANE_AXES)
 
-    packed = call(pack_body, shape((8, 384, 128), BF16), 1 << 16, 3 << 19, ins=3)(q, k, v)
+    packed = pl.pallas_call(
+        pack_body,
+        out_shape=shape((8, 384, 128), BF16),
+        in_specs=[pl.BlockSpec(memory_space=pltpu.HBM)] * 3,
+        out_specs=pl.BlockSpec(memory_space=pltpu.HBM),
+        scratch_shapes=[pltpu.SemaphoreType.DMA((3, HEADS))],
+        compiler_params=pltpu.CompilerParams(vmem_limit_bytes=VMEM_LIMIT),
+        cost_estimate=pl.CostEstimate(flops=1 << 16, bytes_accessed=3 << 19, transcendentals=0),
+    )(q, k, v)
     recv = plane_exchange(packed)
 
     place = lax.axis_index("z") * PLANE
@@ -249,22 +306,25 @@
     low = (start[::TILE] + PLANE) // TILE
     start = start.reshape(8, 128)
 
-    gd = call(dgated_body, shape((8, 256, 128), BF16), 1 << 28, 3 << 20, ins=3)(cot, gate, w_out)
+    pair, cot_now = lax.optimization_barrier((recv[:, 128:384], cot))
+    halo = lax.ppermute(pair, "z", [(i, i + 1) for i in range(planes - 1)])
+    gd = call(dgated_body, "hhh", shape((8, 256, 128), BF16), 1 << 28)(cot_now, gate, w_out)
     gd_recv = plane_exchange(gd)
 
-    halo = lax.ppermute(recv[:, 128:384], "z", [(i, i + 1) for i in range(planes - 1)])
+    head = shape((128, PLANE), F32)
+    head16 = shape((128, PLANE), BF16)
     vt = pltpu.VMEM((TILES, 128, TILE), BF16)
     acc = pltpu.VMEM((TILES, TILE, 128), F32)
-    part, qt = call(
-        fwd_own_body, [shape((128, PLANE), F32), shape((128, PLANE), BF16)], 1 << 29, 1 << 21, [vt], smem=1, ins=3
-    )(low, recv, start)
-    mixt, stats = call(
-        fwd_halo_body, [shape((128, PLANE), F32), shape((8, 32, 128), F32)], 1 << 28, 1 << 21, [vt], smem=1, ins=6
-    )(low, halo, start, qt, part, gd_recv)
+    part, qt = call(fwd_own_body, "shh", [head, head16], 1 << 29, [vt])(low, recv, start)
+    mixt, stats = call(fwd_halo_body, "shhhhh", [head, shape((8, 32, 128), F32)], 1 << 28, [vt], ROOM)(
+        low, halo, start, qt, part, gd_recv
+    )
     stats = plane_exchange(stats)
-    gated, gg, dmix = call(finish_body, [shape((128, PLANE), BF16)] * 3, 1 << 22, 1 << 21, ins=3)(mixt, gd_recv, stats)
-
-    partial = call(weight_body, shape((128, 1024), BF16), 1 << 28, 5 << 19, ins=2)(gated, cot_plane)
+    gated, gg, dmix, dqt, back, partial = call(
+        middle_body, "shhhhhhhl", [head16, head16, head16, head, shape((8, 256, 128), BF16), head16], 1 << 29, [vt, acc, acc]
+    )(low, mixt, gd_recv, stats, halo, recv, start, qt, cot_plane)
+    back = lax.ppermute(back, "z", [(i, i - 1) for i in range(1, planes)])
+
     shares = lax.all_to_all(partial, ("dp", "z"), 0, 0, tiled=True).reshape(dp * planes, 4, 1024)
     summed = jnp.sum(shares.astype(F32), axis=0)
     route = []
@@ -275,19 +335,12 @@
                 route.append(((d * planes + z) * 8 + r, rows // 4))
     weight_grad = lax.ppermute(summed, ("dp", "z", "x", "c"), route)
 
-    dqt, back = call(
-        bwd_halo_body, [shape((128, PLANE), F32), shape((8, 256, 128), BF16)], 1 << 29, 1 << 21, [vt, acc, acc], smem=1, ins=6
-    )(low, halo, recv, start, qt, dmix)
-    back = lax.ppermute(back, "z", [(i, i - 1) for i in range(1, planes)])
-    dq, dk, dv = call(
-        bwd_own_body,
-        [shape((TILES, TILE, 128), BF16), shape((TILES, TILE, 128), F32), shape((TILES, TILE, 128), F32)],
-        1 << 30, 1 << 22, [vt], smem=1, ins=6,
-    )(low, recv, start, qt, dmix, dqt)
-    sent = call(gather_body, shape((8, 640, 128), BF16), 1 << 20, 1 << 22, ins=6)(gated, gg, dq, dk, dv, back)
+    sent = call(bwd_own_body, "shhhhhhhl", shape((8, 640, 128), BF16), 1 << 30, [vt, acc, acc], ROOM)(
+        low, recv, start, qt, dmix, dqt, gated, gg, back
+    )
     got = plane_exchange(sent)
     rows = shape((TOK, 1024), BF16)
-    out, dq, dk, dv, gg = call(final_body, [rows] * 5, 1 << 28, 5 << 20, ins=2)(got, w_out)
+    out, dq, dk, dv, gg = call(final_body, "hl", [rows] * 5, 1 << 28, (), VMEM_LIMIT // 2)(got, w_out)
     return out[None], dq[None], dk[None], dv[None], gg[None], weight_grad
 
 

time: 140 us -> 159 us (1.14)
  the two profiles are of different devices: /device:TPU:1 before, /device:TPU:128 now
where the time goes in v2:
time: 159 us; the launch traced here: 158 us
  Pallas kernels  55.4 us (35%)
  waiting for transfers between devices  38.8 us (24%)
  starting transfers between devices  32.1 us (20%)
  between operations  14.2 us (9%)
  blocking collectives  10.1 us (6%)
  local copies, waits for them, and re-layouts  5.02 us (3%)
  other arithmetic  2.5 us (2%)
    pallas_call x6, Pallas kernels, build(): pl.pallas_call(whole, out_shape=outs, in_specs=[pl.BlockSpec(memory_space...  30.2 us
    pallas_call x1, Pallas kernels, shards(): pl.pallas_call(pack_body, out_shape=shape((8, 384, 128), BF16), in_specs=...  25.1 us
    all_to_all x3, waiting for transfers between devices, plane_exchange(): return lax.all_to_all(blocks, PLANE_AXES, 0, 0, tiled=True)  24.4 us
    all_to_all x3, starting transfers between devices, plane_exchange(): return lax.all_to_all(blocks, PLANE_AXES, 0, 0, tiled=True)  11.4 us
    all_to_all x1, blocking collectives, plane_exchange(): return lax.all_to_all(blocks, PLANE_AXES, 0, 0, tiled=True)  10.1 us
    ppermute x1, starting transfers between devices, shards(): back = lax.ppermute(back, 'z', [(i, i - 1) for i in range(1, planes)])  8.47 us
    all_to_all x1, starting transfers between devices, shards(): lax.all_to_all(partial, ('dp', 'z'), 0, 0, tiled=True)  7.4 us
    ppermute x1, waiting for transfers between devices, shards(): weight_grad = lax.ppermute(summed, ('dp', 'z', 'x', 'c'), route)  7.04 us
  transfers between devices with their start and end apart: 8, of which 5 were waited for; matrix products, arithmetic and copies ran while one was open for 2% of the time, Pallas kernels for 30%

profile of v2, /device:TPU:128, one launch (start us, length us, event | category | flops | bytes accessed | tf_op | source)
XLA Modules:
  0.0 158.1 jit_solution(6056028770522335784)
XLA Ops:
  7.2 0.7 all-gather.2.cloned.1.call-update
  7.9 25.1 %shard_map.118 = bf16[8,384,128]{2,1,0:T(8,128)(2,1)} custom-call(bf16[128,1024]{1,0:T(8,128)(2,1)} %bitcast.16, bf16[128,1024]{1,0:T(8,128)(2,1)} %bitcast.17, bf16[128,1024]{1,0:T(8,128)(2,1)} %bitcast.18), custom_call_target="tpu_custom_call" | custom-call | flops 65536 | bytes 1572864 | tf_op jit(solution)/shard_map/pallas_call | solution.py:290
  33.1 4.3 %all-to-all-start = ((bf16[8,384,128]{2,1,0:T(8,128)(2,1)}), bf16[8,384,128]{2,1,0:T(8,128)(2,1)S(1)}, u32[]{:S(2)}, u32[]{:S(2)}) async-start(bf16[8,384,128]{2,1,0:T(8,128)(2,1)} %shard_map.118), calls=%async_computation | async-start | bytes 1572864 | tf_op jit(solution)/shard_map/all_to_all | solution.py:282
  37.4 0.2 convert_reduce_fusion
  37.6 0.1 select_reduce_fusion
  37.7 12.8 %all-to-all-done.refs_1_.refs_5_ = bf16[8,384,128]{2,1,0:T(8,128)(2,1)S(1)} async-done(((bf16[8,384,128]{2,1,0:T(8,128)(2,1)}), bf16[8,384,128]{2,1,0:T(8,128)(2,1)S(1)}, u32[]{:S(2)}, u32[]{:S(2)}) %all-to-all-start) | async-done | bytes 786464 | tf_op jit(solution)/shard_map/all_to_all | solution.py:282
  50.6 2.9 %collective-permute-start = (bf16[8,256,128]{2,1,0:T(8,128)(2,1)S(1)}, bf16[8,256,128]{2,1,0:T(8,128)(2,1)S(1)}, u32[]{:S(2)}, u32[]{:S(2)}) collective-permute-start(bf16[8,256,128]{2,1,0:T(8,128)(2,1)S(1)} %slice.8), channel_id=1, source_target_pairs={{0,8},{8,16},{16,24},{24,32},{32,40},{40,48},{48,56},{1,9},{9,17},... | collective-permute-start | bytes 1572872 | tf_op jit(solution)/shard_map/ppermute | solution.py:310
  53.6 3.3 %shard_map.120 = bf16[8,256,128]{2,1,0:T(8,128)(2,1)} custom-call(bf16[128,1024]{1,0:T(8,128)(2,1)} %bitcast.14, bf16[128,1024]{1,0:T(8,128)(2,1)} %bitcast.15, bf16[1024,1024]{1,0:T(8,128)(2,1)} %refs_1_.1), custom_call_target="tpu_custom_call" | custom-call | flops 268435456 | bytes 3145728 | tf_op jit(solution)/shard_map/pallas_call | solution.py:73
  57.0 3.5 %all-to-all-start.1 = ((bf16[8,256,128]{2,1,0:T(8,128)(2,1)}), bf16[8,256,128]{2,1,0:T(8,128)(2,1)S(1)}, u32[]{:S(2)}, u32[]{:S(2)}) async-start(bf16[8,256,128]{2,1,0:T(8,128)(2,1)} %shard_map.120), calls=%async_computation.1 | async-start | bytes 1048576 | tf_op jit(solution)/shard_map/all_to_all | solution.py:282
  60.5 0.5 and_select_fusion.refs_0_
  61.0 0.6 fusion.refs_2_.refs_6_
  61.6 6.9 %shard_map.119 = (f32[128,1024]{1,0:T(8,128)}, bf16[128,1024]{1,0:T(8,128)(2,1)}) custom-call(s32[4]{0:T(128)} %and_select_fusion.refs_0_, bf16[8,384,128]{2,1,0:T(8,128)(2,1)} %copy-done.1, s32[8,128]{1,0:T(8,128)} %fusion.refs_2_.refs_6_), custom_call_target="tpu_custom_call" | custom-call | flops 536870912 | bytes 1576976 | tf_op jit(solution)/shard_map/pallas_call | solution.py:73
  68.5 2.2 %all-to-all-done.1.refs_5_.refs_2_ = bf16[8,256,128]{2,1,0:T(8,128)(2,1)S(1)} async-done(((bf16[8,256,128]{2,1,0:T(8,128)(2,1)}), bf16[8,256,128]{2,1,0:T(8,128)(2,1)S(1)}, u32[]{:S(2)}, u32[]{:S(2)}) %all-to-all-start.1) | async-done | bytes 524320 | tf_op jit(solution)/shard_map/all_to_all | solution.py:282
  70.7 0.8 copy-done.2
  71.5 0.2 copy-done.3
  71.7 3.6 %shard_map.121 = (f32[128,1024]{1,0:T(8,128)}, f32[8,32,128]{2,1,0:T(8,128)}) custom-call(s32[4]{0:T(128)} %and_select_fusion.refs_0_, bf16[8,256,128]{2,1,0:T(8,128)(2,1)} %copy-done.3, s32[8,128]{1,0:T(8,128)} %fusion.refs_2_.refs_6_, bf16[128,1024]{1,0:T(8,128)(2,1)} %get-tuple-element.23.refs_3_.refs_7_, f32[128,1024]{1,0:T(8,128)} %get-tuple-element.25.refs_4_, ...), custom_call_target="tpu_custom_call" | custom-call | flops 268435456 | bytes 2494480 | tf_op jit(solution)/shard_map/pallas_call | solution.py:73
  75.3 10.1 %all_to_all.29.refs_3_ = f32[8,32,128]{2,1,0:T(8,128)} all-to-all(f32[8,32,128]{2,1,0:T(8,128)} %get-tuple-element.28), channel_id=1, replica_groups=mesh['dp'=4,'z'=8,'x'=4,'c'=2] {'x','c'}, dimensions={0} | all-to-all | bytes 262144 | tf_op jit(solution)/shard_map/all_to_all | solution.py:282
  85.4 5.0 %shard_map.122 = (bf16[128,1024]{1,0:T(8,128)(2,1)}, bf16[128,1024]{1,0:T(8,128)(2,1)}, bf16[128,1024]{1,0:T(8,128)(2,1)}, f32[128,1024]{1,0:T(8,128)}, bf16[8,2...) custom-call(s32[4]{0:T(128)} %and_select_fusion.refs_0_, f32[128,1024]{1,0:T(8,128)} %get-tuple-element.27.refs_1_, ...), custom_call_target="tpu_custom_call" | custom-call | flops 536870912 | bytes 6950928 | tf_op jit(solution)/shard_map/pallas_call | solution.py:73
  90.5 8.5 %collective-permute-start.1 = (bf16[8,256,128]{2,1,0:T(8,128)(2,1)}, bf16[8,256,128]{2,1,0:T(8,128)(2,1)S(1)}, u32[]{:S(2)}, u32[]{:S(2)}) collective-permute-start(bf16[8,256,128]{2,1,0:T(8,128)(2,1)} %get-tuple-element.33), channel_id=1, source_target_pairs={{8,0},{16,8},{24,16},{32,24},{40,32},{48,40},{56,48},{9,1},{17,9},... | collective-permute-start | bytes 1572872 | tf_op jit(solution)/shard_map/ppermute | solution.py:326
  98.9 1.8 %all_to_all.22 = bf16[32,4,1024]{2,1,0:T(4,128)(2,1)} reshape(bf16[128,1024]{1,0:T(8,128)(2,1)} %get-tuple-element.39) | data formatting | bytes 524288 | tf_op jit(solution)/shard_map/all_to_all | solution.py:328
  100.7 7.4 %all-to-all-start.4 = ((bf16[32,4,1024]{2,1,0:T(4,128)(2,1)}), bf16[32,4,1024]{2,1,0:T(4,128)(2,1)S(1)}, u32[]{:S(2)}, u32[]{:S(2)}) async-start(bf16[32,4,1024]{2,1,0:T(4,128)(2,1)} %all_to_all.22), calls=%async_computation.4 | async-start | bytes 524288 | tf_op jit(solution)/shard_map/all_to_all | solution.py:328
  108.1 6.6 %collective-permute-done.1.refs_8_ = bf16[8,256,128]{2,1,0:T(8,128)(2,1)S(1)} collective-permute-done((bf16[8,256,128]{2,1,0:T(8,128)(2,1)}, bf16[8,256,128]{2,1,0:T(8,128)(2,1)S(1)}, u32[]{:S(2)}, u32[]{:S(2)}) %collective-permute-start.1) | collective-permute-done | bytes 524320 | tf_op jit(solution)/shard_map/ppermute | solution.py:326
  114.8 0.8 copy-done.5
  115.6 8.9 %shard_map.123 = bf16[8,640,128]{2,1,0:T(8,128)(2,1)} custom-call(s32[4]{0:T(128)} %and_select_fusion.refs_0_, bf16[8,384,128]{2,1,0:T(8,128)(2,1)} %copy-done.1, s32[8,128]{1,0:T(8,128)} %fusion.refs_2_.refs_6_, bf16[128,1024]{1,0:T(8,128)(2,1)} %get-tuple-element.23.refs_3_.refs_7_, bf16[128,1024]{1,0:T(8,128)(2,1)} %get-tuple-element.29.refs_4_, ...), custom_call_target="tpu_custom_call" | custom-call | flops 1073741824 | bytes 4198416 | tf_op jit(solution)/shard_map/pallas_call | solution.py:73
  124.5 0.7 copy-done.4
  125.2 3.6 %all-to-all-start.3 = ((bf16[8,640,128]{2,1,0:T(8,128)(2,1)}), bf16[8,640,128]{2,1,0:T(8,128)(2,1)S(1)}, u32[]{:S(2)}, u32[]{:S(2)}) async-start(bf16[8,640,128]{2,1,0:T(8,128)(2,1)} %shard_map.123), calls=%async_computation.3 | async-start | bytes 2621440 | tf_op jit(solution)/shard_map/all_to_all | solution.py:282
  128.8 1.1 convert_reduce_fusion.1
  129.9 1.9 %collective-permute-start.2 = (f32[4,1024]{1,0:T(4,128)S(1)}, f32[4,1024]{1,0:T(4,128)S(1)}, u32[]{:S(2)}, u32[]{:S(2)}) collective-permute-start(f32[4,1024]{1,0:T(4,128)S(1)} %convert_reduce_fusion.1), channel_id=1, source_target_pairs={{0,0},{1,32},{2,64},{3,96},{4,128},{5,160},{6,192},{7,224},{8,1},{... | collective-permute-start | bytes 49160 | tf_op jit(solution)/shard_map/ppermute | solution.py:336
  131.8 7.0 %collective-permute-done.2 = f32[4,1024]{1,0:T(4,128)S(1)} collective-permute-done((f32[4,1024]{1,0:T(4,128)S(1)}, f32[4,1024]{1,0:T(4,128)S(1)}, u32[]{:S(2)}, u32[]{:S(2)}) %collective-permute-start.2) | collective-permute-done | bytes 16416 | tf_op jit(solution)/shard_map/ppermute | solution.py:336
  138.8 9.4 %all-to-all-done.3.refs_0_ = bf16[8,640,128]{2,1,0:T(8,128)(2,1)S(1)} async-done(((bf16[8,640,128]{2,1,0:T(8,128)(2,1)}), bf16[8,640,128]{2,1,0:T(8,128)(2,1)S(1)}, u32[]{:S(2)}, u32[]{:S(2)}) %all-to-all-start.3) | async-done | bytes 1310752 | tf_op jit(solution)/shard_map/all_to_all | solution.py:282
  148.2 2.4 %shard_map.124 = (bf16[128,1024]{1,0:T(8,128)(2,1)}, bf16[128,1024]{1,0:T(8,128)(2,1)}, bf16[128,1024]{1,0:T(8,128)(2,1)}, bf16[128,1024]{1,0:T(8,128)(2,1)}, bf16[128,1024]{1,0:T(8,128)(2,1)}) custom-call(bf16[8,640,128]{2,1,0:T(8,128)(2,1)S(1)} %all-to-all-done.3.refs_0_, bf16[1024,1024]{1,0:T(8,128)(2,1)S(1)} %copy-done), custom_call_target="tpu_custom_call" | custom-call | flops 268435456 | bytes 4718592 | tf_op jit(solution)/shard_map/pallas_call | solution.py:73
  150.7 0.6 copy.14
  (18 shorter events, 0.2 us)
Async XLA Ops:
  7.2 30.2 %copy-start.6 = (s32[1,8192]{1,0:T(1,128)S(1)}, s32[1,8192]{1,0:T(1,128)}, u32[]{:S(2)}) copy-start(s32[1,8192]{1,0:T(1,128)} %param.12) | copy-start | bytes 98308
  7.2 78.3 %all-gather.2.cloned.1.call-start = ((), (), s32[]{:S(2)}) async-start(), calls=%async_computation.5 | async-start | bytes 2359296 | tf_op jit(solution)/shard_map/all_gather | solution.py:288
  33.1 17.5 %all-to-all-start = ((bf16[8,384,128]{2,1,0:T(8,128)(2,1)}), bf16[8,384,128]{2,1,0:T(8,128)(2,1)S(1)}, u32[]{:S(2)}, u32[]{:S(2)}) async-start(bf16[8,384,128]{2,1,0:T(8,128)(2,1)} %shard_map.118), calls=%async_computation | async-start | bytes 1572864 | tf_op jit(solution)/shard_map/all_to_all | solution.py:282
  50.5 6.4 %copy-start.1 = (bf16[8,384,128]{2,1,0:T(8,128)(2,1)}, bf16[8,384,128]{2,1,0:T(8,128)(2,1)S(1)}, u32[]{:S(2)}) copy-start(bf16[8,384,128]{2,1,0:T(8,128)(2,1)S(1)} %all-to-all-done.refs_1_.refs_5_) | copy-start | bytes 2359300
  50.6 20.2 %collective-permute-start = (bf16[8,256,128]{2,1,0:T(8,128)(2,1)S(1)}, bf16[8,256,128]{2,1,0:T(8,128)(2,1)S(1)}, u32[]{:S(2)}, u32[]{:S(2)}) collective-permute-start(bf16[8,256,128]{2,1,0:T(8,128)(2,1)S(1)} %slice.8), channel_id=1, source_target_pairs={{0,8},{8,16},{16,24},{24,32},{32,40},{40,48},{48,56},{1,9},{9,17},... | collective-permute-start | bytes 1572872 | tf_op jit(solution)/shard_map/ppermute | solution.py:310
  57.0 13.8 %all-to-all-start.1 = ((bf16[8,256,128]{2,1,0:T(8,128)(2,1)}), bf16[8,256,128]{2,1,0:T(8,128)(2,1)S(1)}, u32[]{:S(2)}, u32[]{:S(2)}) async-start(bf16[8,256,128]{2,1,0:T(8,128)(2,1)} %shard_map.120), calls=%async_computation.1 | async-start | bytes 1048576 | tf_op jit(solution)/shard_map/all_to_all | solution.py:282
  70.7 0.8 copy-start.2
  70.7 1.0 copy-start.3
  90.5 24.3 %collective-permute-start.1 = (bf16[8,256,128]{2,1,0:T(8,128)(2,1)}, bf16[8,256,128]{2,1,0:T(8,128)(2,1)S(1)}, u32[]{:S(2)}, u32[]{:S(2)}) collective-permute-start(bf16[8,256,128]{2,1,0:T(8,128)(2,1)} %get-tuple-element.33), channel_id=1, source_target_pairs={{8,0},{16,8},{24,16},{32,24},{40,32},{48,40},{56,48},{9,1},{17,9},... | collective-permute-start | bytes 1572872 | tf_op jit(solution)/shard_map/ppermute | solution.py:326
  100.7 23.8 %all-to-all-start.4 = ((bf16[32,4,1024]{2,1,0:T(4,128)(2,1)}), bf16[32,4,1024]{2,1,0:T(4,128)(2,1)S(1)}, u32[]{:S(2)}, u32[]{:S(2)}) async-start(bf16[32,4,1024]{2,1,0:T(4,128)(2,1)} %all_to_all.22), calls=%async_computation.4 | async-start | bytes 524288 | tf_op jit(solution)/shard_map/all_to_all | solution.py:328
  114.8 0.8 copy-start.5
  124.5 23.7 %copy-start = (bf16[1024,1024]{1,0:T(8,128)(2,1)S(1)}, bf16[1024,1024]{1,0:T(8,128)(2,1)}, u32[]{:S(2)}) copy-start(bf16[1024,1024]{1,0:T(8,128)(2,1)} %refs_1_.1) | copy-start | bytes 6291460
  124.5 0.7 copy-start.4
  125.2 23.0 %all-to-all-start.3 = ((bf16[8,640,128]{2,1,0:T(8,128)(2,1)}), bf16[8,640,128]{2,1,0:T(8,128)(2,1)S(1)}, u32[]{:S(2)}, u32[]{:S(2)}) async-start(bf16[8,640,128]{2,1,0:T(8,128)(2,1)} %shard_map.123), calls=%async_computation.3 | async-start | bytes 2621440 | tf_op jit(solution)/shard_map/all_to_all | solution.py:282
  129.9 9.0 %collective-permute-start.2 = (f32[4,1024]{1,0:T(4,128)S(1)}, f32[4,1024]{1,0:T(4,128)S(1)}, u32[]{:S(2)}, u32[]{:S(2)}) collective-permute-start(f32[4,1024]{1,0:T(4,128)S(1)} %convert_reduce_fusion.1), channel_id=1, source_target_pairs={{0,0},{1,32},{2,64},{3,96},{4,128},{5,160},{6,192},{7,224},{8,1},{... | collective-permute-start | bytes 49160 | tf_op jit(solution)/shard_map/ppermute | solution.py:336
Sparse Core Ops, SparseCore 0:
  9.9 29.2 all-gather.1

commit v3 on v2

v3 whole, which is shorter than its diff:
```python
import functools
import math

import jax
import jax.numpy as jnp
from jax import lax
from jax.experimental import pallas as pl
from jax.experimental.pallas import tpu as pltpu
from jax.sharding import Mesh
from jax.sharding import PartitionSpec as P

HEADS = 8
EPS = 1e-05
USERS = 32
TOK = 128
PLANE = 1024
TILE = 256
TILES = PLANE // TILE
SCALE = 1.0 / math.sqrt(128.0)
F32 = jnp.float32
BF16 = jnp.bfloat16
PLANE_AXES = ("x", "c")
VMEM_LIMIT = 60 * 1024 * 1024
ROOM = 30 * 1024 * 1024

NN = (((1,), (0,)), ((), ()))
NT = (((1,), (1,)), ((), ()))
TN = (((0,), (0,)), ((), ()))


def dot(a, b, dims=NN):
    return lax.dot_general(a, b, dims, preferred_element_type=F32)


def flip(block):
    return block.astype(F32).T.astype(BF16)


class Held:
    def __init__(self, ref, copy):
        self.ref, self.copy = ref, copy

    def get(self):
        if self.copy is not None:
            self.copy.wait()
            self.copy = None
        return self.ref


class Made:
    def __init__(self, ref, target, log):
        self.ref, self.target, self.log = ref, target, log

    def send(self, src=(), dst=None):
        where = src if dst is None else dst
        self.log((self.ref.at[src] if src != () else self.ref, self.target.at[where] if where != () else self.target))


def call(body, places, outs, flops, scratch=(), limit=VMEM_LIMIT, sends=16, kept=None, held=None):
    outs, kept, held = list(outs), dict(kept or {}), dict(held or {})

    def build(*args):
        staged = [n for n, place in enumerate(places) if place == "h"]
        shapes = [held[n][1] if n in held else args[n].shape for n in staged]

        def whole(*refs):
            refs = list(refs)
            given, refs = refs[: len(args)], refs[len(args) :]
            results, refs = refs[: len(outs)], refs[len(outs) :]
            here, refs = refs[: len(staged)], refs[len(staged) :]
            made, refs = refs[: len(outs)], refs[len(outs) :]
            in_sems, out_sems, extra = refs[0], refs[1], refs[2:]
            for m, n in enumerate(staged):
                source = given[n].at[held[n][0]] if n in held else given[n]
                copy = pltpu.make_async_copy(source, here[m], in_sems.at[m])
                copy.start()
                given[n] = Held(here[m], copy)
            sent = []

            def log(pair):
                copy = pltpu.make_async_copy(pair[0], pair[1], out_sems.at[len(sent)])
                copy.start()
                sent.append(copy)

            body(*(g for g, place in zip(given, places) if place != "a"), *(Made(v, t, log) for v, t in zip(made, results)), *extra)
            for n in staged:
                given[n].get()
            for copy in sent:
                copy.wait()

        moved = sum(a.size * a.dtype.itemsize for a in args) + sum(o.size * o.dtype.itemsize for o in outs)
        return pl.pallas_call(
            whole,
            out_shape=outs,
            in_specs=[pl.BlockSpec(memory_space=pltpu.SMEM if place == "s" else pltpu.HBM) for place in places],
            out_specs=[pl.BlockSpec(memory_space=pltpu.HBM)] * len(outs),
            input_output_aliases={places.index("a"): 0} if "a" in places else {},
            scratch_shapes=[pltpu.VMEM(dims, args[n].dtype) for dims, n in zip(shapes, staged)]
            + [pltpu.VMEM(kept.get(m, o.shape), o.dtype) for m, o in enumerate(outs)]
            + [pltpu.SemaphoreType.DMA((len(staged) + 1,)), pltpu.SemaphoreType.DMA((sends,))]
            + list(scratch),
            compiler_params=pltpu.CompilerParams(vmem_limit_bytes=limit),
            cost_estimate=pl.CostEstimate(flops=flops, bytes_accessed=moved, transcendentals=0),
        )(*args)

    return build


def shape(dims, dtype):
    return jax.ShapeDtypeStruct(dims, dtype)


def pack_body(q, k, v, out):
    for n, held in enumerate((q, k, v)):
        ref = held.get()
        rows = slice(n * TOK, (n + 1) * TOK)
        for h in range(HEADS):
            out.ref[h, rows, :] = ref[:, h * TOK : (h + 1) * TOK]
        out.send((slice(None), rows))


def dgated_body(cot, gate, w, out):
    gate_ref = gate.get()
    for h in range(HEADS):
        out.ref[h, 0:128, :] = flip(gate_ref[:, h * TOK : (h + 1) * TOK])
    cotangent, w_ref = cot.get()[...], w.get()
    for h in range(HEADS):
        out.ref[h, 128:256, :] = dot(w_ref[h * TOK : (h + 1) * TOK, :], cotangent, NT).astype(BF16)
    out.send()


def tile_of(ref, j, rows):
    return ref[pl.ds(2 * j, 2), rows, :].reshape(TILE, 128)


def tile_mask(start_ref, i, first_key):
    start = jnp.concatenate([start_ref[2 * i : 2 * i + 1, :], start_ref[2 * i + 1 : 2 * i + 2, :]], axis=1)
    key_place = first_key + lax.broadcasted_iota(jnp.int32, (TILE, TILE), 0)
    query_place = i * TILE + lax.broadcasted_iota(jnp.int32, (TILE, TILE), 1)
    return (key_place >= start) & (key_place <= query_place)


def sigmoid(s):
    return 1.0 / (1.0 + jnp.exp(-s))


def flip_tiles(ref, rows, tiles):
    for t in range(HEADS):
        tiles[t // 2, :, (t % 2) * TOK : (t % 2 + 1) * TOK] = flip(ref[t, rows, :])


def forward_tiles(i, low, high, first, keys_ref, key_rows, start_ref, qt, vt_ref, total):
    def step(j, acc):
        s = dot(tile_of(keys_ref, j, key_rows), qt) * SCALE
        mask = tile_mask(start_ref, i, first + j * TILE)
        w = jnp.where(mask, s * sigmoid(s), 0.0).astype(BF16)
        return acc + dot(vt_ref[j], w)

    return lax.fori_loop(low, high, step, total)


def fwd_own_body(low_ref, recv, start, mixt, qt, vt_ref):
    recv_ref, start_ref = recv.get(), start.get()
    flip_tiles(recv_ref, slice(0, 128), qt.ref)
    qt.send()
    flip_tiles(recv_ref, slice(256, 384), vt_ref)
    for i in range(TILES):
        low = jnp.maximum(low_ref[i] - TILES, 0)
        mixt.ref[i] = forward_tiles(
            i, low, i + 1, 0, recv_ref, slice(128, 256), start_ref, qt.ref[i], vt_ref, jnp.zeros((128, TILE), F32)
        )
        mixt.send((i,))


def fwd_halo_body(low_ref, halo, start, qt, part, gd, mixt, stats, vt_ref):
    halo_ref, start_ref = halo.get(), start.get()
    flip_tiles(halo_ref, slice(128, 256), vt_ref)
    qt_ref, part_ref, gd_ref = qt.get(), part.get(), gd.get()
    for i in range(TILES):
        mixt.ref[i] = forward_tiles(
            i, low_ref[i], TILES, -PLANE, halo_ref, slice(0, 128), start_ref, qt_ref[i], vt_ref, part_ref[i]
        )
        mixt.send((i,))
        for b in (2 * i, 2 * i + 1):
            mix = mixt.ref[i, :, (b % 2) * TOK : (b % 2 + 1) * TOK]
            dn = gd_ref[b, 0:128, :].astype(F32) * gd_ref[b, 128:256, :].astype(F32)
            mean = jnp.sum(mix, axis=0, keepdims=True) * (1.0 / 128.0)
            centred = mix - mean
            rows = (
                mean,
                jnp.sum(centred * centred, axis=0, keepdims=True),
                jnp.sum(dn, axis=0, keepdims=True),
                jnp.sum(dn * centred, axis=0, keepdims=True),
            )
            for k, row in enumerate(rows):
                stats.ref[0, 8 * k + b : 8 * k + b + 1, :] = row
    for d in range(HEADS):
        stats.send((0,), (d,))


def finish(mixt_ref, gd_ref, stats_ref, gate_out, dmix_ref):
    means = [stats_ref[h, 0:8, :] for h in range(HEADS)]
    mean = sum(means) * (1.0 / HEADS)
    square = sum(stats_ref[h, 8:16, :] for h in range(HEADS))
    square = square + 128.0 * sum((m - mean) * (m - mean) for m in means)
    inverse = lax.rsqrt(square * (1.0 / 1024.0) + EPS)
    dmean = sum(stats_ref[h, 16:24, :] for h in range(HEADS)) * (1.0 / 1024.0)
    cross = sum(stats_ref[h, 24:32, :] + (means[h] - mean) * stats_ref[h, 16:24, :] for h in range(HEADS))
    dcross = cross * inverse * (1.0 / 1024.0)
    for b in range(HEADS):
        cols = slice((b % 2) * TOK, (b % 2 + 1) * TOK)
        one = slice(b, b + 1)
        inv = inverse[one, :]
        normed = (mixt_ref[b // 2, :, cols] - mean[one, :]) * inv
        gate = gd_ref[b, 0:128, :].astype(F32)
        dgated = gd_ref[b, 128:256, :].astype(F32)
        gate_out[b, 0:128, :] = (normed * gate).astype(BF16)
        gate_out[b, 128:256, :] = (normed * dgated).astype(BF16)
        dmix_ref[b // 2, :, cols] = (inv * (dgated * gate - dmean[one, :] - normed * dcross[one, :])).astype(BF16)


def backward_tiles(i, low, high, first, keys_ref, key_rows, value_rows, start_ref, qt, q, dmt, kt_ref, dk_ref, dv_ref, total):
    def step(j, acc):
        s = dot(tile_of(keys_ref, j, key_rows), qt) * SCALE
        mask = tile_mask(start_ref, i, first + j * TILE)
        sig = sigmoid(s)
        w = jnp.where(mask, s * sig, 0.0).astype(BF16)
        dw = dot(tile_of(keys_ref, j, value_rows), dmt)
        ds = jnp.where(mask, dw * (sig * (1.0 + s * (1.0 - sig))) * SCALE, 0.0).astype(BF16)
        dv_ref[j] += dot(w, dmt, NT)
        dk_ref[j] += dot(ds, q)
        return acc + dot(kt_ref[j], ds)

    return lax.fori_loop(low, high, step, total)


def middle_body(
    low_ref, who_ref, mixt, gd, stats, halo, recv, start, qt, cot, sent, dmix, dqt, back, own, far1, far2, far3, kt_ref, dk_ref, dv_ref
):
    finish(mixt.get(), gd.get(), stats.get(), sent.ref, dmix.ref)
    sent.send((), (slice(None), slice(0, 256)))
    dmix.send()
    halo_ref, recv_ref, start_ref, qt_ref = halo.get(), recv.get(), start.get(), qt.get()
    flip_tiles(halo_ref, slice(0, 128), kt_ref)
    dk_ref[...] = jnp.zeros_like(dk_ref)
    dv_ref[...] = jnp.zeros_like(dv_ref)
    for i in range(TILES):
        dqt.ref[i] = backward_tiles(
            i, low_ref[i], TILES, -PLANE, halo_ref, slice(0, 128), slice(128, 256), start_ref, qt_ref[i],
            tile_of(recv_ref, i, slice(0, 128)), dmix.ref[i], kt_ref, dk_ref, dv_ref, jnp.zeros((128, TILE), F32),
        )
    dqt.send()
    for j in range(TILES):
        back.ref[2 * j : 2 * j + 2, 0:128, :] = dk_ref[j].astype(BF16).reshape(2, 128, 128)
        back.ref[2 * j : 2 * j + 2, 128:256, :] = dv_ref[j].astype(BF16).reshape(2, 128, 128)
    back.send()
    row = lax.broadcasted_iota(jnp.int32, (128, 128), 0)
    feature = lax.broadcasted_iota(jnp.int32, (128, 128), 1)
    replica = jnp.bitwise_and(row // 32 + who_ref[0], 3)
    plane = jnp.bitwise_and(row // 4 + who_ref[1], 7)
    pick = jnp.where(feature == 32 * replica + 4 * plane + jnp.bitwise_and(row, 3), 1.0, 0.0).astype(BF16)
    cot_ref = cot.get()
    total = jnp.zeros((128, 1024), F32)
    for b in range(HEADS):
        total = total + dot(dot(pick, sent.ref[b, 0:128, :]).astype(BF16), cot_ref[b])
    own.ref[...] = total[0:32]
    own.send()
    for n, far in enumerate((far1, far2, far3)):
        far.ref[...] = total[32 * (n + 1) : 32 * (n + 2)].astype(BF16)
        far.send()


def replica_sum_body(own, got1, got2, got3, *outs):
    total = own.get()[...]
    for got in (got1, got2, got3):
        total = total + got.get()[...].astype(F32)
    for s, out in enumerate(outs):
        out.ref[...] = total[4 * s : 4 * s + 4]
        out.send()


def bwd_own_body(low_ref, recv, start, qt, dmix, part, out, dk, dv, kt_ref):
    recv_ref, start_ref = recv.get(), start.get()
    flip_tiles(recv_ref, slice(128, 256), kt_ref)
    dk.ref[...] = jnp.zeros_like(dk.ref)
    dv.ref[...] = jnp.zeros_like(dv.ref)
    qt_ref, dmix_ref, part_ref = qt.get(), dmix.get(), part.get()
    for i in range(TILES - 1, -1, -1):
        low = jnp.maximum(low_ref[i] - TILES, 0)
        dqt = backward_tiles(
            i, low, i + 1, 0, recv_ref, slice(128, 256), slice(256, 384), start_ref, qt_ref[i],
            tile_of(recv_ref, i, slice(0, 128)), dmix_ref[i], kt_ref, dk.ref, dv.ref, part_ref[i],
        )
        out.ref[2 * i : 2 * i + 2] = dqt.T.astype(BF16).reshape(2, 128, 128)
        blocks = slice(2 * i, 2 * i + 2)
        out.send((blocks,), (blocks, slice(256, 384)))
        dk.send((i,))
        dv.send((i,))


def add_body(dk, dv, back, out):
    next_ref, dk_ref, dv_ref = back.get(), dk.get(), dv.get()
    for b in range(HEADS):
        rows = slice((b % 2) * TOK, (b % 2 + 1) * TOK)
        out.ref[b, 0:128, :] = (dk_ref[b // 2, rows, :] + next_ref[b, 0:128, :].astype(F32)).astype(BF16)
        out.ref[b, 128:256, :] = (dv_ref[b // 2, rows, :] + next_ref[b, 128:256, :].astype(F32)).astype(BF16)
    out.send((), (slice(None), slice(384, 640)))


def final_body(recv, w, p0, p1, p2, p3, p4, p5, p6, p7, out, dq, dk, dv, gg, wg):
    total = p0.get()[...]
    for piece in (p1, p2, p3, p4, p5, p6, p7):
        total = total + piece.get()[...]
    wg.ref[...] = total
    wg.send()
    recv_ref, w_ref = recv.get(), w.get()
    for n, made in enumerate((dq, dk, dv)):
        for h in range(HEADS):
            made.ref[:, h * TOK : (h + 1) * TOK] = recv_ref[h, 256 + 128 * n : 384 + 128 * n, :]
        made.send()
    for h in range(HEADS):
        gg.ref[:, h * TOK : (h + 1) * TOK] = flip(recv_ref[h, 128:256, :])
    gg.send()
    total = dot(flip(recv_ref[0, 0:128, :]), w_ref[0:TOK, :])
    for h in range(1, HEADS):
        total = total + dot(flip(recv_ref[h, 0:128, :]), w_ref[h * TOK : (h + 1) * TOK, :])
    out.ref[...] = total.astype(BF16)
    out.send()


def plane_exchange(blocks):
    return lax.all_to_all(blocks, PLANE_AXES, 0, 0, tiled=True)


def shards(sizes, queries, keys, values, gates, cotangent, segment, w_out):
    dp, planes = sizes
    q, k, v, gate, cot, seg = (a[0] for a in (queries, keys, values, gates, cotangent, segment))
    cot_plane = lax.all_gather(cot, PLANE_AXES)
    rows = shape((TOK, 1024), BF16)
    head = shape((TILES, 128, TILE), F32)
    head16 = shape((TILES, 128, TILE), BF16)
    share = shape((4, 1024), F32)
    grad = shape((TILES, TILE, 128), F32)
    vt = pltpu.VMEM((TILES, 128, TILE), BF16)
    acc = pltpu.VMEM((TILES, TILE, 128), F32)

    (packed,) = call(pack_body, "hhh", [shape((8, 384, 128), BF16)], 1 << 16)(q, k, v)
    recv = plane_exchange(packed)

    replica, plane = lax.axis_index("dp"), lax.axis_index("z")
    who = jnp.stack([replica, plane]).astype(jnp.int32)
    place = plane * PLANE
    users = jnp.arange(USERS, dtype=jnp.int32)[:, None]
    first = jnp.sum((seg[None, :] < users).astype(jnp.int32), axis=1)
    mine = lax.dynamic_slice_in_dim(seg, place, PLANE)
    start = jnp.sum(jnp.where(mine[None, :] == users, first[:, None], 0), axis=0) - place
    low = (start[::TILE] + PLANE) // TILE
    start = start.reshape(8, 128)
    (gd,) = call(dgated_body, "hhh", [shape((8, 256, 128), BF16)], 1 << 28)(cot, gate, w_out)

    pair, gd, start, low, who = lax.optimization_barrier((recv[:, 128:384], gd, start, low, who))
    halo = lax.ppermute(pair, "z", [(i, i + 1) for i in range(planes - 1)])
    gd_recv = plane_exchange(gd)
    part, qt = call(fwd_own_body, "shh", [head, head16], 1 << 29, [vt])(low, recv, start)
    mixt, stats = call(fwd_halo_body, "shhhhh", [head, shape((8, 32, 128), F32)], 1 << 28, [vt], kept={1: (1, 32, 128)})(
        low, halo, start, qt, part, gd_recv
    )
    stats = plane_exchange(stats)

    only_q = {6: ((slice(None), slice(0, 128)), (8, 128, 128))}
    far = shape((32, 1024), BF16)
    sent, dmix, dqt, back, own, *fars = call(
        middle_body, "sshhhhhhhh",
        [shape((8, 640, 128), BF16), head16, head, shape((8, 256, 128), BF16), shape((32, 1024), F32), far, far, far],
        1 << 29, [vt, acc, acc], kept={0: (8, 256, 128)}, held=only_q,
    )(low, who, mixt, gd_recv, stats, halo, recv, start, qt, cot_plane)
    back = lax.ppermute(back, "z", [(i, i - 1) for i in range(1, planes)])
    fars = [lax.ppermute(x, "dp", [(i, (i + n + 1) % dp) for i in range(dp)]) for n, x in enumerate(fars)]
    pieces = call(replica_sum_body, "hhhh", [share] * 8, 1 << 16)(own, *fars)
    sent, dk, dv = call(
        bwd_own_body, "shhhhha", [shape((8, 640, 128), BF16), grad, grad], 1 << 30, [vt], kept={0: (8, 128, 128)}
    )(low, recv, start, qt, dmix, dqt, sent)
    (sent,) = call(add_body, "hhha", [shape((8, 640, 128), BF16)], 1 << 20, kept={0: (8, 256, 128)})(dk, dv, back, sent)
    sent, pieces = lax.optimization_barrier((sent, pieces))
    landed = []
    for s, piece in enumerate(pieces):
        route = []
        for d in range(dp):
            for z in range(planes):
                for r in range(8):
                    owner = (r // 2 * planes + (r % 2) * 4 + d) * 8 + (z + s) % 8
                    route.append(((d * planes + z) * 8 + r, owner))
        landed.append(lax.ppermute(piece, ("dp", "z", "x", "c"), route))
    got = plane_exchange(sent)
    out, dq, dk, dv, gg, weight_grad = call(final_body, "h" * 10, [rows] * 5 + [share], 1 << 28, (), ROOM)(got, w_out, *landed)
    return out[None], dq[None], dk[None], dv[None], gg[None], weight_grad


def solution(mesh):
    dp, seq = mesh.shape["dp"], mesh.shape["seq"]
    planes = seq // 8
    grid = Mesh(mesh.devices.reshape(dp, planes, 4, 2), ("dp", "z", "x", "c"))
    tokens = P("dp", ("z", "x", "c"), None)
    return jax.shard_map(
        functools.partial(shards, (dp, planes)),
        mesh=grid,
        in_specs=(tokens,) * 5 + (P("dp", None), P()),
        out_specs=(tokens,) * 5 + (P(("dp", "z", "x", "c"), None),),
        check_vma=False,
    )
```

time: 159 us -> 158 us (level)
  the two profiles are of different devices: /device:TPU:128 before, /device:TPU:19 now
where the time goes in v3:
time: 158 us; the launch traced here: 157 us
  starting transfers between devices  70.8 us (45%)
  Pallas kernels  34.1 us (22%)
  waiting for transfers between devices  23 us (15%)
  between operations  14.4 us (9%)
  blocking collectives  9.82 us (6%)
  local copies, waits for them, and re-layouts  2.56 us (2%)
  other arithmetic  2.13 us (1%)
    ppermute x8, starting transfers between devices, shards(): landed.append(lax.ppermute(piece, ('dp', 'z', 'x', 'c'), route))  46.6 us
    pallas_call x9, Pallas kernels, build(): pl.pallas_call(whole, out_shape=outs, in_specs=[pl.BlockSpec(memory_space...  34.1 us
    all_to_all x3, starting transfers between devices, plane_exchange(): return lax.all_to_all(blocks, PLANE_AXES, 0, 0, tiled=True)  17 us
    ppermute x8, waiting for transfers between devices, shards(): landed.append(lax.ppermute(piece, ('dp', 'z', 'x', 'c'), route))  10.3 us
    all_to_all x1, blocking collectives, plane_exchange(): return lax.all_to_all(blocks, PLANE_AXES, 0, 0, tiled=True)  9.82 us
    all_to_all x3, waiting for transfers between devices, plane_exchange(): return lax.all_to_all(blocks, PLANE_AXES, 0, 0, tiled=True)  8.12 us
    ppermute x1, waiting for transfers between devices, shards(): back = lax.ppermute(back, 'z', [(i, i - 1) for i in range(1, planes)])  3.89 us
    ppermute x1, starting transfers between devices, shards(): halo = lax.ppermute(pair, 'z', [(i, i + 1) for i in range(planes - 1)])  3.57 us
  transfers between devices with their start and end apart: 17, of which 4 were waited for; matrix products, arithmetic and copies ran while one was open for 1% of the time, Pallas kernels for 15%

profile of v3, /device:TPU:19, one launch (start us, length us, event | category | flops | bytes accessed | tf_op | source)
XLA Modules:
  0.0 156.9 jit_solution(14340429048787900678)
XLA Ops:
  7.2 0.7 all-gather.2.cloned.1.call-update
  7.9 2.1 %shard_map.118 = bf16[8,384,128]{2,1,0:T(8,128)(2,1)} custom-call(bf16[128,1024]{1,0:T(8,128)(2,1)} %bitcast.18, bf16[128,1024]{1,0:T(8,128)(2,1)} %bitcast.19, bf16[128,1024]{1,0:T(8,128)(2,1)} %bitcast.20), custom_call_target="tpu_custom_call" | custom-call | flops 65536 | bytes 1572864 | tf_op jit(solution)/shard_map/pallas_call | solution.py:92
  10.0 5.2 %all-to-all-start = ((bf16[8,384,128]{2,1,0:T(8,128)(2,1)}), bf16[8,384,128]{2,1,0:T(8,128)(2,1)S(1)}, u32[]{:S(2)}, u32[]{:S(2)}) async-start(bf16[8,384,128]{2,1,0:T(8,128)(2,1)} %shard_map.118), calls=%async_computation | async-start | bytes 1572864 | tf_op jit(solution)/shard_map/all_to_all | solution.py:332
  15.6 3.4 %shard_map.119 = bf16[8,256,128]{2,1,0:T(8,128)(2,1)} custom-call(bf16[128,1024]{1,0:T(8,128)(2,1)} %bitcast.16, bf16[128,1024]{1,0:T(8,128)(2,1)} %bitcast.17, bf16[1024,1024]{1,0:T(8,128)(2,1)} %refs_1_.1), custom_call_target="tpu_custom_call" | custom-call | flops 268435456 | bytes 3145728 | tf_op jit(solution)/shard_map/pallas_call | solution.py:92
  20.8 5.5 %all-to-all-done.refs_1_.refs_6_ = bf16[8,384,128]{2,1,0:T(8,128)(2,1)S(1)} async-done(((bf16[8,384,128]{2,1,0:T(8,128)(2,1)}), bf16[8,384,128]{2,1,0:T(8,128)(2,1)S(1)}, u32[]{:S(2)}, u32[]{:S(2)}) %all-to-all-start) | async-done | bytes 786464 | tf_op jit(solution)/shard_map/all_to_all | solution.py:332
  26.4 3.6 %collective-permute-start = (bf16[8,256,128]{2,1,0:T(8,128)(2,1)S(1)}, bf16[8,256,128]{2,1,0:T(8,128)(2,1)S(1)}, u32[]{:S(2)}, u32[]{:S(2)}) collective-permute-start(bf16[8,256,128]{2,1,0:T(8,128)(2,1)S(1)} %slice.8), channel_id=1, source_target_pairs={{0,8},{8,16},{16,24},{24,32},{32,40},{40,48},{48,56},{1,9},{9,17},... | collective-permute-start | bytes 1572872 | tf_op jit(solution)/shard_map/ppermute | solution.py:362
  30.0 5.7 %all-to-all-start.1 = ((bf16[8,256,128]{2,1,0:T(8,128)(2,1)}), bf16[8,256,128]{2,1,0:T(8,128)(2,1)S(1)}, u32[]{:S(2)}, u32[]{:S(2)}) async-start(bf16[8,256,128]{2,1,0:T(8,128)(2,1)} %shard_map.119), calls=%async_computation.1 | async-start | bytes 1048576 | tf_op jit(solution)/shard_map/all_to_all | solution.py:332
  35.6 6.1 %shard_map.120 = (f32[4,128,256]{2,1,0:T(8,128)}, bf16[4,128,256]{2,1,0:T(8,128)(2,1)}) custom-call(s32[4]{0:T(128)} %and_select_fusion.refs_0_, bf16[8,384,128]{2,1,0:T(8,128)(2,1)} %copy-done.1, s32[8,128]{1,0:T(8,128)} %fusion.refs_2_.refs_7_), custom_call_target="tpu_custom_call" | custom-call | flops 536870912 | bytes 1576976 | tf_op jit(solution)/shard_map/pallas_call | solution.py:92
  41.7 2.6 %all-to-all-done.1.refs_5_.refs_3_ = bf16[8,256,128]{2,1,0:T(8,128)(2,1)S(1)} async-done(((bf16[8,256,128]{2,1,0:T(8,128)(2,1)}), bf16[8,256,128]{2,1,0:T(8,128)(2,1)S(1)}, u32[]{:S(2)}, u32[]{:S(2)}) %all-to-all-start.1) | async-done | bytes 524320 | tf_op jit(solution)/shard_map/all_to_all | solution.py:332
  44.3 0.8 copy-done.2
  45.3 3.2 %shard_map.121 = (f32[4,128,256]{2,1,0:T(8,128)}, f32[8,32,128]{2,1,0:T(8,128)}) custom-call(s32[4]{0:T(128)} %and_select_fusion.refs_0_, bf16[8,256,128]{2,1,0:T(8,128)(2,1)} %copy-done.3, s32[8,128]{1,0:T(8,128)} %fusion.refs_2_.refs_7_, bf16[4,128,256]{2,1,0:T(8,128)(2,1)} %get-tuple-element.51.refs_3_.refs_8_, f32[4,128,256]{2,1,0:T(8,128)} %get-tuple-element.54.refs_4_, ...), custom_call_target="tpu_custom_call" | custom-call | flops 268435456 | bytes 2494480 | tf_op jit(solution)/shard_map/pallas_call | solution.py:92
  48.6 9.8 %all_to_all.20.refs_4_ = f32[8,32,128]{2,1,0:T(8,128)} all-to-all(f32[8,32,128]{2,1,0:T(8,128)} %get-tuple-element.57), channel_id=1, replica_groups=mesh['dp'=4,'z'=8,'x'=4,'c'=2] {'x','c'}, dimensions={0} | all-to-all | bytes 262144 | tf_op jit(solution)/shard_map/all_to_all | solution.py:332
  58.4 5.5 %shard_map.122 = (bf16[8,640,128]{2,1,0:T(8,128)(2,1)}, bf16[4,128,256]{2,1,0:T(8,128)(2,1)}, f32[4,128,256]{2,1,0:T(8,128)}, bf16[8,256,128]{2,1,0:T(8,128)(2,1...) custom-call(s32[4]{0:T(128)} %and_select_fusion.refs_0_, ...), custom_call_target="tpu_custom_call" | custom-call | flops 536870912 | bytes 7802904 | tf_op jit(solution)/shard_map/pallas_call | solution.py:92
  63.9 1.3 collective-permute-start.1
  65.2 1.1 collective-permute-start.2
  66.6 0.9 collective-permute-start.4
  67.5 7.2 %shard_map.123 = (bf16[8,640,128]{2,1,0:T(8,128)(2,1)}, f32[4,256,128]{2,1,0:T(8,128)}, f32[4,256,128]{2,1,0:T(8,128)}) custom-call(s32[4]{0:T(128)} %and_select_fusion.refs_0_, bf16[8,384,128]{2,1,0:T(8,128)(2,1)} %copy-done.1, s32[8,128]{1,0:T(8,128)} %fusion.refs_2_.refs_7_, ...), custom_call_target="tpu_custom_call", output_to_operand_aliasing={{0}: (6, {})} | custom-call | flops 1073741824 | bytes 5509136 | tf_op jit(solution)/shard_map/pallas_call | solution.py:92
  75.4 1.8 %shard_map.125 = (f32[4,1024]{1,0:T(4,128)}, f32[4,1024]{1,0:T(4,128)}, f32[4,1024]{1,0:T(4,128)}, f32[4,1024]{1,0:T(4,128)}, f32[4,1024]{1,0:T(4,128)}, /*index...) custom-call(f32[32,1024]{1,0:T(8,128)} %get-tuple-element.65.refs_0_, bf16[32,1024]{1,0:T(8,128)(2,1)} %copy-done.5, ...), custom_call_target="tpu_custom_call" | custom-call | flops 65536 | bytes 458752 | tf_op jit(solution)/shard_map/pallas_call | solution.py:92
  77.2 3.9 %collective-permute-done.1.refs_2_ = bf16[8,256,128]{2,1,0:T(8,128)(2,1)S(1)} collective-permute-done((bf16[8,256,128]{2,1,0:T(8,128)(2,1)}, bf16[8,256,128]{2,1,0:T(8,128)(2,1)S(1)}, u32[]{:S(2)}, u32[]{:S(2)}) %collective-permute-start.1) | collective-permute-done | bytes 524320 | tf_op jit(solution)/shard_map/ppermute | solution.py:377
  81.1 0.8 copy-done.4
  81.9 2.4 %shard_map.124 = bf16[8,640,128]{2,1,0:T(8,128)(2,1)} custom-call(f32[4,256,128]{2,1,0:T(8,128)} %get-tuple-element.61.refs_0_, f32[4,256,128]{2,1,0:T(8,128)} %get-tuple-element.62.refs_1_, bf16[8,256,128]{2,1,0:T(8,128)(2,1)} %copy-done.4, bf16[8,640,128]{2,1,0:T(8,128)(2,1)} %get-tuple-element.64.refs_3_), custom_call_target="tpu_custom_call", output_to_operand_aliasing={{}: (3, {})} | custom-call | flops 1048576 | bytes 4194304 | tf_op jit(solution)/shard_map/pallas_call | solution.py:92
  84.4 6.2 %all-to-all-start.3 = ((bf16[8,640,128]{2,1,0:T(8,128)(2,1)}), bf16[8,640,128]{2,1,0:T(8,128)(2,1)S(1)}, u32[]{:S(2)}, u32[]{:S(2)}) async-start(bf16[8,640,128]{2,1,0:T(8,128)(2,1)} %shard_map.124), calls=%async_computation.3 | async-start | bytes 2621440 | tf_op jit(solution)/shard_map/all_to_all | solution.py:332
  90.5 11.1 %collective-permute-start.5 = (f32[4,1024]{1,0:T(4,128)S(1)}, f32[4,1024]{1,0:T(4,128)S(1)}, u32[]{:S(2)}, u32[]{:S(2)}) collective-permute-start(f32[4,1024]{1,0:T(4,128)S(1)} %copy-done.12), channel_id=1, source_target_pairs={{0,0},{1,32},{2,64},{3,96},{4,128},{5,160},{6,192},{7,224},{8,1},{... | collective-permute-start | bytes 49160 | tf_op jit(solution)/shard_map/ppermute | solution.py:393
  101.7 5.7 %collective-permute-start.6 = (f32[4,1024]{1,0:T(4,128)S(1)}, f32[4,1024]{1,0:T(4,128)S(1)}, u32[]{:S(2)}, u32[]{:S(2)}) collective-permute-start(f32[4,1024]{1,0:T(4,128)S(1)} %copy-done.11), channel_id=1, source_target_pairs={{0,1},{1,33},{2,65},{3,97},{4,129},{5,161},{6,193},{7,225},{8,2},{... | collective-permute-start | bytes 49160 | tf_op jit(solution)/shard_map/ppermute | solution.py:393
  107.4 4.1 %collective-permute-start.7 = (f32[4,1024]{1,0:T(4,128)S(1)}, f32[4,1024]{1,0:T(4,128)S(1)}, u32[]{:S(2)}, u32[]{:S(2)}) collective-permute-start(f32[4,1024]{1,0:T(4,128)S(1)} %copy-done.10), channel_id=1, source_target_pairs={{0,2},{1,34},{2,66},{3,98},{4,130},{5,162},{6,194},{7,226},{8,3},{... | collective-permute-start | bytes 49160 | tf_op jit(solution)/shard_map/ppermute | solution.py:393
  111.5 1.9 %collective-permute-start.8 = (f32[4,1024]{1,0:T(4,128)}, f32[4,1024]{1,0:T(4,128)S(1)}, u32[]{:S(2)}, u32[]{:S(2)}) collective-permute-start(f32[4,1024]{1,0:T(4,128)} %get-tuple-element.81), channel_id=1, source_target_pairs={{0,3},{1,35},{2,67},{3,99},{4,131},{5,163},{6,195},{7,227},{8,4},{... | collective-permute-start | bytes 49160 | tf_op jit(solution)/shard_map/ppermute | solution.py:393
  113.5 5.9 %collective-permute-start.9 = (f32[4,1024]{1,0:T(4,128)}, f32[4,1024]{1,0:T(4,128)S(1)}, u32[]{:S(2)}, u32[]{:S(2)}) collective-permute-start(f32[4,1024]{1,0:T(4,128)} %get-tuple-element.82), channel_id=1, source_target_pairs={{0,4},{1,36},{2,68},{3,100},{4,132},{5,164},{6,196},{7,228},{8,5},... | collective-permute-start | bytes 49160 | tf_op jit(solution)/shard_map/ppermute | solution.py:393
  119.4 4.4 %collective-permute-start.10 = (f32[4,1024]{1,0:T(4,128)}, f32[4,1024]{1,0:T(4,128)S(1)}, u32[]{:S(2)}, u32[]{:S(2)}) collective-permute-start(f32[4,1024]{1,0:T(4,128)} %get-tuple-element.83), channel_id=1, source_target_pairs={{0,5},{1,37},{2,69},{3,101},{4,133},{5,165},{6,197},{7,229},{8,6},... | collective-permute-start | bytes 49160 | tf_op jit(solution)/shard_map/ppermute | solution.py:393
  123.8 11.5 %collective-permute-start.11 = (f32[4,1024]{1,0:T(4,128)}, f32[4,1024]{1,0:T(4,128)S(1)}, u32[]{:S(2)}, u32[]{:S(2)}) collective-permute-start(f32[4,1024]{1,0:T(4,128)} %get-tuple-element.84), channel_id=1, source_target_pairs={{0,6},{1,38},{2,70},{3,102},{4,134},{5,166},{6,198},{7,230},{8,7},... | collective-permute-start | bytes 49160 | tf_op jit(solution)/shard_map/ppermute | solution.py:393
  135.3 1.9 %collective-permute-start.12 = (f32[4,1024]{1,0:T(4,128)S(1)}, f32[4,1024]{1,0:T(4,128)S(1)}, u32[]{:S(2)}, u32[]{:S(2)}) collective-permute-start(f32[4,1024]{1,0:T(4,128)S(1)} %copy-done.9), channel_id=1, source_target_pairs={{0,7},{1,39},{2,71},{3,103},{4,135},{5,167},{6,199},{7,231},{8,0},... | collective-permute-start | bytes 49160 | tf_op jit(solution)/shard_map/ppermute | solution.py:393
  137.3 10.3 %collective-permute-done.12.refs_9_ = f32[4,1024]{1,0:T(4,128)S(1)} collective-permute-done((f32[4,1024]{1,0:T(4,128)S(1)}, f32[4,1024]{1,0:T(4,128)S(1)}, u32[]{:S(2)}, u32[]{:S(2)}) %collective-permute-start.12) | collective-permute-done | bytes 16416 | tf_op jit(solution)/shard_map/ppermute | solution.py:393
  147.6 2.4 %shard_map.126 = (bf16[128,1024]{1,0:T(8,128)(2,1)}, bf16[128,1024]{1,0:T(8,128)(2,1)}, bf16[128,1024]{1,0:T(8,128)(2,1)}, bf16[128,1024]{1,0:T(8,128)(2,1)}, bf...) custom-call(bf16[8,640,128]{2,1,0:T(8,128)(2,1)S(1)} %all-to-all-done.3.refs_0_, bf16[1024,1024]{1,0:T(8,128)(2,1)S(1)} %copy-done, ...), custom_call_target="tpu_custom_call" | custom-call | flops 268435456 | bytes 4866048 | tf_op jit(solution)/shard_map/pallas_call | solution.py:92
  (48 shorter events, 3.6 us)
Async XLA Ops:
  7.2 51.2 %all-gather.2.cloned.1.call-start = ((), (), s32[]{:S(2)}) async-start(), calls=%async_computation.4 | async-start | bytes 2359296 | tf_op jit(solution)/shard_map/all_gather | solution.py:338
  7.9 7.2 %copy-start.8 = (s32[1,8192]{1,0:T(1,128)S(1)}, s32[1,8192]{1,0:T(1,128)}, u32[]{:S(2)}) copy-start(s32[1,8192]{1,0:T(1,128)} %param.12) | copy-start | bytes 98308
  10.0 16.3 %all-to-all-start = ((bf16[8,384,128]{2,1,0:T(8,128)(2,1)}), bf16[8,384,128]{2,1,0:T(8,128)(2,1)S(1)}, u32[]{:S(2)}, u32[]{:S(2)}) async-start(bf16[8,384,128]{2,1,0:T(8,128)(2,1)} %shard_map.118), calls=%async_computation | async-start | bytes 1572864 | tf_op jit(solution)/shard_map/all_to_all | solution.py:332
  26.3 9.3 %copy-start.1 = (bf16[8,384,128]{2,1,0:T(8,128)(2,1)}, bf16[8,384,128]{2,1,0:T(8,128)(2,1)S(1)}, u32[]{:S(2)}) copy-start(bf16[8,384,128]{2,1,0:T(8,128)(2,1)S(1)} %all-to-all-done.refs_1_.refs_6_) | copy-start | bytes 2359300
  26.4 18.0 %collective-permute-start = (bf16[8,256,128]{2,1,0:T(8,128)(2,1)S(1)}, bf16[8,256,128]{2,1,0:T(8,128)(2,1)S(1)}, u32[]{:S(2)}, u32[]{:S(2)}) collective-permute-start(bf16[8,256,128]{2,1,0:T(8,128)(2,1)S(1)} %slice.8), channel_id=1, source_target_pairs={{0,8},{8,16},{16,24},{24,32},{32,40},{40,48},{48,56},{1,9},{9,17},... | collective-permute-start | bytes 1572872 | tf_op jit(solution)/shard_map/ppermute | solution.py:362
  30.0 14.4 %all-to-all-start.1 = ((bf16[8,256,128]{2,1,0:T(8,128)(2,1)}), bf16[8,256,128]{2,1,0:T(8,128)(2,1)S(1)}, u32[]{:S(2)}, u32[]{:S(2)}) async-start(bf16[8,256,128]{2,1,0:T(8,128)(2,1)} %shard_map.119), calls=%async_computation.1 | async-start | bytes 1048576 | tf_op jit(solution)/shard_map/all_to_all | solution.py:332
  44.3 0.8 copy-start.2
  44.3 1.0 copy-start.3
  63.9 17.3 %collective-permute-start.1 = (bf16[8,256,128]{2,1,0:T(8,128)(2,1)}, bf16[8,256,128]{2,1,0:T(8,128)(2,1)S(1)}, u32[]{:S(2)}, u32[]{:S(2)}) collective-permute-start(bf16[8,256,128]{2,1,0:T(8,128)(2,1)} %get-tuple-element.63), channel_id=1, source_target_pairs={{8,0},{16,8},{24,16},{32,24},{40,32},{48,40},{56,48},{9,1},{17,9},... | collective-permute-start | bytes 1572872 | tf_op jit(solution)/shard_map/ppermute | solution.py:377
  65.2 9.6 %collective-permute-start.2 = (bf16[32,1024]{1,0:T(8,128)(2,1)}, bf16[32,1024]{1,0:T(8,128)(2,1)S(1)}, u32[]{:S(2)}, u32[]{:S(2)}) collective-permute-start(bf16[32,1024]{1,0:T(8,128)(2,1)} %get-tuple-element.66), channel_id=1, source_target_pairs={{0,64},{64,128},{128,192},{192,0},{1,65},{65,129},{129,193},{193,1... | collective-permute-start | bytes 196616 | tf_op jit(solution)/shard_map/ppermute | solution.py:378
  66.3 8.5 %collective-permute-start.3 = (bf16[32,1024]{1,0:T(8,128)(2,1)}, bf16[32,1024]{1,0:T(8,128)(2,1)S(1)}, u32[]{:S(2)}, u32[]{:S(2)}) collective-permute-start(bf16[32,1024]{1,0:T(8,128)(2,1)} %get-tuple-element.67), channel_id=1, source_target_pairs={{0,128},{64,192},{128,0},{192,64},{1,129},{65,193},{129,1},{193,65... | collective-permute-start | bytes 196616 | tf_op jit(solution)/shard_map/ppermute | solution.py:378
  66.6 8.2 %collective-permute-start.4 = (bf16[32,1024]{1,0:T(8,128)(2,1)}, bf16[32,1024]{1,0:T(8,128)(2,1)S(1)}, u32[]{:S(2)}, u32[]{:S(2)}) collective-permute-start(bf16[32,1024]{1,0:T(8,128)(2,1)} %get-tuple-element.68), channel_id=1, source_target_pairs={{0,192},{64,0},{128,64},{192,128},{1,193},{65,1},{129,65},{193,129... | collective-permute-start | bytes 196616 | tf_op jit(solution)/shard_map/ppermute | solution.py:378
  74.8 0.6 copy-start.5
  74.8 0.6 copy-start.6
  74.8 0.6 copy-start.7
  81.1 0.8 copy-start.4
  84.3 6.2 %copy-start.12 = (f32[4,1024]{1,0:T(4,128)S(1)}, f32[4,1024]{1,0:T(4,128)}, u32[]{:S(2)}) copy-start(f32[4,1024]{1,0:T(4,128)} %get-tuple-element.78) | copy-start | bytes 49156
  84.3 17.3 %copy-start.11 = (f32[4,1024]{1,0:T(4,128)S(1)}, f32[4,1024]{1,0:T(4,128)}, u32[]{:S(2)}) copy-start(f32[4,1024]{1,0:T(4,128)} %get-tuple-element.79) | copy-start | bytes 49156
  84.4 23.0 %copy-start.10 = (f32[4,1024]{1,0:T(4,128)S(1)}, f32[4,1024]{1,0:T(4,128)}, u32[]{:S(2)}) copy-start(f32[4,1024]{1,0:T(4,128)} %get-tuple-element.80) | copy-start | bytes 49156
  84.4 50.9 %copy-start.9 = (f32[4,1024]{1,0:T(4,128)S(1)}, f32[4,1024]{1,0:T(4,128)}, u32[]{:S(2)}) copy-start(f32[4,1024]{1,0:T(4,128)} %get-tuple-element.85) | copy-start | bytes 49156
  84.4 63.2 %copy-start = (bf16[1024,1024]{1,0:T(8,128)(2,1)S(1)}, bf16[1024,1024]{1,0:T(8,128)(2,1)}, u32[]{:S(2)}) copy-start(bf16[1024,1024]{1,0:T(8,128)(2,1)} %refs_1_.1) | copy-start | bytes 6291460
  84.4 63.2 %all-to-all-start.3 = ((bf16[8,640,128]{2,1,0:T(8,128)(2,1)}), bf16[8,640,128]{2,1,0:T(8,128)(2,1)S(1)}, u32[]{:S(2)}, u32[]{:S(2)}) async-start(bf16[8,640,128]{2,1,0:T(8,128)(2,1)} %shard_map.124), calls=%async_computation.3 | async-start | bytes 2621440 | tf_op jit(solution)/shard_map/all_to_all | solution.py:332
  90.5 28.8 %collective-permute-start.5 = (f32[4,1024]{1,0:T(4,128)S(1)}, f32[4,1024]{1,0:T(4,128)S(1)}, u32[]{:S(2)}, u32[]{:S(2)}) collective-permute-start(f32[4,1024]{1,0:T(4,128)S(1)} %copy-done.12), channel_id=1, source_target_pairs={{0,0},{1,32},{2,64},{3,96},{4,128},{5,160},{6,192},{7,224},{8,1},{... | collective-permute-start | bytes 49160 | tf_op jit(solution)/shard_map/ppermute | solution.py:393
  101.7 22.1 %collective-permute-start.6 = (f32[4,1024]{1,0:T(4,128)S(1)}, f32[4,1024]{1,0:T(4,128)S(1)}, u32[]{:S(2)}, u32[]{:S(2)}) collective-permute-start(f32[4,1024]{1,0:T(4,128)S(1)} %copy-done.11), channel_id=1, source_target_pairs={{0,1},{1,33},{2,65},{3,97},{4,129},{5,161},{6,193},{7,225},{8,2},{... | collective-permute-start | bytes 49160 | tf_op jit(solution)/shard_map/ppermute | solution.py:393
  107.4 27.9 %collective-permute-start.7 = (f32[4,1024]{1,0:T(4,128)S(1)}, f32[4,1024]{1,0:T(4,128)S(1)}, u32[]{:S(2)}, u32[]{:S(2)}) collective-permute-start(f32[4,1024]{1,0:T(4,128)S(1)} %copy-done.10), channel_id=1, source_target_pairs={{0,2},{1,34},{2,66},{3,98},{4,130},{5,162},{6,194},{7,226},{8,3},{... | collective-permute-start | bytes 49160 | tf_op jit(solution)/shard_map/ppermute | solution.py:393
  111.5 25.7 %collective-permute-start.8 = (f32[4,1024]{1,0:T(4,128)}, f32[4,1024]{1,0:T(4,128)S(1)}, u32[]{:S(2)}, u32[]{:S(2)}) collective-permute-start(f32[4,1024]{1,0:T(4,128)} %get-tuple-element.81), channel_id=1, source_target_pairs={{0,3},{1,35},{2,67},{3,99},{4,131},{5,163},{6,195},{7,227},{8,4},{... | collective-permute-start | bytes 49160 | tf_op jit(solution)/shard_map/ppermute | solution.py:393
  113.5 23.8 %collective-permute-start.9 = (f32[4,1024]{1,0:T(4,128)}, f32[4,1024]{1,0:T(4,128)S(1)}, u32[]{:S(2)}, u32[]{:S(2)}) collective-permute-start(f32[4,1024]{1,0:T(4,128)} %get-tuple-element.82), channel_id=1, source_target_pairs={{0,4},{1,36},{2,68},{3,100},{4,132},{5,164},{6,196},{7,228},{8,5},... | collective-permute-start | bytes 49160 | tf_op jit(solution)/shard_map/ppermute | solution.py:393
  119.4 17.9 %collective-permute-start.10 = (f32[4,1024]{1,0:T(4,128)}, f32[4,1024]{1,0:T(4,128)S(1)}, u32[]{:S(2)}, u32[]{:S(2)}) collective-permute-start(f32[4,1024]{1,0:T(4,128)} %get-tuple-element.83), channel_id=1, source_target_pairs={{0,5},{1,37},{2,69},{3,101},{4,133},{5,165},{6,197},{7,229},{8,6},... | collective-permute-start | bytes 49160 | tf_op jit(solution)/shard_map/ppermute | solution.py:393
  123.8 13.4 %collective-permute-start.11 = (f32[4,1024]{1,0:T(4,128)}, f32[4,1024]{1,0:T(4,128)S(1)}, u32[]{:S(2)}, u32[]{:S(2)}) collective-permute-start(f32[4,1024]{1,0:T(4,128)} %get-tuple-element.84), channel_id=1, source_target_pairs={{0,6},{1,38},{2,70},{3,102},{4,134},{5,166},{6,198},{7,230},{8,7},... | collective-permute-start | bytes 49160 | tf_op jit(solution)/shard_map/ppermute | solution.py:393
  135.3 12.3 %collective-permute-start.12 = (f32[4,1024]{1,0:T(4,128)S(1)}, f32[4,1024]{1,0:T(4,128)S(1)}, u32[]{:S(2)}, u32[]{:S(2)}) collective-permute-start(f32[4,1024]{1,0:T(4,128)S(1)} %copy-done.9), channel_id=1, source_target_pairs={{0,7},{1,39},{2,71},{3,103},{4,135},{5,167},{6,199},{7,231},{8,0},... | collective-permute-start | bytes 49160 | tf_op jit(solution)/shard_map/ppermute | solution.py:393
Sparse Core Ops, SparseCore 0:
  9.9 30.6 all-gather.1

commit v4 on v3

--- a/solution.py
+++ b/solution.py
@@ -22,6 +22,7 @@
 PLANE_AXES = ("x", "c")
 VMEM_LIMIT = 60 * 1024 * 1024
 ROOM = 30 * 1024 * 1024
+TIGHT = 62_300_000
 
 NN = (((1,), (0,)), ((), ()))
 NT = (((1,), (1,)), ((), ()))
@@ -235,7 +236,7 @@
 
 
 def middle_body(
-    low_ref, who_ref, mixt, gd, stats, halo, recv, start, qt, cot, sent, dmix, dqt, back, own, far1, far2, far3, kt_ref, dk_ref, dv_ref
+    low_ref, who_ref, mixt, gd, stats, halo, recv, start, qt, cot, sent, dmix, dqt, back, own, far1, far2, far3, kt_ref, dk_ref, dv_ref, all_ref
 ):
     finish(mixt.get(), gd.get(), stats.get(), sent.ref, dmix.ref)
     sent.send((), (slice(None), slice(0, 256)))
@@ -254,29 +255,27 @@
         back.ref[2 * j : 2 * j + 2, 0:128, :] = dk_ref[j].astype(BF16).reshape(2, 128, 128)
         back.ref[2 * j : 2 * j + 2, 128:256, :] = dv_ref[j].astype(BF16).reshape(2, 128, 128)
     back.send()
-    row = lax.broadcasted_iota(jnp.int32, (128, 128), 0)
-    feature = lax.broadcasted_iota(jnp.int32, (128, 128), 1)
-    replica = jnp.bitwise_and(row // 32 + who_ref[0], 3)
-    plane = jnp.bitwise_and(row // 4 + who_ref[1], 7)
-    pick = jnp.where(feature == 32 * replica + 4 * plane + jnp.bitwise_and(row, 3), 1.0, 0.0).astype(BF16)
     cot_ref = cot.get()
-    total = jnp.zeros((128, 1024), F32)
-    for b in range(HEADS):
-        total = total + dot(dot(pick, sent.ref[b, 0:128, :]).astype(BF16), cot_ref[b])
-    own.ref[...] = total[0:32]
-    own.send()
-    for n, far in enumerate((far1, far2, far3)):
-        far.ref[...] = total[32 * (n + 1) : 32 * (n + 2)].astype(BF16)
-        far.send()
-
-
-def replica_sum_body(own, got1, got2, got3, *outs):
+    total = dot(sent.ref[0, 0:128, :], cot_ref[0])
+    for b in range(1, HEADS):
+        total = total + dot(sent.ref[b, 0:128, :], cot_ref[b])
+    all_ref[...] = total
+    for n, made in enumerate((own, far1, far2, far3)):
+        block = jnp.bitwise_and(who_ref[0] + n, 3)
+        made.ref[...] = all_ref[pl.ds(pl.multiple_of(32 * block, 32), 32), :].astype(made.ref.dtype)
+        made.send()
+
+
+def replica_sum_body(own, got1, got2, got3, out, total_ref, moved_ref):
     total = own.get()[...]
     for got in (got1, got2, got3):
         total = total + got.get()[...].astype(F32)
-    for s, out in enumerate(outs):
-        out.ref[...] = total[4 * s : 4 * s + 4]
-        out.send()
+    total_ref[...] = total
+    for j in range(8):
+        for b in range(8):
+            moved_ref[j, 4 * b : 4 * b + 4, :] = total_ref[4 * j : 4 * j + 4, 128 * b : 128 * b + 128]
+    out.ref[...] = moved_ref[...].astype(BF16)
+    out.send()
 
 
 def bwd_own_body(low_ref, recv, start, qt, dmix, part, out, dk, dv, kt_ref):
@@ -298,22 +297,25 @@
         dv.send((i,))
 
 
-def add_body(dk, dv, back, out):
-    next_ref, dk_ref, dv_ref = back.get(), dk.get(), dv.get()
+def add_body(dk, dv, back, share, out):
+    share_ref, next_ref, dk_ref, dv_ref = share.get(), back.get(), dk.get(), dv.get()
     for b in range(HEADS):
         rows = slice((b % 2) * TOK, (b % 2 + 1) * TOK)
         out.ref[b, 0:128, :] = (dk_ref[b // 2, rows, :] + next_ref[b, 0:128, :].astype(F32)).astype(BF16)
         out.ref[b, 128:256, :] = (dv_ref[b // 2, rows, :] + next_ref[b, 128:256, :].astype(F32)).astype(BF16)
-    out.send((), (slice(None), slice(384, 640)))
-
-
-def final_body(recv, w, p0, p1, p2, p3, p4, p5, p6, p7, out, dq, dk, dv, gg, wg):
-    total = p0.get()[...]
-    for piece in (p1, p2, p3, p4, p5, p6, p7):
-        total = total + piece.get()[...]
-    wg.ref[...] = total
+    out.ref[:, 256:288, :] = share_ref[...]
+    out.send((), (slice(None), slice(384, 672)))
+
+
+def final_body(recv, w, out, dq, dk, dv, gg, wg):
+    recv_ref = recv.get()
+    share = recv_ref[0, 640:672, :].astype(F32)
+    for n in range(1, HEADS):
+        share = share + recv_ref[n, 640:672, :].astype(F32)
+    for b in range(8):
+        wg.ref[:, 128 * b : 128 * b + 128] = share[4 * b : 4 * b + 4, :]
     wg.send()
-    recv_ref, w_ref = recv.get(), w.get()
+    w_ref = w.get()
     for n, made in enumerate((dq, dk, dv)):
         for h in range(HEADS):
             made.ref[:, h * TOK : (h + 1) * TOK] = recv_ref[h, 256 + 128 * n : 384 + 128 * n, :]
@@ -362,7 +364,7 @@
     halo = lax.ppermute(pair, "z", [(i, i + 1) for i in range(planes - 1)])
     gd_recv = plane_exchange(gd)
     part, qt = call(fwd_own_body, "shh", [head, head16], 1 << 29, [vt])(low, recv, start)
-    mixt, stats = call(fwd_halo_body, "shhhhh", [head, shape((8, 32, 128), F32)], 1 << 28, [vt], kept={1: (1, 32, 128)})(
+    mixt, stats = call(fwd_halo_body, "shhhhh", [head, shape((8, 32, 128), F32)], 1 << 28, [vt], TIGHT, kept={1: (1, 32, 128)})(
         low, halo, start, qt, part, gd_recv
     )
     stats = plane_exchange(stats)
@@ -371,28 +373,26 @@
     far = shape((32, 1024), BF16)
     sent, dmix, dqt, back, own, *fars = call(
         middle_body, "sshhhhhhhh",
-        [shape((8, 640, 128), BF16), head16, head, shape((8, 256, 128), BF16), shape((32, 1024), F32), far, far, far],
-        1 << 29, [vt, acc, acc], kept={0: (8, 256, 128)}, held=only_q,
+        [shape((8, 672, 128), BF16), head16, head, shape((8, 256, 128), BF16), shape((32, 1024), F32), far, far, far],
+        1 << 29, [vt, acc, acc, pltpu.VMEM((128, 1024), F32)], kept={0: (8, 256, 128)}, held=only_q,
     )(low, who, mixt, gd_recv, stats, halo, recv, start, qt, cot_plane)
     back = lax.ppermute(back, "z", [(i, i - 1) for i in range(1, planes)])
     fars = [lax.ppermute(x, "dp", [(i, (i + n + 1) % dp) for i in range(dp)]) for n, x in enumerate(fars)]
-    pieces = call(replica_sum_body, "hhhh", [share] * 8, 1 << 16)(own, *fars)
+    moved = shape((8, 32, 128), BF16)
+    (moved,) = call(replica_sum_body, "hhhh", [moved], 1 << 16, [pltpu.VMEM((32, 1024), F32), pltpu.VMEM((8, 32, 128), F32)])(own, *fars)
+    route = []
+    for d in range(dp):
+        for z in range(planes):
+            for r in range(8):
+                route.append(((d * planes + z) * 8 + r, (r // 2 * planes + (r % 2) * 4 + d) * 8 + z))
+    moved = lax.ppermute(moved, ("dp", "z", "x", "c"), route)
+
     sent, dk, dv = call(
-        bwd_own_body, "shhhhha", [shape((8, 640, 128), BF16), grad, grad], 1 << 30, [vt], kept={0: (8, 128, 128)}
+        bwd_own_body, "shhhhha", [shape((8, 672, 128), BF16), grad, grad], 1 << 30, [vt], kept={0: (8, 128, 128)}
     )(low, recv, start, qt, dmix, dqt, sent)
-    (sent,) = call(add_body, "hhha", [shape((8, 640, 128), BF16)], 1 << 20, kept={0: (8, 256, 128)})(dk, dv, back, sent)
-    sent, pieces = lax.optimization_barrier((sent, pieces))
-    landed = []
-    for s, piece in enumerate(pieces):
-        route = []
-        for d in range(dp):
-            for z in range(planes):
-                for r in range(8):
-                    owner = (r // 2 * planes + (r % 2) * 4 + d) * 8 + (z + s) % 8
-                    route.append(((d * planes + z) * 8 + r, owner))
-        landed.append(lax.ppermute(piece, ("dp", "z", "x", "c"), route))
+    (sent,) = call(add_body, "hhhha", [shape((8, 672, 128), BF16)], 1 << 20, (), TIGHT, kept={0: (8, 288, 128)})(dk, dv, back, moved, sent)
     got = plane_exchange(sent)
-    out, dq, dk, dv, gg, weight_grad = call(final_body, "h" * 10, [rows] * 5 + [share], 1 << 28, (), ROOM)(got, w_out, *landed)
+    out, dq, dk, dv, gg, weight_grad = call(final_body, "hh", [rows] * 5 + [share], 1 << 28, (), ROOM)(got, w_out)
     return out[None], dq[None], dk[None], dv[None], gg[None], weight_grad
 
 

time: 158 us -> 136 us (0.86)
  the two profiles are of different devices: /device:TPU:19 before, /device:TPU:8 now
where the time goes in v4:
time: 136 us; the launch traced here: 135 us
  blocking collectives  40.9 us (30%)
  Pallas kernels  32.4 us (24%)
  starting transfers between devices  27.4 us (20%)
  waiting for transfers between devices  15.5 us (11%)
  between operations  14.2 us (10%)
  local copies, waits for them, and re-layouts  2.57 us (2%)
  other arithmetic  2.13 us (2%)
    all_to_all x2, blocking collectives, plane_exchange(): return lax.all_to_all(blocks, PLANE_AXES, 0, 0, tiled=True)  40.9 us
    pallas_call x9, Pallas kernels, build(): pl.pallas_call(whole, out_shape=outs, in_specs=[pl.BlockSpec(memory_space...  32.4 us
    all_to_all x2, waiting for transfers between devices, plane_exchange(): return lax.all_to_all(blocks, PLANE_AXES, 0, 0, tiled=True)  12 us
    ppermute x1, starting transfers between devices, shards(): moved = lax.ppermute(moved, ('dp', 'z', 'x', 'c'), route)  9.35 us
    all_to_all x2, starting transfers between devices, plane_exchange(): return lax.all_to_all(blocks, PLANE_AXES, 0, 0, tiled=True)  7.82 us
    ppermute x3, starting transfers between devices, shards(): lax.ppermute(x, 'dp', [(i, (i + n + 1) % dp) for i in range(dp)])  5.01 us
    ppermute x1, starting transfers between devices, shards(): halo = lax.ppermute(pair, 'z', [(i, i + 1) for i in range(planes - 1)])  3.85 us
    ppermute x3, waiting for transfers between devices, shards(): lax.ppermute(x, 'dp', [(i, (i + n + 1) % dp) for i in range(dp)])  2.77 us
  transfers between devices with their start and end apart: 9, of which 3 were waited for; matrix products, arithmetic and copies ran while one was open for 2% of the time, Pallas kernels for 17%

profile of v4, /device:TPU:8, one launch (start us, length us, event | category | flops | bytes accessed | tf_op | source)
XLA Modules:
  0.0 135.1 jit_solution(11895272161185485756)
XLA Ops:
  7.2 0.7 all-gather.2.cloned.1.call-update
  7.9 2.1 %shard_map.118 = bf16[8,384,128]{2,1,0:T(8,128)(2,1)} custom-call(bf16[128,1024]{1,0:T(8,128)(2,1)} %bitcast.18, bf16[128,1024]{1,0:T(8,128)(2,1)} %bitcast.19, bf16[128,1024]{1,0:T(8,128)(2,1)} %bitcast.20), custom_call_target="tpu_custom_call" | custom-call | flops 65536 | bytes 1572864 | tf_op jit(solution)/shard_map/pallas_call | solution.py:93
  10.0 4.3 %all-to-all-start = ((bf16[8,384,128]{2,1,0:T(8,128)(2,1)}), bf16[8,384,128]{2,1,0:T(8,128)(2,1)S(1)}, u32[]{:S(2)}, u32[]{:S(2)}) async-start(bf16[8,384,128]{2,1,0:T(8,128)(2,1)} %shard_map.118), calls=%async_computation | async-start | bytes 1572864 | tf_op jit(solution)/shard_map/all_to_all | solution.py:334
  14.3 0.2 convert_reduce_fusion
  14.8 3.4 %shard_map.119 = bf16[8,256,128]{2,1,0:T(8,128)(2,1)} custom-call(bf16[128,1024]{1,0:T(8,128)(2,1)} %bitcast.16, bf16[128,1024]{1,0:T(8,128)(2,1)} %bitcast.17, bf16[1024,1024]{1,0:T(8,128)(2,1)} %refs_1_.1), custom_call_target="tpu_custom_call" | custom-call | flops 268435456 | bytes 3145728 | tf_op jit(solution)/shard_map/pallas_call | solution.py:93
  18.2 0.7 pad_add_fusion.refs_1_
  18.9 0.6 and_select_fusion.refs_0_
  19.4 0.6 fusion.refs_2_.refs_7_
  20.0 7.4 %all-to-all-done.refs_1_.refs_6_ = bf16[8,384,128]{2,1,0:T(8,128)(2,1)S(1)} async-done(((bf16[8,384,128]{2,1,0:T(8,128)(2,1)}), bf16[8,384,128]{2,1,0:T(8,128)(2,1)S(1)}, u32[]{:S(2)}, u32[]{:S(2)}) %all-to-all-start) | async-done | bytes 786464 | tf_op jit(solution)/shard_map/all_to_all | solution.py:334
  27.5 3.9 %collective-permute-start = (bf16[8,256,128]{2,1,0:T(8,128)(2,1)S(1)}, bf16[8,256,128]{2,1,0:T(8,128)(2,1)S(1)}, u32[]{:S(2)}, u32[]{:S(2)}) collective-permute-start(bf16[8,256,128]{2,1,0:T(8,128)(2,1)S(1)} %slice.8), channel_id=1, source_target_pairs={{0,8},{8,16},{16,24},{24,32},{32,40},{40,48},{48,56},{1,9},{9,17},... | collective-permute-start | bytes 1572872 | tf_op jit(solution)/shard_map/ppermute | solution.py:364
  31.4 3.5 %all-to-all-start.1 = ((bf16[8,256,128]{2,1,0:T(8,128)(2,1)}), bf16[8,256,128]{2,1,0:T(8,128)(2,1)S(1)}, u32[]{:S(2)}, u32[]{:S(2)}) async-start(bf16[8,256,128]{2,1,0:T(8,128)(2,1)} %shard_map.119), calls=%async_computation.1 | async-start | bytes 1048576 | tf_op jit(solution)/shard_map/all_to_all | solution.py:334
  34.9 5.7 %shard_map.120 = (f32[4,128,256]{2,1,0:T(8,128)}, bf16[4,128,256]{2,1,0:T(8,128)(2,1)}) custom-call(s32[4]{0:T(128)} %and_select_fusion.refs_0_, bf16[8,384,128]{2,1,0:T(8,128)(2,1)} %copy-done.1, s32[8,128]{1,0:T(8,128)} %fusion.refs_2_.refs_7_), custom_call_target="tpu_custom_call" | custom-call | flops 536870912 | bytes 1576976 | tf_op jit(solution)/shard_map/pallas_call | solution.py:93
  40.6 4.6 %all-to-all-done.1.refs_5_.refs_3_ = bf16[8,256,128]{2,1,0:T(8,128)(2,1)S(1)} async-done(((bf16[8,256,128]{2,1,0:T(8,128)(2,1)}), bf16[8,256,128]{2,1,0:T(8,128)(2,1)S(1)}, u32[]{:S(2)}, u32[]{:S(2)}) %all-to-all-start.1) | async-done | bytes 524320 | tf_op jit(solution)/shard_map/all_to_all | solution.py:334
  45.2 0.8 copy-done.2
  46.0 0.2 copy-done.3
  46.2 3.2 %shard_map.121 = (f32[4,128,256]{2,1,0:T(8,128)}, f32[8,32,128]{2,1,0:T(8,128)}) custom-call(s32[4]{0:T(128)} %and_select_fusion.refs_0_, bf16[8,256,128]{2,1,0:T(8,128)(2,1)} %copy-done.3, s32[8,128]{1,0:T(8,128)} %fusion.refs_2_.refs_7_, bf16[4,128,256]{2,1,0:T(8,128)(2,1)} %get-tuple-element.34.refs_3_.refs_8_, f32[4,128,256]{2,1,0:T(8,128)} %get-tuple-element.37.refs_4_, ...), custom_call_target="tpu_custom_call" | custom-call | flops 268435456 | bytes 2494480 | tf_op jit(solution)/shard_map/pallas_call | solution.py:93
  49.4 10.1 %all_to_all.20.refs_4_ = f32[8,32,128]{2,1,0:T(8,128)} all-to-all(f32[8,32,128]{2,1,0:T(8,128)} %get-tuple-element.40), channel_id=1, replica_groups=mesh['dp'=4,'z'=8,'x'=4,'c'=2] {'x','c'}, dimensions={0} | all-to-all | bytes 262144 | tf_op jit(solution)/shard_map/all_to_all | solution.py:334
  59.5 4.6 %shard_map.122 = (bf16[8,672,128]{2,1,0:T(8,128)(2,1)}, bf16[4,128,256]{2,1,0:T(8,128)(2,1)}, f32[4,128,256]{2,1,0:T(8,128)}, bf16[8,256,128]{2,1,0:T(8,128)(2,1...) custom-call(s32[4]{0:T(128)} %and_select_fusion.refs_0_, ...), custom_call_target="tpu_custom_call" | custom-call | flops 536870912 | bytes 7868440 | tf_op jit(solution)/shard_map/pallas_call | solution.py:93
  64.2 1.3 collective-permute-start.1
  65.5 1.7 %collective-permute-start.2 = (bf16[32,1024]{1,0:T(8,128)(2,1)}, bf16[32,1024]{1,0:T(8,128)(2,1)S(1)}, u32[]{:S(2)}, u32[]{:S(2)}) collective-permute-start(bf16[32,1024]{1,0:T(8,128)(2,1)} %get-tuple-element.48), channel_id=1, source_target_pairs={{0,64},{64,128},{128,192},{192,0},{1,65},{65,129},{129,193},{193,1... | collective-permute-start | bytes 196616 | tf_op jit(solution)/shard_map/ppermute | solution.py:380
  67.1 0.9 collective-permute-start.3
  68.1 2.4 %collective-permute-start.4 = (bf16[32,1024]{1,0:T(8,128)(2,1)}, bf16[32,1024]{1,0:T(8,128)(2,1)S(1)}, u32[]{:S(2)}, u32[]{:S(2)}) collective-permute-start(bf16[32,1024]{1,0:T(8,128)(2,1)} %get-tuple-element.50), channel_id=1, source_target_pairs={{0,192},{64,0},{128,64},{192,128},{1,193},{65,1},{129,65},{193,129... | collective-permute-start | bytes 196616 | tf_op jit(solution)/shard_map/ppermute | solution.py:380
  70.5 2.7 %collective-permute-done.3.refs_2_ = bf16[32,1024]{1,0:T(8,128)(2,1)S(1)} collective-permute-done((bf16[32,1024]{1,0:T(8,128)(2,1)}, bf16[32,1024]{1,0:T(8,128)(2,1)S(1)}, u32[]{:S(2)}, u32[]{:S(2)}) %collective-permute-start.3) | collective-permute-done | bytes 65568 | tf_op jit(solution)/shard_map/ppermute | solution.py:380
  73.3 0.6 copy-done.7
  73.9 1.8 %shard_map.124 = bf16[8,32,128]{2,1,0:T(8,128)(2,1)} custom-call(f32[32,1024]{1,0:T(8,128)} %get-tuple-element.47.refs_0_, bf16[32,1024]{1,0:T(8,128)(2,1)} %copy-done.6, bf16[32,1024]{1,0:T(8,128)(2,1)} %copy-done.7, bf16[32,1024]{1,0:T(8,128)(2,1)} %copy-done.8), custom_call_target="tpu_custom_call" | custom-call | flops 65536 | bytes 393216 | tf_op jit(solution)/shard_map/pallas_call | solution.py:93
  75.7 9.4 %collective-permute-start.5 = (bf16[8,32,128]{2,1,0:T(8,128)(2,1)}, bf16[8,32,128]{2,1,0:T(8,128)(2,1)S(1)}, u32[]{:S(2)}, u32[]{:S(2)}) collective-permute-start(bf16[8,32,128]{2,1,0:T(8,128)(2,1)} %shard_map.124), channel_id=1, source_target_pairs={{0,0},{1,32},{2,64},{3,96},{4,128},{5,160},{6,192},{7,224},{8,1},{... | collective-permute-start | bytes 196616 | tf_op jit(solution)/shard_map/ppermute | solution.py:388
  85.1 6.8 %shard_map.123 = (bf16[8,672,128]{2,1,0:T(8,128)(2,1)}, f32[4,256,128]{2,1,0:T(8,128)}, f32[4,256,128]{2,1,0:T(8,128)}) custom-call(s32[4]{0:T(128)} %and_select_fusion.refs_0_, bf16[8,384,128]{2,1,0:T(8,128)(2,1)} %copy-done.1, s32[8,128]{1,0:T(8,128)} %fusion.refs_2_.refs_7_, ...), custom_call_target="tpu_custom_call", output_to_operand_aliasing={{0}: (6, {})} | custom-call | flops 1073741824 | bytes 5640208 | tf_op jit(solution)/shard_map/pallas_call | solution.py:93
  91.9 0.6 copy-done.5
  92.5 0.2 copy-done.4
  92.7 2.5 %shard_map.125 = bf16[8,672,128]{2,1,0:T(8,128)(2,1)} custom-call(f32[4,256,128]{2,1,0:T(8,128)} %get-tuple-element.44.refs_0_, f32[4,256,128]{2,1,0:T(8,128)} %get-tuple-element.45.refs_1_, bf16[8,256,128]{2,1,0:T(8,128)(2,1)} %copy-done.4, bf16[8,32,128]{2,1,0:T(8,128)(2,1)} %copy-done.5, ...), custom_call_target="tpu_custom_call", output_to_operand_aliasing={{}: (4, {})} | custom-call | flops 1048576 | bytes 4390912 | tf_op jit(solution)/shard_map/pallas_call | solution.py:93
  95.2 30.8 %all_to_all.21.refs_0_ = bf16[8,672,128]{2,1,0:T(8,128)(2,1)S(1)} all-to-all(bf16[8,672,128]{2,1,0:T(8,128)(2,1)} %shard_map.125), channel_id=1, replica_groups=mesh['dp'=4,'z'=8,'x'=4,'c'=2] {'x','c'}, dimensions={0} | all-to-all | bytes 2752512 | tf_op jit(solution)/shard_map/all_to_all | solution.py:334
  126.0 2.3 %shard_map.126 = (bf16[128,1024]{1,0:T(8,128)(2,1)}, bf16[128,1024]{1,0:T(8,128)(2,1)}, bf16[128,1024]{1,0:T(8,128)(2,1)}, bf16[128,1024]{1,0:T(8,128)(2,1)}, bf...) custom-call(bf16[8,672,128]{2,1,0:T(8,128)(2,1)S(1)} %all_to_all.21.refs_0_, bf16[1024,1024]{1,0:T(8,128)(2,1)S(1)} %copy-done), custom_call_target="tpu_custom_call" | custom-call | flops 268435456 | bytes 4800512 | tf_op jit(solution)/shard_map/pallas_call | solution.py:93
  (27 shorter events, 0.4 us)
Async XLA Ops:
  7.2 52.4 %all-gather.2.cloned.1.call-start = ((), (), s32[]{:S(2)}) async-start(), calls=%async_computation.4 | async-start | bytes 2359296 | tf_op jit(solution)/shard_map/all_gather | solution.py:340
  7.9 6.4 %copy-start.9 = (s32[1,8192]{1,0:T(1,128)S(1)}, s32[1,8192]{1,0:T(1,128)}, u32[]{:S(2)}) copy-start(s32[1,8192]{1,0:T(1,128)} %param.12) | copy-start | bytes 98308
  10.0 17.5 %all-to-all-start = ((bf16[8,384,128]{2,1,0:T(8,128)(2,1)}), bf16[8,384,128]{2,1,0:T(8,128)(2,1)S(1)}, u32[]{:S(2)}, u32[]{:S(2)}) async-start(bf16[8,384,128]{2,1,0:T(8,128)(2,1)} %shard_map.118), calls=%async_computation | async-start | bytes 1572864 | tf_op jit(solution)/shard_map/all_to_all | solution.py:334
  27.5 7.4 %copy-start.1 = (bf16[8,384,128]{2,1,0:T(8,128)(2,1)}, bf16[8,384,128]{2,1,0:T(8,128)(2,1)S(1)}, u32[]{:S(2)}) copy-start(bf16[8,384,128]{2,1,0:T(8,128)(2,1)S(1)} %all-to-all-done.refs_1_.refs_6_) | copy-start | bytes 2359300
  27.5 17.6 %collective-permute-start = (bf16[8,256,128]{2,1,0:T(8,128)(2,1)S(1)}, bf16[8,256,128]{2,1,0:T(8,128)(2,1)S(1)}, u32[]{:S(2)}, u32[]{:S(2)}) collective-permute-start(bf16[8,256,128]{2,1,0:T(8,128)(2,1)S(1)} %slice.8), channel_id=1, source_target_pairs={{0,8},{8,16},{16,24},{24,32},{32,40},{40,48},{48,56},{1,9},{9,17},... | collective-permute-start | bytes 1572872 | tf_op jit(solution)/shard_map/ppermute | solution.py:364
  31.4 13.8 %all-to-all-start.1 = ((bf16[8,256,128]{2,1,0:T(8,128)(2,1)}), bf16[8,256,128]{2,1,0:T(8,128)(2,1)S(1)}, u32[]{:S(2)}, u32[]{:S(2)}) async-start(bf16[8,256,128]{2,1,0:T(8,128)(2,1)} %shard_map.119), calls=%async_computation.1 | async-start | bytes 1048576 | tf_op jit(solution)/shard_map/all_to_all | solution.py:334
  45.2 0.8 copy-start.2
  45.2 1.0 copy-start.3
  64.2 27.7 %collective-permute-start.1 = (bf16[8,256,128]{2,1,0:T(8,128)(2,1)}, bf16[8,256,128]{2,1,0:T(8,128)(2,1)S(1)}, u32[]{:S(2)}, u32[]{:S(2)}) collective-permute-start(bf16[8,256,128]{2,1,0:T(8,128)(2,1)} %get-tuple-element.46), channel_id=1, source_target_pairs={{8,0},{16,8},{24,16},{32,24},{40,32},{48,40},{56,48},{9,1},{17,9},... | collective-permute-start | bytes 1572872 | tf_op jit(solution)/shard_map/ppermute | solution.py:379
  65.5 5.0 %collective-permute-start.2 = (bf16[32,1024]{1,0:T(8,128)(2,1)}, bf16[32,1024]{1,0:T(8,128)(2,1)S(1)}, u32[]{:S(2)}, u32[]{:S(2)}) collective-permute-start(bf16[32,1024]{1,0:T(8,128)(2,1)} %get-tuple-element.48), channel_id=1, source_target_pairs={{0,64},{64,128},{128,192},{192,0},{1,65},{65,129},{129,193},{193,1... | collective-permute-start | bytes 196616 | tf_op jit(solution)/shard_map/ppermute | solution.py:380
  67.1 6.1 %collective-permute-start.3 = (bf16[32,1024]{1,0:T(8,128)(2,1)}, bf16[32,1024]{1,0:T(8,128)(2,1)S(1)}, u32[]{:S(2)}, u32[]{:S(2)}) collective-permute-start(bf16[32,1024]{1,0:T(8,128)(2,1)} %get-tuple-element.49), channel_id=1, source_target_pairs={{0,128},{64,192},{128,0},{192,64},{1,129},{65,193},{129,1},{193,65... | collective-permute-start | bytes 196616 | tf_op jit(solution)/shard_map/ppermute | solution.py:380
  68.1 5.2 %collective-permute-start.4 = (bf16[32,1024]{1,0:T(8,128)(2,1)}, bf16[32,1024]{1,0:T(8,128)(2,1)S(1)}, u32[]{:S(2)}, u32[]{:S(2)}) collective-permute-start(bf16[32,1024]{1,0:T(8,128)(2,1)} %get-tuple-element.50), channel_id=1, source_target_pairs={{0,192},{64,0},{128,64},{192,128},{1,193},{65,1},{129,65},{193,129... | collective-permute-start | bytes 196616 | tf_op jit(solution)/shard_map/ppermute | solution.py:380
  70.5 2.8 %copy-start.6 = (bf16[32,1024]{1,0:T(8,128)(2,1)}, bf16[32,1024]{1,0:T(8,128)(2,1)S(1)}, u32[]{:S(2)}) copy-start(bf16[32,1024]{1,0:T(8,128)(2,1)S(1)} %collective-permute-done.2.refs_1_) | copy-start | bytes 196612
  73.2 0.6 copy-start.7
  73.3 0.6 copy-start.8
  75.7 16.2 %collective-permute-start.5 = (bf16[8,32,128]{2,1,0:T(8,128)(2,1)}, bf16[8,32,128]{2,1,0:T(8,128)(2,1)S(1)}, u32[]{:S(2)}, u32[]{:S(2)}) collective-permute-start(bf16[8,32,128]{2,1,0:T(8,128)(2,1)} %shard_map.124), channel_id=1, source_target_pairs={{0,0},{1,32},{2,64},{3,96},{4,128},{5,160},{6,192},{7,224},{8,1},{... | collective-permute-start | bytes 196616 | tf_op jit(solution)/shard_map/ppermute | solution.py:388
  91.9 0.6 copy-start.5
  91.9 0.8 copy-start.4
  95.2 30.8 %copy-start = (bf16[1024,1024]{1,0:T(8,128)(2,1)S(1)}, bf16[1024,1024]{1,0:T(8,128)(2,1)}, u32[]{:S(2)}) copy-start(bf16[1024,1024]{1,0:T(8,128)(2,1)} %refs_1_.1) | copy-start | bytes 6291460
Sparse Core Ops, SparseCore 0:
  9.9 30.5 all-gather.1

commit v5 on v4

--- a/solution.py
+++ b/solution.py
@@ -239,7 +239,7 @@
     low_ref, who_ref, mixt, gd, stats, halo, recv, start, qt, cot, sent, dmix, dqt, back, own, far1, far2, far3, kt_ref, dk_ref, dv_ref, all_ref
 ):
     finish(mixt.get(), gd.get(), stats.get(), sent.ref, dmix.ref)
-    sent.send((), (slice(None), slice(0, 256)))
+    sent.send()
     dmix.send()
     halo_ref, recv_ref, start_ref, qt_ref = halo.get(), recv.get(), start.get(), qt.get()
     flip_tiles(halo_ref, slice(0, 128), kt_ref)
@@ -292,42 +292,50 @@
         )
         out.ref[2 * i : 2 * i + 2] = dqt.T.astype(BF16).reshape(2, 128, 128)
         blocks = slice(2 * i, 2 * i + 2)
-        out.send((blocks,), (blocks, slice(256, 384)))
+        out.send((blocks,), (blocks, slice(0, 128)))
         dk.send((i,))
         dv.send((i,))
 
 
-def add_body(dk, dv, back, share, out):
-    share_ref, next_ref, dk_ref, dv_ref = share.get(), back.get(), dk.get(), dv.get()
+def add_body(dk, dv, back, out):
+    next_ref, dk_ref, dv_ref = back.get(), dk.get(), dv.get()
     for b in range(HEADS):
         rows = slice((b % 2) * TOK, (b % 2 + 1) * TOK)
         out.ref[b, 0:128, :] = (dk_ref[b // 2, rows, :] + next_ref[b, 0:128, :].astype(F32)).astype(BF16)
         out.ref[b, 128:256, :] = (dv_ref[b // 2, rows, :] + next_ref[b, 128:256, :].astype(F32)).astype(BF16)
-    out.ref[:, 256:288, :] = share_ref[...]
-    out.send((), (slice(None), slice(384, 672)))
-
-
-def final_body(recv, w, out, dq, dk, dv, gg, wg):
+    out.send((), (slice(None), slice(128, 384)))
+
+
+def share_body(share, out):
+    out.ref[...] = share.get()[...]
+    out.send((), (slice(None), slice(384, 416)))
+
+
+def gate_body(recv, w, out, gg):
     recv_ref = recv.get()
-    share = recv_ref[0, 640:672, :].astype(F32)
-    for n in range(1, HEADS):
-        share = share + recv_ref[n, 640:672, :].astype(F32)
-    for b in range(8):
-        wg.ref[:, 128 * b : 128 * b + 128] = share[4 * b : 4 * b + 4, :]
-    wg.send()
-    w_ref = w.get()
-    for n, made in enumerate((dq, dk, dv)):
-        for h in range(HEADS):
-            made.ref[:, h * TOK : (h + 1) * TOK] = recv_ref[h, 256 + 128 * n : 384 + 128 * n, :]
-        made.send()
     for h in range(HEADS):
         gg.ref[:, h * TOK : (h + 1) * TOK] = flip(recv_ref[h, 128:256, :])
     gg.send()
+    w_ref = w.get()
     total = dot(flip(recv_ref[0, 0:128, :]), w_ref[0:TOK, :])
     for h in range(1, HEADS):
         total = total + dot(flip(recv_ref[h, 0:128, :]), w_ref[h * TOK : (h + 1) * TOK, :])
     out.ref[...] = total.astype(BF16)
     out.send()
+
+
+def final_body(recv, dq, dk, dv, wg):
+    recv_ref = recv.get()
+    for n, made in enumerate((dq, dk, dv)):
+        for h in range(HEADS):
+            made.ref[:, h * TOK : (h + 1) * TOK] = recv_ref[h, 128 * n : 128 * n + 128, :]
+        made.send()
+    share = recv_ref[0, 384:416, :].astype(F32)
+    for n in range(1, HEADS):
+        share = share + recv_ref[n, 384:416, :].astype(F32)
+    for b in range(8):
+        wg.ref[:, 128 * b : 128 * b + 128] = share[4 * b : 4 * b + 4, :]
+    wg.send()
 
 
 def plane_exchange(blocks):
@@ -371,10 +379,10 @@
 
     only_q = {6: ((slice(None), slice(0, 128)), (8, 128, 128))}
     far = shape((32, 1024), BF16)
-    sent, dmix, dqt, back, own, *fars = call(
+    gate_pack, dmix, dqt, back, own, *fars = call(
         middle_body, "sshhhhhhhh",
-        [shape((8, 672, 128), BF16), head16, head, shape((8, 256, 128), BF16), shape((32, 1024), F32), far, far, far],
-        1 << 29, [vt, acc, acc, pltpu.VMEM((128, 1024), F32)], kept={0: (8, 256, 128)}, held=only_q,
+        [shape((8, 256, 128), BF16), head16, head, shape((8, 256, 128), BF16), shape((32, 1024), F32), far, far, far],
+        1 << 29, [vt, acc, acc, pltpu.VMEM((128, 1024), F32)], held=only_q,
     )(low, who, mixt, gd_recv, stats, halo, recv, start, qt, cot_plane)
     back = lax.ppermute(back, "z", [(i, i - 1) for i in range(1, planes)])
     fars = [lax.ppermute(x, "dp", [(i, (i + n + 1) % dp) for i in range(dp)]) for n, x in enumerate(fars)]
@@ -385,14 +393,20 @@
         for z in range(planes):
             for r in range(8):
                 route.append(((d * planes + z) * 8 + r, (r // 2 * planes + (r % 2) * 4 + d) * 8 + z))
+    got_gate = plane_exchange(gate_pack)
+
+    sent, dk, dv = call(
+        bwd_own_body, "shhhhh", [shape((8, 416, 128), BF16), grad, grad], 1 << 30, [vt], kept={0: (8, 128, 128)}
+    )(low, recv, start, qt, dmix, dqt)
+    moved, back, dk = lax.optimization_barrier((moved, back, dk))
     moved = lax.ppermute(moved, ("dp", "z", "x", "c"), route)
-
-    sent, dk, dv = call(
-        bwd_own_body, "shhhhha", [shape((8, 672, 128), BF16), grad, grad], 1 << 30, [vt], kept={0: (8, 128, 128)}
-    )(low, recv, start, qt, dmix, dqt, sent)
-    (sent,) = call(add_body, "hhhha", [shape((8, 672, 128), BF16)], 1 << 20, (), TIGHT, kept={0: (8, 288, 128)})(dk, dv, back, moved, sent)
+    sent, got_gate = lax.optimization_barrier((sent, got_gate))
+    whole = [shape((8, 416, 128), BF16)]
+    (sent,) = call(add_body, "hhha", whole, 1 << 20, (), TIGHT, kept={0: (8, 256, 128)})(dk, dv, back, sent)
+    (sent,) = call(share_body, "ha", whole, 1 << 10, kept={0: (8, 32, 128)})(moved, sent)
     got = plane_exchange(sent)
-    out, dq, dk, dv, gg, weight_grad = call(final_body, "hh", [rows] * 5 + [share], 1 << 28, (), ROOM)(got, w_out)
+    out, gg = call(gate_body, "hh", [rows, rows], 1 << 28)(got_gate, w_out)
+    dq, dk, dv, weight_grad = call(final_body, "h", [rows] * 3 + [share], 1 << 20, (), ROOM)(got)
     return out[None], dq[None], dk[None], dv[None], gg[None], weight_grad
 
 

time: 136 us -> 134 us (0.985)
  the two profiles are of different devices: /device:TPU:8 before, /device:TPU:104 now
where the time goes in v5:
time: 134 us
  Pallas kernels  40.3 us (30%)
  starting transfers between devices  34.1 us (25%)
  waiting for transfers between devices  30.3 us (23%)
  between operations  14.3 us (11%)
  blocking collectives  10.1 us (8%)
  local copies, waits for them, and re-layouts  2.41 us (2%)
  other arithmetic  2.11 us (2%)
    pallas_call x11, Pallas kernels, build(): pl.pallas_call(whole, out_shape=outs, in_specs=[pl.BlockSpec(memory_space...  40.3 us
    all_to_all x4, waiting for transfers between devices, plane_exchange(): return lax.all_to_all(blocks, PLANE_AXES, 0, 0, tiled=True)  22.1 us
    all_to_all x4, starting transfers between devices, plane_exchange(): return lax.all_to_all(blocks, PLANE_AXES, 0, 0, tiled=True)  18.4 us
    all_to_all x1, blocking collectives, plane_exchange(): return lax.all_to_all(blocks, PLANE_AXES, 0, 0, tiled=True)  10.1 us
    ppermute x1, waiting for transfers between devices, shards(): moved = lax.ppermute(moved, ('dp', 'z', 'x', 'c'), route)  7.47 us
    ppermute x3, starting transfers between devices, shards(): lax.ppermute(x, 'dp', [(i, (i + n + 1) % dp) for i in range(dp)])  6.77 us
    ppermute x1, starting transfers between devices, shards(): halo = lax.ppermute(pair, 'z', [(i, i + 1) for i in range(planes - 1)])  5.05 us
  transfers between devices with their start and end apart: 11, of which 4 were waited for; matrix products, arithmetic and copies ran while one was open for 2% of the time, Pallas kernels for 24%

profile of v5, /device:TPU:104, one launch (start us, length us, event | category | flops | bytes accessed | tf_op | source)
XLA Modules:
  0.0 133.6 jit_solution(9281714150409669427)
XLA Ops:
  7.2 0.7 all-gather.2.cloned.1.call-update
  7.9 2.0 %shard_map.118 = bf16[8,384,128]{2,1,0:T(8,128)(2,1)} custom-call(bf16[128,1024]{1,0:T(8,128)(2,1)} %bitcast.18, bf16[128,1024]{1,0:T(8,128)(2,1)} %bitcast.19, bf16[128,1024]{1,0:T(8,128)(2,1)} %bitcast.20), custom_call_target="tpu_custom_call" | custom-call | flops 65536 | bytes 1572864 | tf_op jit(solution)/shard_map/pallas_call | solution.py:93
  10.0 4.3 %all-to-all-start = ((bf16[8,384,128]{2,1,0:T(8,128)(2,1)}), bf16[8,384,128]{2,1,0:T(8,128)(2,1)S(1)}, u32[]{:S(2)}, u32[]{:S(2)}) async-start(bf16[8,384,128]{2,1,0:T(8,128)(2,1)} %shard_map.118), calls=%async_computation | async-start | bytes 1572864 | tf_op jit(solution)/shard_map/all_to_all | solution.py:342
  14.7 3.5 %shard_map.119 = bf16[8,256,128]{2,1,0:T(8,128)(2,1)} custom-call(bf16[128,1024]{1,0:T(8,128)(2,1)} %bitcast.16, bf16[128,1024]{1,0:T(8,128)(2,1)} %bitcast.17, bf16[1024,1024]{1,0:T(8,128)(2,1)} %refs_1_.1), custom_call_target="tpu_custom_call" | custom-call | flops 268435456 | bytes 3145728 | tf_op jit(solution)/shard_map/pallas_call | solution.py:93
  18.2 0.6 pad_add_fusion.refs_1_
  18.8 0.6 and_select_fusion.refs_0_
  19.4 0.6 fusion.refs_2_.refs_7_
  20.0 7.4 %all-to-all-done.refs_1_.refs_6_ = bf16[8,384,128]{2,1,0:T(8,128)(2,1)S(1)} async-done(((bf16[8,384,128]{2,1,0:T(8,128)(2,1)}), bf16[8,384,128]{2,1,0:T(8,128)(2,1)S(1)}, u32[]{:S(2)}, u32[]{:S(2)}) %all-to-all-start) | async-done | bytes 786464 | tf_op jit(solution)/shard_map/all_to_all | solution.py:342
  27.5 5.1 %collective-permute-start = (bf16[8,256,128]{2,1,0:T(8,128)(2,1)S(1)}, bf16[8,256,128]{2,1,0:T(8,128)(2,1)S(1)}, u32[]{:S(2)}, u32[]{:S(2)}) collective-permute-start(bf16[8,256,128]{2,1,0:T(8,128)(2,1)S(1)} %slice.8), channel_id=1, source_target_pairs={{0,8},{8,16},{16,24},{24,32},{32,40},{40,48},{48,56},{1,9},{9,17},... | collective-permute-start | bytes 1572872 | tf_op jit(solution)/shard_map/ppermute | solution.py:372
  32.5 3.5 %all-to-all-start.1 = ((bf16[8,256,128]{2,1,0:T(8,128)(2,1)}), bf16[8,256,128]{2,1,0:T(8,128)(2,1)S(1)}, u32[]{:S(2)}, u32[]{:S(2)}) async-start(bf16[8,256,128]{2,1,0:T(8,128)(2,1)} %shard_map.119), calls=%async_computation.1 | async-start | bytes 1048576 | tf_op jit(solution)/shard_map/all_to_all | solution.py:342
  36.1 6.0 %shard_map.120 = (f32[4,128,256]{2,1,0:T(8,128)}, bf16[4,128,256]{2,1,0:T(8,128)(2,1)}) custom-call(s32[4]{0:T(128)} %and_select_fusion.refs_0_, bf16[8,384,128]{2,1,0:T(8,128)(2,1)} %copy-done, s32[8,128]{1,0:T(8,128)} %fusion.refs_2_.refs_7_), custom_call_target="tpu_custom_call" | custom-call | flops 536870912 | bytes 1576976 | tf_op jit(solution)/shard_map/pallas_call | solution.py:93
  42.1 4.2 %all-to-all-done.1.refs_5_.refs_3_ = bf16[8,256,128]{2,1,0:T(8,128)(2,1)S(1)} async-done(((bf16[8,256,128]{2,1,0:T(8,128)(2,1)}), bf16[8,256,128]{2,1,0:T(8,128)(2,1)S(1)}, u32[]{:S(2)}, u32[]{:S(2)}) %all-to-all-start.1) | async-done | bytes 524320 | tf_op jit(solution)/shard_map/all_to_all | solution.py:342
  46.3 0.8 copy-done.1
  47.3 4.8 %shard_map.121 = (f32[4,128,256]{2,1,0:T(8,128)}, f32[8,32,128]{2,1,0:T(8,128)}) custom-call(s32[4]{0:T(128)} %and_select_fusion.refs_0_, bf16[8,256,128]{2,1,0:T(8,128)(2,1)} %copy-done.3, s32[8,128]{1,0:T(8,128)} %fusion.refs_2_.refs_7_, bf16[4,128,256]{2,1,0:T(8,128)(2,1)} %get-tuple-element.39.refs_3_.refs_8_, f32[4,128,256]{2,1,0:T(8,128)} %get-tuple-element.42.refs_4_, ...), custom_call_target="tpu_custom_call" | custom-call | flops 268435456 | bytes 2494480 | tf_op jit(solution)/shard_map/pallas_call | solution.py:93
  52.2 10.1 %all_to_all.25.refs_4_ = f32[8,32,128]{2,1,0:T(8,128)} all-to-all(f32[8,32,128]{2,1,0:T(8,128)} %get-tuple-element.45), channel_id=1, replica_groups=mesh['dp'=4,'z'=8,'x'=4,'c'=2] {'x','c'}, dimensions={0} | all-to-all | bytes 262144 | tf_op jit(solution)/shard_map/all_to_all | solution.py:342
  62.3 6.0 %shard_map.122 = (bf16[8,256,128]{2,1,0:T(8,128)(2,1)}, bf16[4,128,256]{2,1,0:T(8,128)(2,1)}, f32[4,128,256]{2,1,0:T(8,128)}, bf16[8,256,128]{2,1,0:T(8,128)(2,1...) custom-call(s32[4]{0:T(128)} %and_select_fusion.refs_0_, ...), custom_call_target="tpu_custom_call" | custom-call | flops 536870912 | bytes 7016472 | tf_op jit(solution)/shard_map/pallas_call | solution.py:93
  68.3 1.9 %collective-permute-start.4 = (bf16[8,256,128]{2,1,0:T(8,128)(2,1)}, bf16[8,256,128]{2,1,0:T(8,128)(2,1)S(1)}, u32[]{:S(2)}, u32[]{:S(2)}) collective-permute-start(bf16[8,256,128]{2,1,0:T(8,128)(2,1)} %get-tuple-element.56), channel_id=1, source_target_pairs={{8,0},{16,8},{24,16},{32,24},{40,32},{48,40},{56,48},{9,1},{17,9},... | collective-permute-start | bytes 1572872 | tf_op jit(solution)/shard_map/ppermute | solution.py:387
  70.2 3.5 %all-to-all-start.3 = ((bf16[8,256,128]{2,1,0:T(8,128)(2,1)}), bf16[8,256,128]{2,1,0:T(8,128)(2,1)S(1)}, u32[]{:S(2)}, u32[]{:S(2)}) async-start(bf16[8,256,128]{2,1,0:T(8,128)(2,1)} %get-tuple-element.49), calls=%async_computation.3 | async-start | bytes 1048576 | tf_op jit(solution)/shard_map/all_to_all | solution.py:342
  73.8 4.2 %collective-permute-start.2 = (bf16[32,1024]{1,0:T(8,128)(2,1)}, bf16[32,1024]{1,0:T(8,128)(2,1)S(1)}, u32[]{:S(2)}, u32[]{:S(2)}) collective-permute-start(bf16[32,1024]{1,0:T(8,128)(2,1)} %get-tuple-element.54), channel_id=1, source_target_pairs={{0,128},{64,192},{128,0},{192,64},{1,129},{65,193},{129,1},{193,65... | collective-permute-start | bytes 196616 | tf_op jit(solution)/shard_map/ppermute | solution.py:388
  78.0 2.5 %collective-permute-start.3 = (bf16[32,1024]{1,0:T(8,128)(2,1)}, bf16[32,1024]{1,0:T(8,128)(2,1)S(1)}, u32[]{:S(2)}, u32[]{:S(2)}) collective-permute-start(bf16[32,1024]{1,0:T(8,128)(2,1)} %get-tuple-element.55), channel_id=1, source_target_pairs={{0,192},{64,0},{128,64},{192,128},{1,193},{65,1},{129,65},{193,129... | collective-permute-start | bytes 196616 | tf_op jit(solution)/shard_map/ppermute | solution.py:388
  80.5 7.2 %shard_map.123 = (bf16[8,416,128]{2,1,0:T(8,128)(2,1)}, f32[4,256,128]{2,1,0:T(8,128)}, f32[4,256,128]{2,1,0:T(8,128)}) custom-call(s32[4]{0:T(128)} %and_select_fusion.refs_0_, bf16[8,384,128]{2,1,0:T(8,128)(2,1)} %copy-done, s32[8,128]{1,0:T(8,128)} %fusion.refs_2_.refs_7_, bf16[4,128,256]{2,1,0:T(8,128)(2,1)} %get-tuple-element.39.refs_3_.refs_8_, ...), custom_call_target="tpu_custom_call" | custom-call | flops 1073741824 | bytes 3739664 | tf_op jit(solution)/shard_map/pallas_call | solution.py:93
  87.8 0.6 copy-done.6
  88.4 1.8 %shard_map.125 = bf16[8,32,128]{2,1,0:T(8,128)(2,1)} custom-call(f32[32,1024]{1,0:T(8,128)} %get-tuple-element.52.refs_0_, bf16[32,1024]{1,0:T(8,128)(2,1)} %copy-done.6, bf16[32,1024]{1,0:T(8,128)(2,1)} %copy-done.7, bf16[32,1024]{1,0:T(8,128)(2,1)} %copy-done.8), custom_call_target="tpu_custom_call" | custom-call | flops 65536 | bytes 393216 | tf_op jit(solution)/shard_map/pallas_call | solution.py:93
  90.3 1.9 %collective-permute-start.5 = (bf16[8,32,128]{2,1,0:T(8,128)(2,1)}, bf16[8,32,128]{2,1,0:T(8,128)(2,1)S(1)}, u32[]{:S(2)}, u32[]{:S(2)}) collective-permute-start(bf16[8,32,128]{2,1,0:T(8,128)(2,1)} %shard_map.125), channel_id=1, source_target_pairs={{0,0},{1,32},{2,64},{3,96},{4,128},{5,160},{6,192},{7,224},{8,1},{... | collective-permute-start | bytes 196616 | tf_op jit(solution)/shard_map/ppermute | solution.py:402
  92.2 2.6 %shard_map.126.refs_1_ = bf16[8,416,128]{2,1,0:T(8,128)(2,1)} custom-call(f32[4,256,128]{2,1,0:T(8,128)} %get-tuple-element.59.refs_0_, f32[4,256,128]{2,1,0:T(8,128)} %get-tuple-element.60.refs_1_, bf16[8,256,128]{2,1,0:T(8,128)(2,1)} %copy-done.4, bf16[8,416,128]{2,1,0:T(8,128)(2,1)} %get-tuple-element.62.refs_3_), custom_call_target="tpu_custom_call", output_to_operand_aliasing={{}: (3, {})} | custom-call | flops 1048576 | bytes 3276800 | tf_op jit(solution)/shard_map/pallas_call | solution.py:93
  94.8 7.5 %collective-permute-done.5.refs_0_ = bf16[8,32,128]{2,1,0:T(8,128)(2,1)S(1)} collective-permute-done((bf16[8,32,128]{2,1,0:T(8,128)(2,1)}, bf16[8,32,128]{2,1,0:T(8,128)(2,1)S(1)}, u32[]{:S(2)}, u32[]{:S(2)}) %collective-permute-start.5) | collective-permute-done | bytes 65568 | tf_op jit(solution)/shard_map/ppermute | solution.py:402
  102.3 0.6 copy-done.5
  102.9 1.6 %shard_map.127 = bf16[8,416,128]{2,1,0:T(8,128)(2,1)} custom-call(bf16[8,32,128]{2,1,0:T(8,128)(2,1)} %copy-done.5, bf16[8,416,128]{2,1,0:T(8,128)(2,1)} %shard_map.126.refs_1_), custom_call_target="tpu_custom_call", output_to_operand_aliasing={{}: (1, {})} | custom-call | flops 1024 | bytes 1769472 | tf_op jit(solution)/shard_map/pallas_call | solution.py:93
  104.6 7.0 %all-to-all-start.4 = ((bf16[8,416,128]{2,1,0:T(8,128)(2,1)}), bf16[8,416,128]{2,1,0:T(8,128)(2,1)S(1)}, u32[]{:S(2)}, u32[]{:S(2)}) async-start(bf16[8,416,128]{2,1,0:T(8,128)(2,1)} %shard_map.127), calls=%async_computation.4 | async-start | bytes 1703936 | tf_op jit(solution)/shard_map/all_to_all | solution.py:342
  111.6 3.4 %shard_map.124 = (bf16[128,1024]{1,0:T(8,128)(2,1)}, bf16[128,1024]{1,0:T(8,128)(2,1)}) custom-call(bf16[8,256,128]{2,1,0:T(8,128)(2,1)} %copy-done.2, bf16[1024,1024]{1,0:T(8,128)(2,1)} %refs_1_.1), custom_call_target="tpu_custom_call" | custom-call | flops 268435456 | bytes 3145728 | tf_op jit(solution)/shard_map/pallas_call | solution.py:93
  115.0 10.5 %all-to-all-done.4.refs_0_ = bf16[8,416,128]{2,1,0:T(8,128)(2,1)S(1)} async-done(((bf16[8,416,128]{2,1,0:T(8,128)(2,1)}), bf16[8,416,128]{2,1,0:T(8,128)(2,1)S(1)}, u32[]{:S(2)}, u32[]{:S(2)}) %all-to-all-start.4) | async-done | bytes 852000 | tf_op jit(solution)/shard_map/all_to_all | solution.py:342
  125.5 1.2 shard_map.128
  (32 shorter events, 0.8 us)
Async XLA Ops:
  7.2 7.1 %copy-start.9 = (s32[1,8192]{1,0:T(1,128)S(1)}, s32[1,8192]{1,0:T(1,128)}, u32[]{:S(2)}) copy-start(s32[1,8192]{1,0:T(1,128)} %param.12) | copy-start | bytes 98308
  7.2 55.1 %all-gather.2.cloned.1.call-start = ((), (), s32[]{:S(2)}) async-start(), calls=%async_computation.5 | async-start | bytes 2359296 | tf_op jit(solution)/shard_map/all_gather | solution.py:348
  10.0 17.5 %all-to-all-start = ((bf16[8,384,128]{2,1,0:T(8,128)(2,1)}), bf16[8,384,128]{2,1,0:T(8,128)(2,1)S(1)}, u32[]{:S(2)}, u32[]{:S(2)}) async-start(bf16[8,384,128]{2,1,0:T(8,128)(2,1)} %shard_map.118), calls=%async_computation | async-start | bytes 1572864 | tf_op jit(solution)/shard_map/all_to_all | solution.py:342
  27.4 8.6 %copy-start = (bf16[8,384,128]{2,1,0:T(8,128)(2,1)}, bf16[8,384,128]{2,1,0:T(8,128)(2,1)S(1)}, u32[]{:S(2)}) copy-start(bf16[8,384,128]{2,1,0:T(8,128)(2,1)S(1)} %all-to-all-done.refs_1_.refs_6_) | copy-start | bytes 2359300
  27.5 18.8 %collective-permute-start = (bf16[8,256,128]{2,1,0:T(8,128)(2,1)S(1)}, bf16[8,256,128]{2,1,0:T(8,128)(2,1)S(1)}, u32[]{:S(2)}, u32[]{:S(2)}) collective-permute-start(bf16[8,256,128]{2,1,0:T(8,128)(2,1)S(1)} %slice.8), channel_id=1, source_target_pairs={{0,8},{8,16},{16,24},{24,32},{32,40},{40,48},{48,56},{1,9},{9,17},... | collective-permute-start | bytes 1572872 | tf_op jit(solution)/shard_map/ppermute | solution.py:372
  32.5 13.8 %all-to-all-start.1 = ((bf16[8,256,128]{2,1,0:T(8,128)(2,1)}), bf16[8,256,128]{2,1,0:T(8,128)(2,1)S(1)}, u32[]{:S(2)}, u32[]{:S(2)}) async-start(bf16[8,256,128]{2,1,0:T(8,128)(2,1)} %shard_map.119), calls=%async_computation.1 | async-start | bytes 1048576 | tf_op jit(solution)/shard_map/all_to_all | solution.py:342
  46.3 0.8 copy-start.1
  46.3 1.0 copy-start.3
  68.3 22.0 %collective-permute-start.4 = (bf16[8,256,128]{2,1,0:T(8,128)(2,1)}, bf16[8,256,128]{2,1,0:T(8,128)(2,1)S(1)}, u32[]{:S(2)}, u32[]{:S(2)}) collective-permute-start(bf16[8,256,128]{2,1,0:T(8,128)(2,1)} %get-tuple-element.56), channel_id=1, source_target_pairs={{8,0},{16,8},{24,16},{32,24},{40,32},{48,40},{56,48},{9,1},{17,9},... | collective-permute-start | bytes 1572872 | tf_op jit(solution)/shard_map/ppermute | solution.py:387
  70.2 22.0 %all-to-all-start.3 = ((bf16[8,256,128]{2,1,0:T(8,128)(2,1)}), bf16[8,256,128]{2,1,0:T(8,128)(2,1)S(1)}, u32[]{:S(2)}, u32[]{:S(2)}) async-start(bf16[8,256,128]{2,1,0:T(8,128)(2,1)} %get-tuple-element.49), calls=%async_computation.3 | async-start | bytes 1048576 | tf_op jit(solution)/shard_map/all_to_all | solution.py:342
  73.7 14.0 %collective-permute-start.1 = (bf16[32,1024]{1,0:T(8,128)(2,1)}, bf16[32,1024]{1,0:T(8,128)(2,1)S(1)}, u32[]{:S(2)}, u32[]{:S(2)}) collective-permute-start(bf16[32,1024]{1,0:T(8,128)(2,1)} %get-tuple-element.53), channel_id=1, source_target_pairs={{0,64},{64,128},{128,192},{192,0},{1,65},{65,129},{129,193},{193,1... | collective-permute-start | bytes 196616 | tf_op jit(solution)/shard_map/ppermute | solution.py:388
  73.8 13.9 %collective-permute-start.2 = (bf16[32,1024]{1,0:T(8,128)(2,1)}, bf16[32,1024]{1,0:T(8,128)(2,1)S(1)}, u32[]{:S(2)}, u32[]{:S(2)}) collective-permute-start(bf16[32,1024]{1,0:T(8,128)(2,1)} %get-tuple-element.54), channel_id=1, source_target_pairs={{0,128},{64,192},{128,0},{192,64},{1,129},{65,193},{129,1},{193,65... | collective-permute-start | bytes 196616 | tf_op jit(solution)/shard_map/ppermute | solution.py:388
  78.0 9.8 %collective-permute-start.3 = (bf16[32,1024]{1,0:T(8,128)(2,1)}, bf16[32,1024]{1,0:T(8,128)(2,1)S(1)}, u32[]{:S(2)}, u32[]{:S(2)}) collective-permute-start(bf16[32,1024]{1,0:T(8,128)(2,1)} %get-tuple-element.55), channel_id=1, source_target_pairs={{0,192},{64,0},{128,64},{192,128},{1,193},{65,1},{129,65},{193,129... | collective-permute-start | bytes 196616 | tf_op jit(solution)/shard_map/ppermute | solution.py:388
  87.7 0.6 copy-start.6
  87.7 0.6 copy-start.7
  87.8 0.6 copy-start.8
  90.2 2.0 %copy-start.4 = (bf16[8,256,128]{2,1,0:T(8,128)(2,1)}, bf16[8,256,128]{2,1,0:T(8,128)(2,1)S(1)}, u32[]{:S(2)}) copy-start(bf16[8,256,128]{2,1,0:T(8,128)(2,1)S(1)} %collective-permute-done.4.refs_2_) | copy-start | bytes 1572868
  90.3 12.0 %collective-permute-start.5 = (bf16[8,32,128]{2,1,0:T(8,128)(2,1)}, bf16[8,32,128]{2,1,0:T(8,128)(2,1)S(1)}, u32[]{:S(2)}, u32[]{:S(2)}) collective-permute-start(bf16[8,32,128]{2,1,0:T(8,128)(2,1)} %shard_map.125), channel_id=1, source_target_pairs={{0,0},{1,32},{2,64},{3,96},{4,128},{5,160},{6,192},{7,224},{8,1},{... | collective-permute-start | bytes 196616 | tf_op jit(solution)/shard_map/ppermute | solution.py:402
  92.2 12.4 %copy-start.2 = (bf16[8,256,128]{2,1,0:T(8,128)(2,1)}, bf16[8,256,128]{2,1,0:T(8,128)(2,1)S(1)}, u32[]{:S(2)}) copy-start(bf16[8,256,128]{2,1,0:T(8,128)(2,1)S(1)} %all-to-all-done.3.refs_0_) | copy-start | bytes 1572868
  102.3 0.6 copy-start.5
  104.6 20.9 %all-to-all-start.4 = ((bf16[8,416,128]{2,1,0:T(8,128)(2,1)}), bf16[8,416,128]{2,1,0:T(8,128)(2,1)S(1)}, u32[]{:S(2)}, u32[]{:S(2)}) async-start(bf16[8,416,128]{2,1,0:T(8,128)(2,1)} %shard_map.127), calls=%async_computation.4 | async-start | bytes 1703936 | tf_op jit(solution)/shard_map/all_to_all | solution.py:342
Sparse Core Ops, SparseCore 0:
  9.9 29.4 all-gather.1

commit v6 on v5

--- a/solution.py
+++ b/solution.py
@@ -306,11 +306,6 @@
     out.send((), (slice(None), slice(128, 384)))
 
 
-def share_body(share, out):
-    out.ref[...] = share.get()[...]
-    out.send((), (slice(None), slice(384, 416)))
-
-
 def gate_body(recv, w, out, gg):
     recv_ref = recv.get()
     for h in range(HEADS):
@@ -324,15 +319,19 @@
     out.send()
 
 
-def final_body(recv, dq, dk, dv, wg):
+def final_body(recv, dq, dk, dv):
     recv_ref = recv.get()
     for n, made in enumerate((dq, dk, dv)):
         for h in range(HEADS):
             made.ref[:, h * TOK : (h + 1) * TOK] = recv_ref[h, 128 * n : 128 * n + 128, :]
         made.send()
-    share = recv_ref[0, 384:416, :].astype(F32)
+
+
+def weight_body(recv, wg):
+    recv_ref = recv.get()
+    share = recv_ref[0].astype(F32)
     for n in range(1, HEADS):
-        share = share + recv_ref[n, 384:416, :].astype(F32)
+        share = share + recv_ref[n].astype(F32)
     for b in range(8):
         wg.ref[:, 128 * b : 128 * b + 128] = share[4 * b : 4 * b + 4, :]
     wg.send()
@@ -396,17 +395,17 @@
     got_gate = plane_exchange(gate_pack)
 
     sent, dk, dv = call(
-        bwd_own_body, "shhhhh", [shape((8, 416, 128), BF16), grad, grad], 1 << 30, [vt], kept={0: (8, 128, 128)}
+        bwd_own_body, "shhhhh", [shape((8, 384, 128), BF16), grad, grad], 1 << 30, [vt], kept={0: (8, 128, 128)}
     )(low, recv, start, qt, dmix, dqt)
-    moved, back, dk = lax.optimization_barrier((moved, back, dk))
+    sent, got_gate = lax.optimization_barrier((sent, got_gate))
+    (sent,) = call(add_body, "hhha", [shape((8, 384, 128), BF16)], 1 << 20, (), TIGHT, kept={0: (8, 256, 128)})(dk, dv, back, sent)
+    sent, moved = lax.optimization_barrier((sent, moved))
     moved = lax.ppermute(moved, ("dp", "z", "x", "c"), route)
-    sent, got_gate = lax.optimization_barrier((sent, got_gate))
-    whole = [shape((8, 416, 128), BF16)]
-    (sent,) = call(add_body, "hhha", whole, 1 << 20, (), TIGHT, kept={0: (8, 256, 128)})(dk, dv, back, sent)
-    (sent,) = call(share_body, "ha", whole, 1 << 10, kept={0: (8, 32, 128)})(moved, sent)
     got = plane_exchange(sent)
     out, gg = call(gate_body, "hh", [rows, rows], 1 << 28)(got_gate, w_out)
-    dq, dk, dv, weight_grad = call(final_body, "h", [rows] * 3 + [share], 1 << 20, (), ROOM)(got)
+    moved, got = lax.optimization_barrier((moved, got))
+    dq, dk, dv = call(final_body, "h", [rows] * 3, 1 << 20, (), ROOM)(got)
+    (weight_grad,) = call(weight_body, "h", [share], 1 << 16, (), ROOM)(plane_exchange(moved))
     return out[None], dq[None], dk[None], dv[None], gg[None], weight_grad
 
 

time: 134 us -> 132 us (0.985)
  the two profiles are of different devices: /device:TPU:104 before, /device:TPU:128 now
where the time goes in v6:
time: 132 us
  Pallas kernels  38.4 us (29%)
  starting transfers between devices  37 us (28%)
  waiting for transfers between devices  27.3 us (21%)
  between operations  14.3 us (11%)
  blocking collectives  10.1 us (8%)
  local copies, waits for them, and re-layouts  2.6 us (2%)
  other arithmetic  2.13 us (2%)
    pallas_call x11, Pallas kernels, build(): pl.pallas_call(whole, out_shape=outs, in_specs=[pl.BlockSpec(memory_space...  38.4 us
    all_to_all x5, starting transfers between devices, plane_exchange(): return lax.all_to_all(blocks, PLANE_AXES, 0, 0, tiled=True)  19.2 us
    all_to_all x5, waiting for transfers between devices, plane_exchange(): return lax.all_to_all(blocks, PLANE_AXES, 0, 0, tiled=True)  18.9 us
    all_to_all x1, blocking collectives, plane_exchange(): return lax.all_to_all(blocks, PLANE_AXES, 0, 0, tiled=True)  10.1 us
    ppermute x1, starting transfers between devices, shards(): back = lax.ppermute(back, 'z', [(i, i - 1) for i in range(1, planes)])  8.31 us
    ppermute x1, waiting for transfers between devices, shards(): moved = lax.ppermute(moved, ('dp', 'z', 'x', 'c'), route)  7.68 us
    ppermute x3, starting transfers between devices, shards(): lax.ppermute(x, 'dp', [(i, (i + n + 1) % dp) for i in range(dp)])  4.44 us
    ppermute x1, starting transfers between devices, shards(): halo = lax.ppermute(pair, 'z', [(i, i + 1) for i in range(planes - 1)])  3.04 us
  transfers between devices with their start and end apart: 12, of which 5 were waited for; matrix products, arithmetic and copies ran while one was open for 2% of the time, Pallas kernels for 23%

profile of v6, /device:TPU:128, one launch (start us, length us, event | category | flops | bytes accessed | tf_op | source)
XLA Modules:
  0.0 131.9 jit_solution(6708521424460741108)
XLA Ops:
  7.2 0.7 all-gather.2.cloned.1.call-update
  7.9 2.1 %shard_map.118 = bf16[8,384,128]{2,1,0:T(8,128)(2,1)} custom-call(bf16[128,1024]{1,0:T(8,128)(2,1)} %bitcast.18, bf16[128,1024]{1,0:T(8,128)(2,1)} %bitcast.19, bf16[128,1024]{1,0:T(8,128)(2,1)} %bitcast.20), custom_call_target="tpu_custom_call" | custom-call | flops 65536 | bytes 1572864 | tf_op jit(solution)/shard_map/pallas_call | solution.py:93
  10.0 4.3 %all-to-all-start = ((bf16[8,384,128]{2,1,0:T(8,128)(2,1)}), bf16[8,384,128]{2,1,0:T(8,128)(2,1)S(1)}, u32[]{:S(2)}, u32[]{:S(2)}) async-start(bf16[8,384,128]{2,1,0:T(8,128)(2,1)} %shard_map.118), calls=%async_computation | async-start | bytes 1572864 | tf_op jit(solution)/shard_map/all_to_all | solution.py:341
  14.7 3.5 %shard_map.119 = bf16[8,256,128]{2,1,0:T(8,128)(2,1)} custom-call(bf16[128,1024]{1,0:T(8,128)(2,1)} %bitcast.16, bf16[128,1024]{1,0:T(8,128)(2,1)} %bitcast.17, bf16[1024,1024]{1,0:T(8,128)(2,1)} %refs_1_.1), custom_call_target="tpu_custom_call" | custom-call | flops 268435456 | bytes 3145728 | tf_op jit(solution)/shard_map/pallas_call | solution.py:93
  18.2 0.7 pad_add_fusion.refs_1_
  19.4 0.6 fusion.refs_2_.refs_7_
  20.0 7.4 %all-to-all-done.refs_1_.refs_6_ = bf16[8,384,128]{2,1,0:T(8,128)(2,1)S(1)} async-done(((bf16[8,384,128]{2,1,0:T(8,128)(2,1)}), bf16[8,384,128]{2,1,0:T(8,128)(2,1)S(1)}, u32[]{:S(2)}, u32[]{:S(2)}) %all-to-all-start) | async-done | bytes 786464 | tf_op jit(solution)/shard_map/all_to_all | solution.py:341
  27.5 3.0 %collective-permute-start = (bf16[8,256,128]{2,1,0:T(8,128)(2,1)S(1)}, bf16[8,256,128]{2,1,0:T(8,128)(2,1)S(1)}, u32[]{:S(2)}, u32[]{:S(2)}) collective-permute-start(bf16[8,256,128]{2,1,0:T(8,128)(2,1)S(1)} %slice.8), channel_id=1, source_target_pairs={{0,8},{8,16},{16,24},{24,32},{32,40},{40,48},{48,56},{1,9},{9,17},... | collective-permute-start | bytes 1572872 | tf_op jit(solution)/shard_map/ppermute | solution.py:371
  30.5 3.5 %all-to-all-start.1 = ((bf16[8,256,128]{2,1,0:T(8,128)(2,1)}), bf16[8,256,128]{2,1,0:T(8,128)(2,1)S(1)}, u32[]{:S(2)}, u32[]{:S(2)}) async-start(bf16[8,256,128]{2,1,0:T(8,128)(2,1)} %shard_map.119), calls=%async_computation.1 | async-start | bytes 1048576 | tf_op jit(solution)/shard_map/all_to_all | solution.py:341
  34.1 6.8 %shard_map.120 = (f32[4,128,256]{2,1,0:T(8,128)}, bf16[4,128,256]{2,1,0:T(8,128)(2,1)}) custom-call(s32[4]{0:T(128)} %and_select_fusion.refs_0_, bf16[8,384,128]{2,1,0:T(8,128)(2,1)} %copy-done, s32[8,128]{1,0:T(8,128)} %fusion.refs_2_.refs_7_), custom_call_target="tpu_custom_call" | custom-call | flops 536870912 | bytes 1576976 | tf_op jit(solution)/shard_map/pallas_call | solution.py:93
  40.9 3.4 %all-to-all-done.1.refs_5_.refs_3_ = bf16[8,256,128]{2,1,0:T(8,128)(2,1)S(1)} async-done(((bf16[8,256,128]{2,1,0:T(8,128)(2,1)}), bf16[8,256,128]{2,1,0:T(8,128)(2,1)S(1)}, u32[]{:S(2)}, u32[]{:S(2)}) %all-to-all-start.1) | async-done | bytes 524320 | tf_op jit(solution)/shard_map/all_to_all | solution.py:341
  44.3 0.8 copy-done.1
  45.3 3.6 %shard_map.121 = (f32[4,128,256]{2,1,0:T(8,128)}, f32[8,32,128]{2,1,0:T(8,128)}) custom-call(s32[4]{0:T(128)} %and_select_fusion.refs_0_, bf16[8,256,128]{2,1,0:T(8,128)(2,1)} %copy-done.3, s32[8,128]{1,0:T(8,128)} %fusion.refs_2_.refs_7_, bf16[4,128,256]{2,1,0:T(8,128)(2,1)} %get-tuple-element.39.refs_3_.refs_8_, f32[4,128,256]{2,1,0:T(8,128)} %get-tuple-element.42.refs_4_, ...), custom_call_target="tpu_custom_call" | custom-call | flops 268435456 | bytes 2494480 | tf_op jit(solution)/shard_map/pallas_call | solution.py:93
  49.0 10.1 %all_to_all.30.refs_4_ = f32[8,32,128]{2,1,0:T(8,128)} all-to-all(f32[8,32,128]{2,1,0:T(8,128)} %get-tuple-element.45), channel_id=1, replica_groups=mesh['dp'=4,'z'=8,'x'=4,'c'=2] {'x','c'}, dimensions={0} | all-to-all | bytes 262144 | tf_op jit(solution)/shard_map/all_to_all | solution.py:341
  59.1 4.6 %shard_map.122 = (bf16[8,256,128]{2,1,0:T(8,128)(2,1)}, bf16[4,128,256]{2,1,0:T(8,128)(2,1)}, f32[4,128,256]{2,1,0:T(8,128)}, bf16[8,256,128]{2,1,0:T(8,128)(2,1...) custom-call(s32[4]{0:T(128)} %and_select_fusion.refs_0_, ...), custom_call_target="tpu_custom_call" | custom-call | flops 536870912 | bytes 7016472 | tf_op jit(solution)/shard_map/pallas_call | solution.py:93
  63.7 8.3 %collective-permute-start.1 = (bf16[8,256,128]{2,1,0:T(8,128)(2,1)}, bf16[8,256,128]{2,1,0:T(8,128)(2,1)S(1)}, u32[]{:S(2)}, u32[]{:S(2)}) collective-permute-start(bf16[8,256,128]{2,1,0:T(8,128)(2,1)} %get-tuple-element.54), channel_id=1, source_target_pairs={{8,0},{16,8},{24,16},{32,24},{40,32},{48,40},{56,48},{9,1},{17,9},... | collective-permute-start | bytes 1572872 | tf_op jit(solution)/shard_map/ppermute | solution.py:386
  72.0 3.5 %all-to-all-start.3 = ((bf16[8,256,128]{2,1,0:T(8,128)(2,1)}), bf16[8,256,128]{2,1,0:T(8,128)(2,1)S(1)}, u32[]{:S(2)}, u32[]{:S(2)}) async-start(bf16[8,256,128]{2,1,0:T(8,128)(2,1)} %get-tuple-element.49), calls=%async_computation.3 | async-start | bytes 1048576 | tf_op jit(solution)/shard_map/all_to_all | solution.py:341
  75.6 1.7 %collective-permute-start.2 = (bf16[32,1024]{1,0:T(8,128)(2,1)}, bf16[32,1024]{1,0:T(8,128)(2,1)S(1)}, u32[]{:S(2)}, u32[]{:S(2)}) collective-permute-start(bf16[32,1024]{1,0:T(8,128)(2,1)} %get-tuple-element.57), channel_id=1, source_target_pairs={{0,64},{64,128},{128,192},{192,0},{1,65},{65,129},{129,193},{193,1... | collective-permute-start | bytes 196616 | tf_op jit(solution)/shard_map/ppermute | solution.py:387
  77.6 2.4 %collective-permute-start.4 = (bf16[32,1024]{1,0:T(8,128)(2,1)}, bf16[32,1024]{1,0:T(8,128)(2,1)S(1)}, u32[]{:S(2)}, u32[]{:S(2)}) collective-permute-start(bf16[32,1024]{1,0:T(8,128)(2,1)} %get-tuple-element.59), channel_id=1, source_target_pairs={{0,192},{64,0},{128,64},{192,128},{1,193},{65,1},{129,65},{193,129... | collective-permute-start | bytes 196616 | tf_op jit(solution)/shard_map/ppermute | solution.py:387
  80.0 8.2 %shard_map.123 = (bf16[8,384,128]{2,1,0:T(8,128)(2,1)}, f32[4,256,128]{2,1,0:T(8,128)}, f32[4,256,128]{2,1,0:T(8,128)}) custom-call(s32[4]{0:T(128)} %and_select_fusion.refs_0_, bf16[8,384,128]{2,1,0:T(8,128)(2,1)} %copy-done, s32[8,128]{1,0:T(8,128)} %fusion.refs_2_.refs_7_, bf16[4,128,256]{2,1,0:T(8,128)(2,1)} %get-tuple-element.39.refs_3_.refs_8_, ...), custom_call_target="tpu_custom_call" | custom-call | flops 1073741824 | bytes 3674128 | tf_op jit(solution)/shard_map/pallas_call | solution.py:93
  88.9 1.8 %shard_map.126 = bf16[8,32,128]{2,1,0:T(8,128)(2,1)} custom-call(f32[32,1024]{1,0:T(8,128)} %get-tuple-element.56.refs_0_, bf16[32,1024]{1,0:T(8,128)(2,1)} %copy-done.5, bf16[32,1024]{1,0:T(8,128)(2,1)} %copy-done.6, bf16[32,1024]{1,0:T(8,128)(2,1)} %copy-done.8), custom_call_target="tpu_custom_call" | custom-call | flops 65536 | bytes 393216 | tf_op jit(solution)/shard_map/pallas_call | solution.py:93
  90.7 0.8 copy-done.4
  91.5 2.5 %shard_map.125 = bf16[8,384,128]{2,1,0:T(8,128)(2,1)} custom-call(f32[4,256,128]{2,1,0:T(8,128)} %get-tuple-element.52.refs_0_, f32[4,256,128]{2,1,0:T(8,128)} %get-tuple-element.53.refs_1_, bf16[8,256,128]{2,1,0:T(8,128)(2,1)} %copy-done.4, bf16[8,384,128]{2,1,0:T(8,128)(2,1)} %get-tuple-element.55.refs_3_), custom_call_target="tpu_custom_call", output_to_operand_aliasing={{}: (3, {})} | custom-call | flops 1048576 | bytes 3145728 | tf_op jit(solution)/shard_map/pallas_call | solution.py:93
  94.0 4.6 %all-to-all-start.4 = ((bf16[8,384,128]{2,1,0:T(8,128)(2,1)}), bf16[8,384,128]{2,1,0:T(8,128)(2,1)S(1)}, u32[]{:S(2)}, u32[]{:S(2)}) async-start(bf16[8,384,128]{2,1,0:T(8,128)(2,1)} %shard_map.125), calls=%async_computation.4 | async-start | bytes 1572864 | tf_op jit(solution)/shard_map/all_to_all | solution.py:341
  98.6 1.9 %collective-permute-start.5 = (bf16[8,32,128]{2,1,0:T(8,128)(2,1)S(1)}, bf16[8,32,128]{2,1,0:T(8,128)(2,1)}, u32[]{:S(2)}, u32[]{:S(2)}) collective-permute-start(bf16[8,32,128]{2,1,0:T(8,128)(2,1)S(1)} %copy-done.7), channel_id=1, source_target_pairs={{0,0},{1,32},{2,64},{3,96},{4,128},{5,160},{6,192},{7,224},{8,1},{... | collective-permute-start | bytes 196616 | tf_op jit(solution)/shard_map/ppermute | solution.py:403
  100.5 7.7 %collective-permute-done.5 = bf16[8,32,128]{2,1,0:T(8,128)(2,1)} collective-permute-done((bf16[8,32,128]{2,1,0:T(8,128)(2,1)S(1)}, bf16[8,32,128]{2,1,0:T(8,128)(2,1)}, u32[]{:S(2)}, u32[]{:S(2)}) %collective-permute-start.5) | collective-permute-done | bytes 65568 | tf_op jit(solution)/shard_map/ppermute | solution.py:403
  108.2 7.1 %all-to-all-done.4.refs_0_ = bf16[8,384,128]{2,1,0:T(8,128)(2,1)S(1)} async-done(((bf16[8,384,128]{2,1,0:T(8,128)(2,1)}), bf16[8,384,128]{2,1,0:T(8,128)(2,1)S(1)}, u32[]{:S(2)}, u32[]{:S(2)}) %all-to-all-start.4) | async-done | bytes 786464 | tf_op jit(solution)/shard_map/all_to_all | solution.py:341
  115.3 3.3 %all-to-all-start.5 = ((bf16[8,32,128]{2,1,0:T(8,128)(2,1)}), bf16[8,32,128]{2,1,0:T(8,128)(2,1)S(1)}, u32[]{:S(2)}, u32[]{:S(2)}) async-start(bf16[8,32,128]{2,1,0:T(8,128)(2,1)} %collective-permute-done.5), calls=%async_computation.5 | async-start | bytes 131072 | tf_op jit(solution)/shard_map/all_to_all | solution.py:341
  118.6 3.4 %shard_map.124 = (bf16[128,1024]{1,0:T(8,128)(2,1)}, bf16[128,1024]{1,0:T(8,128)(2,1)}) custom-call(bf16[8,256,128]{2,1,0:T(8,128)(2,1)} %copy-done.2, bf16[1024,1024]{1,0:T(8,128)(2,1)} %refs_1_.1), custom_call_target="tpu_custom_call" | custom-call | flops 268435456 | bytes 3145728 | tf_op jit(solution)/shard_map/pallas_call | solution.py:93
  122.0 1.2 shard_map.127
  123.2 1.0 all-to-all-done.5.refs_0_
  124.2 0.8 shard_map.128
  (34 shorter events, 2.2 us)
Async XLA Ops:
  7.2 7.1 %copy-start.9 = (s32[1,8192]{1,0:T(1,128)S(1)}, s32[1,8192]{1,0:T(1,128)}, u32[]{:S(2)}) copy-start(s32[1,8192]{1,0:T(1,128)} %param.12) | copy-start | bytes 98308
  7.2 51.9 %all-gather.2.cloned.1.call-start = ((), (), s32[]{:S(2)}) async-start(), calls=%async_computation.6 | async-start | bytes 2359296 | tf_op jit(solution)/shard_map/all_gather | solution.py:347
  10.0 17.5 %all-to-all-start = ((bf16[8,384,128]{2,1,0:T(8,128)(2,1)}), bf16[8,384,128]{2,1,0:T(8,128)(2,1)S(1)}, u32[]{:S(2)}, u32[]{:S(2)}) async-start(bf16[8,384,128]{2,1,0:T(8,128)(2,1)} %shard_map.118), calls=%async_computation | async-start | bytes 1572864 | tf_op jit(solution)/shard_map/all_to_all | solution.py:341
  27.5 6.6 %copy-start = (bf16[8,384,128]{2,1,0:T(8,128)(2,1)}, bf16[8,384,128]{2,1,0:T(8,128)(2,1)S(1)}, u32[]{:S(2)}) copy-start(bf16[8,384,128]{2,1,0:T(8,128)(2,1)S(1)} %all-to-all-done.refs_1_.refs_6_) | copy-start | bytes 2359300
  27.5 16.8 %collective-permute-start = (bf16[8,256,128]{2,1,0:T(8,128)(2,1)S(1)}, bf16[8,256,128]{2,1,0:T(8,128)(2,1)S(1)}, u32[]{:S(2)}, u32[]{:S(2)}) collective-permute-start(bf16[8,256,128]{2,1,0:T(8,128)(2,1)S(1)} %slice.8), channel_id=1, source_target_pairs={{0,8},{8,16},{16,24},{24,32},{32,40},{40,48},{48,56},{1,9},{9,17},... | collective-permute-start | bytes 1572872 | tf_op jit(solution)/shard_map/ppermute | solution.py:371
  30.5 13.8 %all-to-all-start.1 = ((bf16[8,256,128]{2,1,0:T(8,128)(2,1)}), bf16[8,256,128]{2,1,0:T(8,128)(2,1)S(1)}, u32[]{:S(2)}, u32[]{:S(2)}) async-start(bf16[8,256,128]{2,1,0:T(8,128)(2,1)} %shard_map.119), calls=%async_computation.1 | async-start | bytes 1048576 | tf_op jit(solution)/shard_map/all_to_all | solution.py:341
  44.3 0.8 copy-start.1
  44.3 1.0 copy-start.3
  63.7 27.0 %collective-permute-start.1 = (bf16[8,256,128]{2,1,0:T(8,128)(2,1)}, bf16[8,256,128]{2,1,0:T(8,128)(2,1)S(1)}, u32[]{:S(2)}, u32[]{:S(2)}) collective-permute-start(bf16[8,256,128]{2,1,0:T(8,128)(2,1)} %get-tuple-element.54), channel_id=1, source_target_pairs={{8,0},{16,8},{24,16},{32,24},{40,32},{48,40},{56,48},{9,1},{17,9},... | collective-permute-start | bytes 1572872 | tf_op jit(solution)/shard_map/ppermute | solution.py:386
  72.0 18.6 %all-to-all-start.3 = ((bf16[8,256,128]{2,1,0:T(8,128)(2,1)}), bf16[8,256,128]{2,1,0:T(8,128)(2,1)S(1)}, u32[]{:S(2)}, u32[]{:S(2)}) async-start(bf16[8,256,128]{2,1,0:T(8,128)(2,1)} %get-tuple-element.49), calls=%async_computation.3 | async-start | bytes 1048576 | tf_op jit(solution)/shard_map/all_to_all | solution.py:341
  75.6 12.6 %collective-permute-start.2 = (bf16[32,1024]{1,0:T(8,128)(2,1)}, bf16[32,1024]{1,0:T(8,128)(2,1)S(1)}, u32[]{:S(2)}, u32[]{:S(2)}) collective-permute-start(bf16[32,1024]{1,0:T(8,128)(2,1)} %get-tuple-element.57), channel_id=1, source_target_pairs={{0,64},{64,128},{128,192},{192,0},{1,65},{65,129},{129,193},{193,1... | collective-permute-start | bytes 196616 | tf_op jit(solution)/shard_map/ppermute | solution.py:387
  77.2 11.0 %collective-permute-start.3 = (bf16[32,1024]{1,0:T(8,128)(2,1)}, bf16[32,1024]{1,0:T(8,128)(2,1)S(1)}, u32[]{:S(2)}, u32[]{:S(2)}) collective-permute-start(bf16[32,1024]{1,0:T(8,128)(2,1)} %get-tuple-element.58), channel_id=1, source_target_pairs={{0,128},{64,192},{128,0},{192,64},{1,129},{65,193},{129,1},{193,65... | collective-permute-start | bytes 196616 | tf_op jit(solution)/shard_map/ppermute | solution.py:387
  77.6 10.7 %collective-permute-start.4 = (bf16[32,1024]{1,0:T(8,128)(2,1)}, bf16[32,1024]{1,0:T(8,128)(2,1)S(1)}, u32[]{:S(2)}, u32[]{:S(2)}) collective-permute-start(bf16[32,1024]{1,0:T(8,128)(2,1)} %get-tuple-element.59), channel_id=1, source_target_pairs={{0,192},{64,0},{128,64},{192,128},{1,193},{65,1},{129,65},{193,129... | collective-permute-start | bytes 196616 | tf_op jit(solution)/shard_map/ppermute | solution.py:387
  88.2 0.6 copy-start.5
  88.2 0.6 copy-start.6
  88.2 0.6 copy-start.8
  90.7 3.3 %copy-start.2 = (bf16[8,256,128]{2,1,0:T(8,128)(2,1)}, bf16[8,256,128]{2,1,0:T(8,128)(2,1)S(1)}, u32[]{:S(2)}) copy-start(bf16[8,256,128]{2,1,0:T(8,128)(2,1)S(1)} %all-to-all-done.3.refs_0_) | copy-start | bytes 1572868
  90.7 0.8 copy-start.4
  91.5 7.0 %copy-start.7 = (bf16[8,32,128]{2,1,0:T(8,128)(2,1)S(1)}, bf16[8,32,128]{2,1,0:T(8,128)(2,1)}, u32[]{:S(2)}) copy-start(bf16[8,32,128]{2,1,0:T(8,128)(2,1)} %shard_map.126) | copy-start | bytes 196612
  94.0 21.2 %all-to-all-start.4 = ((bf16[8,384,128]{2,1,0:T(8,128)(2,1)}), bf16[8,384,128]{2,1,0:T(8,128)(2,1)S(1)}, u32[]{:S(2)}, u32[]{:S(2)}) async-start(bf16[8,384,128]{2,1,0:T(8,128)(2,1)} %shard_map.125), calls=%async_computation.4 | async-start | bytes 1572864 | tf_op jit(solution)/shard_map/all_to_all | solution.py:341
  98.6 9.6 %collective-permute-start.5 = (bf16[8,32,128]{2,1,0:T(8,128)(2,1)S(1)}, bf16[8,32,128]{2,1,0:T(8,128)(2,1)}, u32[]{:S(2)}, u32[]{:S(2)}) collective-permute-start(bf16[8,32,128]{2,1,0:T(8,128)(2,1)S(1)} %copy-done.7), channel_id=1, source_target_pairs={{0,0},{1,32},{2,64},{3,96},{4,128},{5,160},{6,192},{7,224},{8,1},{... | collective-permute-start | bytes 196616 | tf_op jit(solution)/shard_map/ppermute | solution.py:403
  115.3 8.9 %all-to-all-start.5 = ((bf16[8,32,128]{2,1,0:T(8,128)(2,1)}), bf16[8,32,128]{2,1,0:T(8,128)(2,1)S(1)}, u32[]{:S(2)}, u32[]{:S(2)}) async-start(bf16[8,32,128]{2,1,0:T(8,128)(2,1)} %collective-permute-done.5), calls=%async_computation.5 | async-start | bytes 131072 | tf_op jit(solution)/shard_map/all_to_all | solution.py:341
Sparse Core Ops, SparseCore 0:
  9.9 29.3 all-gather.1

commit v7 on v4

--- a/solution.py
+++ b/solution.py
@@ -297,25 +297,17 @@
         dv.send((i,))
 
 
-def add_body(dk, dv, back, share, out):
-    share_ref, next_ref, dk_ref, dv_ref = share.get(), back.get(), dk.get(), dv.get()
+def add_body(dk, dv, back, out):
+    next_ref, dk_ref, dv_ref = back.get(), dk.get(), dv.get()
     for b in range(HEADS):
         rows = slice((b % 2) * TOK, (b % 2 + 1) * TOK)
         out.ref[b, 0:128, :] = (dk_ref[b // 2, rows, :] + next_ref[b, 0:128, :].astype(F32)).astype(BF16)
         out.ref[b, 128:256, :] = (dv_ref[b // 2, rows, :] + next_ref[b, 128:256, :].astype(F32)).astype(BF16)
-    out.ref[:, 256:288, :] = share_ref[...]
-    out.send((), (slice(None), slice(384, 672)))
-
-
-def final_body(recv, w, out, dq, dk, dv, gg, wg):
+    out.send((), (slice(None), slice(384, 640)))
+
+
+def final_body(recv, w, out, dq, dk, dv, gg):
     recv_ref = recv.get()
-    share = recv_ref[0, 640:672, :].astype(F32)
-    for n in range(1, HEADS):
-        share = share + recv_ref[n, 640:672, :].astype(F32)
-    for b in range(8):
-        wg.ref[:, 128 * b : 128 * b + 128] = share[4 * b : 4 * b + 4, :]
-    wg.send()
-    w_ref = w.get()
     for n, made in enumerate((dq, dk, dv)):
         for h in range(HEADS):
             made.ref[:, h * TOK : (h + 1) * TOK] = recv_ref[h, 256 + 128 * n : 384 + 128 * n, :]
@@ -323,11 +315,23 @@
     for h in range(HEADS):
         gg.ref[:, h * TOK : (h + 1) * TOK] = flip(recv_ref[h, 128:256, :])
     gg.send()
+    w_ref = w.get()
     total = dot(flip(recv_ref[0, 0:128, :]), w_ref[0:TOK, :])
     for h in range(1, HEADS):
         total = total + dot(flip(recv_ref[h, 0:128, :]), w_ref[h * TOK : (h + 1) * TOK, :])
     out.ref[...] = total.astype(BF16)
     out.send()
+
+
+def weight_body(who_ref, recv, wg):
+    recv_ref = recv.get()
+    rank = who_ref[2]
+    share = recv_ref[0, rank].astype(F32)
+    for n in range(1, HEADS):
+        share = share + recv_ref[n, rank].astype(F32)
+    for b in range(8):
+        wg.ref[:, 128 * b : 128 * b + 128] = share[4 * b : 4 * b + 4, :]
+    wg.send()
 
 
 def plane_exchange(blocks):
@@ -350,7 +354,7 @@
     recv = plane_exchange(packed)
 
     replica, plane = lax.axis_index("dp"), lax.axis_index("z")
-    who = jnp.stack([replica, plane]).astype(jnp.int32)
+    who = jnp.stack([replica, plane, lax.axis_index(PLANE_AXES)]).astype(jnp.int32)
     place = plane * PLANE
     users = jnp.arange(USERS, dtype=jnp.int32)[:, None]
     first = jnp.sum((seg[None, :] < users).astype(jnp.int32), axis=1)
@@ -373,7 +377,7 @@
     far = shape((32, 1024), BF16)
     sent, dmix, dqt, back, own, *fars = call(
         middle_body, "sshhhhhhhh",
-        [shape((8, 672, 128), BF16), head16, head, shape((8, 256, 128), BF16), shape((32, 1024), F32), far, far, far],
+        [shape((8, 640, 128), BF16), head16, head, shape((8, 256, 128), BF16), shape((32, 1024), F32), far, far, far],
         1 << 29, [vt, acc, acc, pltpu.VMEM((128, 1024), F32)], kept={0: (8, 256, 128)}, held=only_q,
     )(low, who, mixt, gd_recv, stats, halo, recv, start, qt, cot_plane)
     back = lax.ppermute(back, "z", [(i, i - 1) for i in range(1, planes)])
@@ -385,14 +389,17 @@
         for z in range(planes):
             for r in range(8):
                 route.append(((d * planes + z) * 8 + r, (r // 2 * planes + (r % 2) * 4 + d) * 8 + z))
+
+    sent, dk, dv = call(
+        bwd_own_body, "shhhhha", [shape((8, 640, 128), BF16), grad, grad], 1 << 30, [vt], kept={0: (8, 128, 128)}
+    )(low, recv, start, qt, dmix, dqt, sent)
+    (sent,) = call(add_body, "hhha", [shape((8, 640, 128), BF16)], 1 << 20, (), TIGHT, kept={0: (8, 256, 128)})(dk, dv, back, sent)
+    sent, moved = lax.optimization_barrier((sent, moved))
     moved = lax.ppermute(moved, ("dp", "z", "x", "c"), route)
-
-    sent, dk, dv = call(
-        bwd_own_body, "shhhhha", [shape((8, 672, 128), BF16), grad, grad], 1 << 30, [vt], kept={0: (8, 128, 128)}
-    )(low, recv, start, qt, dmix, dqt, sent)
-    (sent,) = call(add_body, "hhhha", [shape((8, 672, 128), BF16)], 1 << 20, (), TIGHT, kept={0: (8, 288, 128)})(dk, dv, back, moved, sent)
     got = plane_exchange(sent)
-    out, dq, dk, dv, gg, weight_grad = call(final_body, "hh", [rows] * 5 + [share], 1 << 28, (), ROOM)(got, w_out)
+    shares = lax.all_gather(moved, PLANE_AXES)
+    out, dq, dk, dv, gg = call(final_body, "hh", [rows] * 5, 1 << 28, (), ROOM)(got, w_out)
+    (weight_grad,) = call(weight_body, "sh", [share], 1 << 16)(who, shares)
     return out[None], dq[None], dk[None], dv[None], gg[None], weight_grad
 
 

time: 136 us -> 140 us (1.029)
  the two profiles are of different devices: /device:TPU:8 before, /device:TPU:203 now
where the time goes in v7:
time: 140 us; the launch traced here: 137 us
  starting transfers between devices  35.6 us (25%)
  Pallas kernels  35.1 us (25%)
  blocking collectives  34.7 us (25%)
  between operations  14.3 us (10%)
  waiting for transfers between devices  13.1 us (9%)
  local copies, waits for them, and re-layouts  2.54 us (2%)
  other arithmetic  2.04 us (1%)
    pallas_call x10, Pallas kernels, build(): pl.pallas_call(whole, out_shape=outs, in_specs=[pl.BlockSpec(memory_space...  35.1 us
    all_gather x1, blocking collectives, shards(): shares = lax.all_gather(moved, PLANE_AXES)  24.6 us
    all_to_all x3, starting transfers between devices, plane_exchange(): return lax.all_to_all(blocks, PLANE_AXES, 0, 0, tiled=True)  18.6 us
    all_to_all x1, blocking collectives, plane_exchange(): return lax.all_to_all(blocks, PLANE_AXES, 0, 0, tiled=True)  10.1 us
    all_to_all x3, waiting for transfers between devices, plane_exchange(): return lax.all_to_all(blocks, PLANE_AXES, 0, 0, tiled=True)  8.32 us
    ppermute x1, starting transfers between devices, shards(): back = lax.ppermute(back, 'z', [(i, i - 1) for i in range(1, planes)])  4.85 us
    ppermute x1, starting transfers between devices, shards(): moved = lax.ppermute(moved, ('dp', 'z', 'x', 'c'), route)  4.81 us
    ppermute x3, starting transfers between devices, shards(): lax.ppermute(x, 'dp', [(i, (i + n + 1) % dp) for i in range(dp)])  4.35 us
  transfers between devices with their start and end apart: 10, of which 3 were waited for; matrix products, arithmetic and copies ran while one was open for 2% of the time, Pallas kernels for 19%

profile of v7, /device:TPU:203, one launch (start us, length us, event | category | flops | bytes accessed | tf_op | source)
XLA Modules:
  0.0 137.4 jit_solution(10775606577846853058)
XLA Ops:
  7.2 0.7 all-gather.3.cloned.1.call-update
  7.9 2.1 %shard_map.118 = bf16[8,384,128]{2,1,0:T(8,128)(2,1)} custom-call(bf16[128,1024]{1,0:T(8,128)(2,1)} %bitcast.21, bf16[128,1024]{1,0:T(8,128)(2,1)} %bitcast.22, bf16[128,1024]{1,0:T(8,128)(2,1)} %bitcast.23), custom_call_target="tpu_custom_call" | custom-call | flops 65536 | bytes 1572864 | tf_op jit(solution)/shard_map/pallas_call | solution.py:93
  10.0 5.2 %all-to-all-start = ((bf16[8,384,128]{2,1,0:T(8,128)(2,1)}), bf16[8,384,128]{2,1,0:T(8,128)(2,1)S(1)}, u32[]{:S(2)}, u32[]{:S(2)}) async-start(bf16[8,384,128]{2,1,0:T(8,128)(2,1)} %shard_map.118), calls=%async_computation | async-start | bytes 1572864 | tf_op jit(solution)/shard_map/all_to_all | solution.py:338
  15.2 0.2 convert_reduce_fusion
  15.6 3.5 %shard_map.119 = bf16[8,256,128]{2,1,0:T(8,128)(2,1)} custom-call(bf16[128,1024]{1,0:T(8,128)(2,1)} %bitcast.19, bf16[128,1024]{1,0:T(8,128)(2,1)} %bitcast.20, bf16[1024,1024]{1,0:T(8,128)(2,1)} %refs_1_.1), custom_call_target="tpu_custom_call" | custom-call | flops 268435456 | bytes 3145728 | tf_op jit(solution)/shard_map/pallas_call | solution.py:93
  19.1 0.6 pad_add_fusion.refs_1_.refs_0_
  19.7 0.5 and_select_fusion.refs_0_
  20.2 0.6 fusion.refs_2_.refs_7_
  20.8 5.6 %all-to-all-done.refs_1_.refs_6_ = bf16[8,384,128]{2,1,0:T(8,128)(2,1)S(1)} async-done(((bf16[8,384,128]{2,1,0:T(8,128)(2,1)}), bf16[8,384,128]{2,1,0:T(8,128)(2,1)S(1)}, u32[]{:S(2)}, u32[]{:S(2)}) %all-to-all-start) | async-done | bytes 786464 | tf_op jit(solution)/shard_map/all_to_all | solution.py:338
  26.4 2.9 %collective-permute-start = (bf16[8,256,128]{2,1,0:T(8,128)(2,1)S(1)}, bf16[8,256,128]{2,1,0:T(8,128)(2,1)S(1)}, u32[]{:S(2)}, u32[]{:S(2)}) collective-permute-start(bf16[8,256,128]{2,1,0:T(8,128)(2,1)S(1)} %slice.8), channel_id=1, source_target_pairs={{0,8},{8,16},{16,24},{24,32},{32,40},{40,48},{48,56},{1,9},{9,17},... | collective-permute-start | bytes 1572872 | tf_op jit(solution)/shard_map/ppermute | solution.py:368
  29.4 6.8 %all-to-all-start.1 = ((bf16[8,256,128]{2,1,0:T(8,128)(2,1)}), bf16[8,256,128]{2,1,0:T(8,128)(2,1)S(1)}, u32[]{:S(2)}, u32[]{:S(2)}) async-start(bf16[8,256,128]{2,1,0:T(8,128)(2,1)} %shard_map.119), calls=%async_computation.1 | async-start | bytes 1048576 | tf_op jit(solution)/shard_map/all_to_all | solution.py:338
  36.1 5.6 %shard_map.120 = (f32[4,128,256]{2,1,0:T(8,128)}, bf16[4,128,256]{2,1,0:T(8,128)(2,1)}) custom-call(s32[4]{0:T(128)} %and_select_fusion.refs_0_, bf16[8,384,128]{2,1,0:T(8,128)(2,1)} %copy-done.1, s32[8,128]{1,0:T(8,128)} %fusion.refs_2_.refs_7_), custom_call_target="tpu_custom_call" | custom-call | flops 536870912 | bytes 1576976 | tf_op jit(solution)/shard_map/pallas_call | solution.py:93
  41.8 2.8 %all-to-all-done.1.refs_5_.refs_3_ = bf16[8,256,128]{2,1,0:T(8,128)(2,1)S(1)} async-done(((bf16[8,256,128]{2,1,0:T(8,128)(2,1)}), bf16[8,256,128]{2,1,0:T(8,128)(2,1)S(1)}, u32[]{:S(2)}, u32[]{:S(2)}) %all-to-all-start.1) | async-done | bytes 524320 | tf_op jit(solution)/shard_map/all_to_all | solution.py:338
  44.5 0.8 copy-done.2
  45.5 3.6 %shard_map.121 = (f32[4,128,256]{2,1,0:T(8,128)}, f32[8,32,128]{2,1,0:T(8,128)}) custom-call(s32[4]{0:T(128)} %and_select_fusion.refs_0_, bf16[8,256,128]{2,1,0:T(8,128)(2,1)} %copy-done.3, s32[8,128]{1,0:T(8,128)} %fusion.refs_2_.refs_7_, bf16[4,128,256]{2,1,0:T(8,128)(2,1)} %get-tuple-element.35.refs_3_.refs_8_, f32[4,128,256]{2,1,0:T(8,128)} %get-tuple-element.38.refs_4_, ...), custom_call_target="tpu_custom_call" | custom-call | flops 268435456 | bytes 2494480 | tf_op jit(solution)/shard_map/pallas_call | solution.py:93
  49.1 10.1 %all_to_all.20.refs_4_ = f32[8,32,128]{2,1,0:T(8,128)} all-to-all(f32[8,32,128]{2,1,0:T(8,128)} %get-tuple-element.41), channel_id=1, replica_groups=mesh['dp'=4,'z'=8,'x'=4,'c'=2] {'x','c'}, dimensions={0} | all-to-all | bytes 262144 | tf_op jit(solution)/shard_map/all_to_all | solution.py:338
  59.3 4.6 %shard_map.122 = (bf16[8,640,128]{2,1,0:T(8,128)(2,1)}, bf16[4,128,256]{2,1,0:T(8,128)(2,1)}, f32[4,128,256]{2,1,0:T(8,128)}, bf16[8,256,128]{2,1,0:T(8,128)(2,1...) custom-call(s32[4]{0:T(128)} %and_select_fusion.refs_0_, ...), custom_call_target="tpu_custom_call" | custom-call | flops 536870912 | bytes 7802908 | tf_op jit(solution)/shard_map/pallas_call | solution.py:93
  63.9 4.9 %collective-permute-start.1 = (bf16[8,256,128]{2,1,0:T(8,128)(2,1)}, bf16[8,256,128]{2,1,0:T(8,128)(2,1)S(1)}, u32[]{:S(2)}, u32[]{:S(2)}) collective-permute-start(bf16[8,256,128]{2,1,0:T(8,128)(2,1)} %get-tuple-element.47), channel_id=1, source_target_pairs={{8,0},{16,8},{24,16},{32,24},{40,32},{48,40},{56,48},{9,1},{17,9},... | collective-permute-start | bytes 1572872 | tf_op jit(solution)/shard_map/ppermute | solution.py:383
  68.8 1.1 collective-permute-start.2
  69.9 1.3 collective-permute-start.3
  71.1 2.0 %collective-permute-start.4 = (bf16[32,1024]{1,0:T(8,128)(2,1)}, bf16[32,1024]{1,0:T(8,128)(2,1)S(1)}, u32[]{:S(2)}, u32[]{:S(2)}) collective-permute-start(bf16[32,1024]{1,0:T(8,128)(2,1)} %get-tuple-element.52), channel_id=1, source_target_pairs={{0,192},{64,0},{128,64},{192,128},{1,193},{65,1},{129,65},{193,129... | collective-permute-start | bytes 196616 | tf_op jit(solution)/shard_map/ppermute | solution.py:384
  73.1 6.8 %shard_map.123 = (bf16[8,640,128]{2,1,0:T(8,128)(2,1)}, f32[4,256,128]{2,1,0:T(8,128)}, f32[4,256,128]{2,1,0:T(8,128)}) custom-call(s32[4]{0:T(128)} %and_select_fusion.refs_0_, bf16[8,384,128]{2,1,0:T(8,128)(2,1)} %copy-done.1, s32[8,128]{1,0:T(8,128)} %fusion.refs_2_.refs_7_, ...), custom_call_target="tpu_custom_call", output_to_operand_aliasing={{0}: (6, {})} | custom-call | flops 1073741824 | bytes 5509136 | tf_op jit(solution)/shard_map/pallas_call | solution.py:93
  80.0 0.6 copy-done.5
  80.6 1.8 %shard_map.125 = bf16[8,32,128]{2,1,0:T(8,128)(2,1)} custom-call(f32[32,1024]{1,0:T(8,128)} %get-tuple-element.49.refs_0_, bf16[32,1024]{1,0:T(8,128)(2,1)} %copy-done.5, bf16[32,1024]{1,0:T(8,128)(2,1)} %copy-done.6, bf16[32,1024]{1,0:T(8,128)(2,1)} %copy-done.7), custom_call_target="tpu_custom_call" | custom-call | flops 65536 | bytes 393216 | tf_op jit(solution)/shard_map/pallas_call | solution.py:93
  82.4 0.8 copy-done.4
  83.2 2.4 %shard_map.124 = bf16[8,640,128]{2,1,0:T(8,128)(2,1)} custom-call(f32[4,256,128]{2,1,0:T(8,128)} %get-tuple-element.45.refs_0_, f32[4,256,128]{2,1,0:T(8,128)} %get-tuple-element.46.refs_1_, bf16[8,256,128]{2,1,0:T(8,128)(2,1)} %copy-done.4, bf16[8,640,128]{2,1,0:T(8,128)(2,1)} %get-tuple-element.48.refs_3_), custom_call_target="tpu_custom_call", output_to_operand_aliasing={{}: (3, {})} | custom-call | flops 1048576 | bytes 4194304 | tf_op jit(solution)/shard_map/pallas_call | solution.py:93
  85.7 6.7 %all-to-all-start.3 = ((bf16[8,640,128]{2,1,0:T(8,128)(2,1)}), bf16[8,640,128]{2,1,0:T(8,128)(2,1)S(1)}, u32[]{:S(2)}, u32[]{:S(2)}) async-start(bf16[8,640,128]{2,1,0:T(8,128)(2,1)} %shard_map.124), calls=%async_computation.3 | async-start | bytes 2621440 | tf_op jit(solution)/shard_map/all_to_all | solution.py:338
  92.4 4.8 %collective-permute-start.5 = (bf16[8,32,128]{2,1,0:T(8,128)(2,1)S(1)}, bf16[8,32,128]{2,1,0:T(8,128)(2,1)S(1)}, u32[]{:S(2)}, u32[]{:S(2)}) collective-permute-start(bf16[8,32,128]{2,1,0:T(8,128)(2,1)S(1)} %copy-done.8), channel_id=1, source_target_pairs={{0,0},{1,32},{2,64},{3,96},{4,128},{5,160},{6,192},{7,224},{8,1},{... | collective-permute-start | bytes 196616 | tf_op jit(solution)/shard_map/ppermute | solution.py:398
  97.2 4.1 %collective-permute-done.5 = bf16[8,32,128]{2,1,0:T(8,128)(2,1)S(1)} collective-permute-done((bf16[8,32,128]{2,1,0:T(8,128)(2,1)S(1)}, bf16[8,32,128]{2,1,0:T(8,128)(2,1)S(1)}, u32[]{:S(2)}, u32[]{:S(2)}) %collective-permute-start.5) | collective-permute-done | bytes 65568 | tf_op jit(solution)/shard_map/ppermute | solution.py:398
  101.3 24.6 %all-gather = bf16[64,32,128]{2,1,0:T(8,128)(2,1)} all-gather(bf16[8,32,128]{2,1,0:T(8,128)(2,1)S(1)} %collective-permute-done.5), channel_id=2, replica_groups=mesh['dp'=4,'z'=8,'x'=4,'c'=2] {'x','c'}, dimensions={0}, use_global_device_ids=true | all-gather | bytes 589824 | tf_op jit(solution)/shard_map/all_gather | solution.py:400
  125.9 2.5 %shard_map.127 = f32[4,1024]{1,0:T(4,128)} custom-call(s32[3]{0:T(128)} %pad_add_fusion.refs_1_.refs_0_, bf16[8,8,32,128]{3,2,1,0:T(8,128)(2,1)} %bitcast.18), custom_call_target="tpu_custom_call" | custom-call | flops 65536 | bytes 540684 | tf_op jit(solution)/shard_map/pallas_call | solution.py:93
  128.4 2.1 %shard_map.126 = (bf16[128,1024]{1,0:T(8,128)(2,1)}, bf16[128,1024]{1,0:T(8,128)(2,1)}, bf16[128,1024]{1,0:T(8,128)(2,1)}, bf16[128,1024]{1,0:T(8,128)(2,1)}, bf16[128,1024]{1,0:T(8,128)(2,1)}) custom-call(bf16[8,640,128]{2,1,0:T(8,128)(2,1)S(1)} %all-to-all-done.3.refs_0_, bf16[1024,1024]{1,0:T(8,128)(2,1)S(1)} %copy-done), custom_call_target="tpu_custom_call" | custom-call | flops 268435456 | bytes 4718592 | tf_op jit(solution)/shard_map/pallas_call | solution.py:93
  (30 shorter events, 0.5 us)
Async XLA Ops:
  7.2 52.1 %all-gather.3.cloned.1.call-start = ((), (), s32[]{:S(2)}) async-start(), calls=%async_computation.4 | async-start | bytes 2359296 | tf_op jit(solution)/shard_map/all_gather | solution.py:344
  7.9 7.3 %copy-start.9 = (s32[1,8192]{1,0:T(1,128)S(1)}, s32[1,8192]{1,0:T(1,128)}, u32[]{:S(2)}) copy-start(s32[1,8192]{1,0:T(1,128)} %param.12) | copy-start | bytes 98308
  10.0 16.3 %all-to-all-start = ((bf16[8,384,128]{2,1,0:T(8,128)(2,1)}), bf16[8,384,128]{2,1,0:T(8,128)(2,1)S(1)}, u32[]{:S(2)}, u32[]{:S(2)}) async-start(bf16[8,384,128]{2,1,0:T(8,128)(2,1)} %shard_map.118), calls=%async_computation | async-start | bytes 1572864 | tf_op jit(solution)/shard_map/all_to_all | solution.py:338
  26.4 9.8 %copy-start.1 = (bf16[8,384,128]{2,1,0:T(8,128)(2,1)}, bf16[8,384,128]{2,1,0:T(8,128)(2,1)S(1)}, u32[]{:S(2)}) copy-start(bf16[8,384,128]{2,1,0:T(8,128)(2,1)S(1)} %all-to-all-done.refs_1_.refs_6_) | copy-start | bytes 2359300
  26.4 18.1 %collective-permute-start = (bf16[8,256,128]{2,1,0:T(8,128)(2,1)S(1)}, bf16[8,256,128]{2,1,0:T(8,128)(2,1)S(1)}, u32[]{:S(2)}, u32[]{:S(2)}) collective-permute-start(bf16[8,256,128]{2,1,0:T(8,128)(2,1)S(1)} %slice.8), channel_id=1, source_target_pairs={{0,8},{8,16},{16,24},{24,32},{32,40},{40,48},{48,56},{1,9},{9,17},... | collective-permute-start | bytes 1572872 | tf_op jit(solution)/shard_map/ppermute | solution.py:368
  29.4 15.2 %all-to-all-start.1 = ((bf16[8,256,128]{2,1,0:T(8,128)(2,1)}), bf16[8,256,128]{2,1,0:T(8,128)(2,1)S(1)}, u32[]{:S(2)}, u32[]{:S(2)}) async-start(bf16[8,256,128]{2,1,0:T(8,128)(2,1)} %shard_map.119), calls=%async_computation.1 | async-start | bytes 1048576 | tf_op jit(solution)/shard_map/all_to_all | solution.py:338
  44.5 0.8 copy-start.2
  44.5 1.0 copy-start.3
  63.9 18.5 %collective-permute-start.1 = (bf16[8,256,128]{2,1,0:T(8,128)(2,1)}, bf16[8,256,128]{2,1,0:T(8,128)(2,1)S(1)}, u32[]{:S(2)}, u32[]{:S(2)}) collective-permute-start(bf16[8,256,128]{2,1,0:T(8,128)(2,1)} %get-tuple-element.47), channel_id=1, source_target_pairs={{8,0},{16,8},{24,16},{32,24},{40,32},{48,40},{56,48},{9,1},{17,9},... | collective-permute-start | bytes 1572872 | tf_op jit(solution)/shard_map/ppermute | solution.py:383
  68.8 11.1 %collective-permute-start.2 = (bf16[32,1024]{1,0:T(8,128)(2,1)}, bf16[32,1024]{1,0:T(8,128)(2,1)S(1)}, u32[]{:S(2)}, u32[]{:S(2)}) collective-permute-start(bf16[32,1024]{1,0:T(8,128)(2,1)} %get-tuple-element.50), channel_id=1, source_target_pairs={{0,64},{64,128},{128,192},{192,0},{1,65},{65,129},{129,193},{193,1... | collective-permute-start | bytes 196616 | tf_op jit(solution)/shard_map/ppermute | solution.py:384
  69.9 10.0 %collective-permute-start.3 = (bf16[32,1024]{1,0:T(8,128)(2,1)}, bf16[32,1024]{1,0:T(8,128)(2,1)S(1)}, u32[]{:S(2)}, u32[]{:S(2)}) collective-permute-start(bf16[32,1024]{1,0:T(8,128)(2,1)} %get-tuple-element.51), channel_id=1, source_target_pairs={{0,128},{64,192},{128,0},{192,64},{1,129},{65,193},{129,1},{193,65... | collective-permute-start | bytes 196616 | tf_op jit(solution)/shard_map/ppermute | solution.py:384
  71.1 8.8 %collective-permute-start.4 = (bf16[32,1024]{1,0:T(8,128)(2,1)}, bf16[32,1024]{1,0:T(8,128)(2,1)S(1)}, u32[]{:S(2)}, u32[]{:S(2)}) collective-permute-start(bf16[32,1024]{1,0:T(8,128)(2,1)} %get-tuple-element.52), channel_id=1, source_target_pairs={{0,192},{64,0},{128,64},{192,128},{1,193},{65,1},{129,65},{193,129... | collective-permute-start | bytes 196616 | tf_op jit(solution)/shard_map/ppermute | solution.py:384
  79.9 0.6 copy-start.5
  79.9 0.6 copy-start.6
  79.9 0.6 copy-start.7
  82.4 0.8 copy-start.4
  85.7 6.7 %copy-start.8 = (bf16[8,32,128]{2,1,0:T(8,128)(2,1)S(1)}, bf16[8,32,128]{2,1,0:T(8,128)(2,1)}, u32[]{:S(2)}) copy-start(bf16[8,32,128]{2,1,0:T(8,128)(2,1)} %shard_map.125) | copy-start | bytes 196612
  85.7 42.7 %copy-start = (bf16[1024,1024]{1,0:T(8,128)(2,1)S(1)}, bf16[1024,1024]{1,0:T(8,128)(2,1)}, u32[]{:S(2)}) copy-start(bf16[1024,1024]{1,0:T(8,128)(2,1)} %refs_1_.1) | copy-start | bytes 6291460
  85.7 42.7 %all-to-all-start.3 = ((bf16[8,640,128]{2,1,0:T(8,128)(2,1)}), bf16[8,640,128]{2,1,0:T(8,128)(2,1)S(1)}, u32[]{:S(2)}, u32[]{:S(2)}) async-start(bf16[8,640,128]{2,1,0:T(8,128)(2,1)} %shard_map.124), calls=%async_computation.3 | async-start | bytes 2621440 | tf_op jit(solution)/shard_map/all_to_all | solution.py:338
  92.4 8.9 %collective-permute-start.5 = (bf16[8,32,128]{2,1,0:T(8,128)(2,1)S(1)}, bf16[8,32,128]{2,1,0:T(8,128)(2,1)S(1)}, u32[]{:S(2)}, u32[]{:S(2)}) collective-permute-start(bf16[8,32,128]{2,1,0:T(8,128)(2,1)S(1)} %copy-done.8), channel_id=1, source_target_pairs={{0,0},{1,32},{2,64},{3,96},{4,128},{5,160},{6,192},{7,224},{8,1},{... | collective-permute-start | bytes 196616 | tf_op jit(solution)/shard_map/ppermute | solution.py:398
Sparse Core Ops, SparseCore 0:
  9.9 28.1 all-gather.2

commit v8 on v7

--- a/solution.py
+++ b/solution.py
@@ -323,12 +323,11 @@
     out.send()
 
 
-def weight_body(who_ref, recv, wg):
+def weight_body(recv, wg):
     recv_ref = recv.get()
-    rank = who_ref[2]
-    share = recv_ref[0, rank].astype(F32)
+    share = recv_ref[0].astype(F32)
     for n in range(1, HEADS):
-        share = share + recv_ref[n, rank].astype(F32)
+        share = share + recv_ref[n].astype(F32)
     for b in range(8):
         wg.ref[:, 128 * b : 128 * b + 128] = share[4 * b : 4 * b + 4, :]
     wg.send()
@@ -354,7 +353,7 @@
     recv = plane_exchange(packed)
 
     replica, plane = lax.axis_index("dp"), lax.axis_index("z")
-    who = jnp.stack([replica, plane, lax.axis_index(PLANE_AXES)]).astype(jnp.int32)
+    who = jnp.stack([replica, plane]).astype(jnp.int32)
     place = plane * PLANE
     users = jnp.arange(USERS, dtype=jnp.int32)[:, None]
     first = jnp.sum((seg[None, :] < users).astype(jnp.int32), axis=1)
@@ -397,9 +396,10 @@
     sent, moved = lax.optimization_barrier((sent, moved))
     moved = lax.ppermute(moved, ("dp", "z", "x", "c"), route)
     got = plane_exchange(sent)
-    shares = lax.all_gather(moved, PLANE_AXES)
+    moved, got = lax.optimization_barrier((moved, got))
+    shares = plane_exchange(moved)
     out, dq, dk, dv, gg = call(final_body, "hh", [rows] * 5, 1 << 28, (), ROOM)(got, w_out)
-    (weight_grad,) = call(weight_body, "sh", [share], 1 << 16)(who, shares)
+    (weight_grad,) = call(weight_body, "h", [share], 1 << 16, (), ROOM)(shares)
     return out[None], dq[None], dk[None], dv[None], gg[None], weight_grad
 
 

time: 140 us -> 133 us (0.950)
  the two profiles are of different devices: /device:TPU:203 before, /device:TPU:128 now
where the time goes in v8:
time: 133 us; the launch traced here: 131 us
  waiting for transfers between devices  35.7 us (27%)
  Pallas kernels  33.5 us (25%)
  starting transfers between devices  32.6 us (25%)
  between operations  14.3 us (11%)
  blocking collectives  10.1 us (8%)
  local copies, waits for them, and re-layouts  2.6 us (2%)
  other arithmetic  2.13 us (2%)
    pallas_call x10, Pallas kernels, build(): pl.pallas_call(whole, out_shape=outs, in_specs=[pl.BlockSpec(memory_space...  33.5 us
    all_to_all x4, waiting for transfers between devices, plane_exchange(): return lax.all_to_all(blocks, PLANE_AXES, 0, 0, tiled=True)  27.3 us
    all_to_all x4, starting transfers between devices, plane_exchange(): return lax.all_to_all(blocks, PLANE_AXES, 0, 0, tiled=True)  14.9 us
    all_to_all x1, blocking collectives, plane_exchange(): return lax.all_to_all(blocks, PLANE_AXES, 0, 0, tiled=True)  10.1 us
    ppermute x1, starting transfers between devices, shards(): back = lax.ppermute(back, 'z', [(i, i - 1) for i in range(1, planes)])  8.32 us
    ppermute x1, waiting for transfers between devices, shards(): moved = lax.ppermute(moved, ('dp', 'z', 'x', 'c'), route)  7.68 us
    ppermute x3, starting transfers between devices, shards(): lax.ppermute(x, 'dp', [(i, (i + n + 1) % dp) for i in range(dp)])  4.42 us
    ppermute x1, starting transfers between devices, shards(): halo = lax.ppermute(pair, 'z', [(i, i + 1) for i in range(planes - 1)])  3.05 us
  transfers between devices with their start and end apart: 11, of which 5 were waited for; matrix products, arithmetic and copies ran while one was open for 2% of the time, Pallas kernels for 20%

profile of v8, /device:TPU:128, one launch (start us, length us, event | category | flops | bytes accessed | tf_op | source)
XLA Modules:
  0.0 130.9 jit_solution(10294995707929185062)
XLA Ops:
  7.2 0.7 all-gather.2.cloned.1.call-update
  7.9 2.1 %shard_map.118 = bf16[8,384,128]{2,1,0:T(8,128)(2,1)} custom-call(bf16[128,1024]{1,0:T(8,128)(2,1)} %bitcast.18, bf16[128,1024]{1,0:T(8,128)(2,1)} %bitcast.19, bf16[128,1024]{1,0:T(8,128)(2,1)} %bitcast.20), custom_call_target="tpu_custom_call" | custom-call | flops 65536 | bytes 1572864 | tf_op jit(solution)/shard_map/pallas_call | solution.py:93
  10.0 4.3 %all-to-all-start = ((bf16[8,384,128]{2,1,0:T(8,128)(2,1)}), bf16[8,384,128]{2,1,0:T(8,128)(2,1)S(1)}, u32[]{:S(2)}, u32[]{:S(2)}) async-start(bf16[8,384,128]{2,1,0:T(8,128)(2,1)} %shard_map.118), calls=%async_computation | async-start | bytes 1572864 | tf_op jit(solution)/shard_map/all_to_all | solution.py:337
  14.7 3.5 %shard_map.119 = bf16[8,256,128]{2,1,0:T(8,128)(2,1)} custom-call(bf16[128,1024]{1,0:T(8,128)(2,1)} %bitcast.16, bf16[128,1024]{1,0:T(8,128)(2,1)} %bitcast.17, bf16[1024,1024]{1,0:T(8,128)(2,1)} %refs_1_.1), custom_call_target="tpu_custom_call" | custom-call | flops 268435456 | bytes 3145728 | tf_op jit(solution)/shard_map/pallas_call | solution.py:93
  18.2 0.7 pad_add_fusion.refs_1_
  18.9 0.6 and_select_fusion.refs_0_
  19.4 0.6 fusion.refs_2_.refs_7_
  20.0 7.4 %all-to-all-done.refs_1_.refs_6_ = bf16[8,384,128]{2,1,0:T(8,128)(2,1)S(1)} async-done(((bf16[8,384,128]{2,1,0:T(8,128)(2,1)}), bf16[8,384,128]{2,1,0:T(8,128)(2,1)S(1)}, u32[]{:S(2)}, u32[]{:S(2)}) %all-to-all-start) | async-done | bytes 786464 | tf_op jit(solution)/shard_map/all_to_all | solution.py:337
  27.5 3.0 %collective-permute-start = (bf16[8,256,128]{2,1,0:T(8,128)(2,1)S(1)}, bf16[8,256,128]{2,1,0:T(8,128)(2,1)S(1)}, u32[]{:S(2)}, u32[]{:S(2)}) collective-permute-start(bf16[8,256,128]{2,1,0:T(8,128)(2,1)S(1)} %slice.8), channel_id=1, source_target_pairs={{0,8},{8,16},{16,24},{24,32},{32,40},{40,48},{48,56},{1,9},{9,17},... | collective-permute-start | bytes 1572872 | tf_op jit(solution)/shard_map/ppermute | solution.py:367
  30.6 3.5 %all-to-all-start.1 = ((bf16[8,256,128]{2,1,0:T(8,128)(2,1)}), bf16[8,256,128]{2,1,0:T(8,128)(2,1)S(1)}, u32[]{:S(2)}, u32[]{:S(2)}) async-start(bf16[8,256,128]{2,1,0:T(8,128)(2,1)} %shard_map.119), calls=%async_computation.1 | async-start | bytes 1048576 | tf_op jit(solution)/shard_map/all_to_all | solution.py:337
  34.1 5.7 %shard_map.120 = (f32[4,128,256]{2,1,0:T(8,128)}, bf16[4,128,256]{2,1,0:T(8,128)(2,1)}) custom-call(s32[4]{0:T(128)} %and_select_fusion.refs_0_, bf16[8,384,128]{2,1,0:T(8,128)(2,1)} %copy-done.1, s32[8,128]{1,0:T(8,128)} %fusion.refs_2_.refs_7_), custom_call_target="tpu_custom_call" | custom-call | flops 536870912 | bytes 1576976 | tf_op jit(solution)/shard_map/pallas_call | solution.py:93
  39.7 4.6 %all-to-all-done.1.refs_5_.refs_3_ = bf16[8,256,128]{2,1,0:T(8,128)(2,1)S(1)} async-done(((bf16[8,256,128]{2,1,0:T(8,128)(2,1)}), bf16[8,256,128]{2,1,0:T(8,128)(2,1)S(1)}, u32[]{:S(2)}, u32[]{:S(2)}) %all-to-all-start.1) | async-done | bytes 524320 | tf_op jit(solution)/shard_map/all_to_all | solution.py:337
  44.3 0.8 copy-done.2
  45.3 3.6 %shard_map.121 = (f32[4,128,256]{2,1,0:T(8,128)}, f32[8,32,128]{2,1,0:T(8,128)}) custom-call(s32[4]{0:T(128)} %and_select_fusion.refs_0_, bf16[8,256,128]{2,1,0:T(8,128)(2,1)} %copy-done.3, s32[8,128]{1,0:T(8,128)} %fusion.refs_2_.refs_7_, bf16[4,128,256]{2,1,0:T(8,128)(2,1)} %get-tuple-element.37.refs_3_.refs_8_, f32[4,128,256]{2,1,0:T(8,128)} %get-tuple-element.40.refs_4_, ...), custom_call_target="tpu_custom_call" | custom-call | flops 268435456 | bytes 2494480 | tf_op jit(solution)/shard_map/pallas_call | solution.py:93
  49.0 10.1 %all_to_all.25.refs_4_ = f32[8,32,128]{2,1,0:T(8,128)} all-to-all(f32[8,32,128]{2,1,0:T(8,128)} %get-tuple-element.43), channel_id=1, replica_groups=mesh['dp'=4,'z'=8,'x'=4,'c'=2] {'x','c'}, dimensions={0} | all-to-all | bytes 262144 | tf_op jit(solution)/shard_map/all_to_all | solution.py:337
  59.1 4.6 %shard_map.122 = (bf16[8,640,128]{2,1,0:T(8,128)(2,1)}, bf16[4,128,256]{2,1,0:T(8,128)(2,1)}, f32[4,128,256]{2,1,0:T(8,128)}, bf16[8,256,128]{2,1,0:T(8,128)(2,1...) custom-call(s32[4]{0:T(128)} %and_select_fusion.refs_0_, ...), custom_call_target="tpu_custom_call" | custom-call | flops 536870912 | bytes 7802904 | tf_op jit(solution)/shard_map/pallas_call | solution.py:93
  63.8 8.3 %collective-permute-start.1 = (bf16[8,256,128]{2,1,0:T(8,128)(2,1)}, bf16[8,256,128]{2,1,0:T(8,128)(2,1)S(1)}, u32[]{:S(2)}, u32[]{:S(2)}) collective-permute-start(bf16[8,256,128]{2,1,0:T(8,128)(2,1)} %get-tuple-element.49), channel_id=1, source_target_pairs={{8,0},{16,8},{24,16},{32,24},{40,32},{48,40},{56,48},{9,1},{17,9},... | collective-permute-start | bytes 1572872 | tf_op jit(solution)/shard_map/ppermute | solution.py:382
  72.1 1.7 %collective-permute-start.2 = (bf16[32,1024]{1,0:T(8,128)(2,1)}, bf16[32,1024]{1,0:T(8,128)(2,1)S(1)}, u32[]{:S(2)}, u32[]{:S(2)}) collective-permute-start(bf16[32,1024]{1,0:T(8,128)(2,1)} %get-tuple-element.52), channel_id=1, source_target_pairs={{0,64},{64,128},{128,192},{192,0},{1,65},{65,129},{129,193},{193,1... | collective-permute-start | bytes 196616 | tf_op jit(solution)/shard_map/ppermute | solution.py:383
  73.7 2.8 %collective-permute-start.4 = (bf16[32,1024]{1,0:T(8,128)(2,1)}, bf16[32,1024]{1,0:T(8,128)(2,1)S(1)}, u32[]{:S(2)}, u32[]{:S(2)}) collective-permute-start(bf16[32,1024]{1,0:T(8,128)(2,1)} %get-tuple-element.54), channel_id=1, source_target_pairs={{0,192},{64,0},{128,64},{192,128},{1,193},{65,1},{129,65},{193,129... | collective-permute-start | bytes 196616 | tf_op jit(solution)/shard_map/ppermute | solution.py:383
  76.5 6.8 %shard_map.123 = (bf16[8,640,128]{2,1,0:T(8,128)(2,1)}, f32[4,256,128]{2,1,0:T(8,128)}, f32[4,256,128]{2,1,0:T(8,128)}) custom-call(s32[4]{0:T(128)} %and_select_fusion.refs_0_, bf16[8,384,128]{2,1,0:T(8,128)(2,1)} %copy-done.1, s32[8,128]{1,0:T(8,128)} %fusion.refs_2_.refs_7_, ...), custom_call_target="tpu_custom_call", output_to_operand_aliasing={{0}: (6, {})} | custom-call | flops 1073741824 | bytes 5509136 | tf_op jit(solution)/shard_map/pallas_call | solution.py:93
  83.3 0.6 copy-done.5
  84.0 1.8 %shard_map.125 = bf16[8,32,128]{2,1,0:T(8,128)(2,1)} custom-call(f32[32,1024]{1,0:T(8,128)} %get-tuple-element.51.refs_0_, bf16[32,1024]{1,0:T(8,128)(2,1)} %copy-done.5, bf16[32,1024]{1,0:T(8,128)(2,1)} %copy-done.6, bf16[32,1024]{1,0:T(8,128)(2,1)} %copy-done.7), custom_call_target="tpu_custom_call" | custom-call | flops 65536 | bytes 393216 | tf_op jit(solution)/shard_map/pallas_call | solution.py:93
  85.8 0.8 copy-done.4
  86.6 2.5 %shard_map.124 = bf16[8,640,128]{2,1,0:T(8,128)(2,1)} custom-call(f32[4,256,128]{2,1,0:T(8,128)} %get-tuple-element.47.refs_0_, f32[4,256,128]{2,1,0:T(8,128)} %get-tuple-element.48.refs_1_, bf16[8,256,128]{2,1,0:T(8,128)(2,1)} %copy-done.4, bf16[8,640,128]{2,1,0:T(8,128)(2,1)} %get-tuple-element.50.refs_3_), custom_call_target="tpu_custom_call", output_to_operand_aliasing={{}: (3, {})} | custom-call | flops 1048576 | bytes 4194304 | tf_op jit(solution)/shard_map/pallas_call | solution.py:93
  89.1 3.7 %all-to-all-start.3 = ((bf16[8,640,128]{2,1,0:T(8,128)(2,1)}), bf16[8,640,128]{2,1,0:T(8,128)(2,1)S(1)}, u32[]{:S(2)}, u32[]{:S(2)}) async-start(bf16[8,640,128]{2,1,0:T(8,128)(2,1)} %shard_map.124), calls=%async_computation.3 | async-start | bytes 2621440 | tf_op jit(solution)/shard_map/all_to_all | solution.py:337
  92.9 1.9 %collective-permute-start.5 = (bf16[8,32,128]{2,1,0:T(8,128)(2,1)S(1)}, bf16[8,32,128]{2,1,0:T(8,128)(2,1)}, u32[]{:S(2)}, u32[]{:S(2)}) collective-permute-start(bf16[8,32,128]{2,1,0:T(8,128)(2,1)S(1)} %copy-done.8), channel_id=1, source_target_pairs={{0,0},{1,32},{2,64},{3,96},{4,128},{5,160},{6,192},{7,224},{8,1},{... | collective-permute-start | bytes 196616 | tf_op jit(solution)/shard_map/ppermute | solution.py:397
  94.8 7.7 %collective-permute-done.5 = bf16[8,32,128]{2,1,0:T(8,128)(2,1)} collective-permute-done((bf16[8,32,128]{2,1,0:T(8,128)(2,1)S(1)}, bf16[8,32,128]{2,1,0:T(8,128)(2,1)}, u32[]{:S(2)}, u32[]{:S(2)}) %collective-permute-start.5) | collective-permute-done | bytes 65568 | tf_op jit(solution)/shard_map/ppermute | solution.py:397
  102.5 11.9 %all-to-all-done.3.refs_0_ = bf16[8,640,128]{2,1,0:T(8,128)(2,1)S(1)} async-done(((bf16[8,640,128]{2,1,0:T(8,128)(2,1)}), bf16[8,640,128]{2,1,0:T(8,128)(2,1)S(1)}, u32[]{:S(2)}, u32[]{:S(2)}) %all-to-all-start.3) | async-done | bytes 1310752 | tf_op jit(solution)/shard_map/all_to_all | solution.py:337
  114.3 3.3 %all-to-all-start.4 = ((bf16[8,32,128]{2,1,0:T(8,128)(2,1)}), bf16[8,32,128]{2,1,0:T(8,128)(2,1)S(1)}, u32[]{:S(2)}, u32[]{:S(2)}) async-start(bf16[8,32,128]{2,1,0:T(8,128)(2,1)} %collective-permute-done.5), calls=%async_computation.4 | async-start | bytes 131072 | tf_op jit(solution)/shard_map/all_to_all | solution.py:337
  117.7 2.1 %shard_map.126 = (bf16[128,1024]{1,0:T(8,128)(2,1)}, bf16[128,1024]{1,0:T(8,128)(2,1)}, bf16[128,1024]{1,0:T(8,128)(2,1)}, bf16[128,1024]{1,0:T(8,128)(2,1)}, bf16[128,1024]{1,0:T(8,128)(2,1)}) custom-call(bf16[8,640,128]{2,1,0:T(8,128)(2,1)S(1)} %all-to-all-done.3.refs_0_, bf16[1024,1024]{1,0:T(8,128)(2,1)S(1)} %copy-done), custom_call_target="tpu_custom_call" | custom-call | flops 268435456 | bytes 4718592 | tf_op jit(solution)/shard_map/pallas_call | solution.py:93
  119.8 3.4 %all-to-all-done.4.refs_0_ = bf16[8,32,128]{2,1,0:T(8,128)(2,1)S(1)} async-done(((bf16[8,32,128]{2,1,0:T(8,128)(2,1)}), bf16[8,32,128]{2,1,0:T(8,128)(2,1)S(1)}, u32[]{:S(2)}, u32[]{:S(2)}) %all-to-all-start.4) | async-done | bytes 65568 | tf_op jit(solution)/shard_map/all_to_all | solution.py:337
  123.2 0.8 shard_map.127
  (31 shorter events, 0.8 us)
Async XLA Ops:
  7.2 51.9 %all-gather.2.cloned.1.call-start = ((), (), s32[]{:S(2)}) async-start(), calls=%async_computation.5 | async-start | bytes 2359296 | tf_op jit(solution)/shard_map/all_gather | solution.py:343
  7.9 6.4 %copy-start.9 = (s32[1,8192]{1,0:T(1,128)S(1)}, s32[1,8192]{1,0:T(1,128)}, u32[]{:S(2)}) copy-start(s32[1,8192]{1,0:T(1,128)} %param.12) | copy-start | bytes 98308
  10.0 17.5 %all-to-all-start = ((bf16[8,384,128]{2,1,0:T(8,128)(2,1)}), bf16[8,384,128]{2,1,0:T(8,128)(2,1)S(1)}, u32[]{:S(2)}, u32[]{:S(2)}) async-start(bf16[8,384,128]{2,1,0:T(8,128)(2,1)} %shard_map.118), calls=%async_computation | async-start | bytes 1572864 | tf_op jit(solution)/shard_map/all_to_all | solution.py:337
  27.5 6.6 %copy-start.1 = (bf16[8,384,128]{2,1,0:T(8,128)(2,1)}, bf16[8,384,128]{2,1,0:T(8,128)(2,1)S(1)}, u32[]{:S(2)}) copy-start(bf16[8,384,128]{2,1,0:T(8,128)(2,1)S(1)} %all-to-all-done.refs_1_.refs_6_) | copy-start | bytes 2359300
  27.5 16.8 %collective-permute-start = (bf16[8,256,128]{2,1,0:T(8,128)(2,1)S(1)}, bf16[8,256,128]{2,1,0:T(8,128)(2,1)S(1)}, u32[]{:S(2)}, u32[]{:S(2)}) collective-permute-start(bf16[8,256,128]{2,1,0:T(8,128)(2,1)S(1)} %slice.8), channel_id=1, source_target_pairs={{0,8},{8,16},{16,24},{24,32},{32,40},{40,48},{48,56},{1,9},{9,17},... | collective-permute-start | bytes 1572872 | tf_op jit(solution)/shard_map/ppermute | solution.py:367
  30.6 13.8 %all-to-all-start.1 = ((bf16[8,256,128]{2,1,0:T(8,128)(2,1)}), bf16[8,256,128]{2,1,0:T(8,128)(2,1)S(1)}, u32[]{:S(2)}, u32[]{:S(2)}) async-start(bf16[8,256,128]{2,1,0:T(8,128)(2,1)} %shard_map.119), calls=%async_computation.1 | async-start | bytes 1048576 | tf_op jit(solution)/shard_map/all_to_all | solution.py:337
  44.3 0.8 copy-start.2
  44.3 1.0 copy-start.3
  63.8 22.0 %collective-permute-start.1 = (bf16[8,256,128]{2,1,0:T(8,128)(2,1)}, bf16[8,256,128]{2,1,0:T(8,128)(2,1)S(1)}, u32[]{:S(2)}, u32[]{:S(2)}) collective-permute-start(bf16[8,256,128]{2,1,0:T(8,128)(2,1)} %get-tuple-element.49), channel_id=1, source_target_pairs={{8,0},{16,8},{24,16},{32,24},{40,32},{48,40},{56,48},{9,1},{17,9},... | collective-permute-start | bytes 1572872 | tf_op jit(solution)/shard_map/ppermute | solution.py:382
  72.1 11.2 %collective-permute-start.2 = (bf16[32,1024]{1,0:T(8,128)(2,1)}, bf16[32,1024]{1,0:T(8,128)(2,1)S(1)}, u32[]{:S(2)}, u32[]{:S(2)}) collective-permute-start(bf16[32,1024]{1,0:T(8,128)(2,1)} %get-tuple-element.52), channel_id=1, source_target_pairs={{0,64},{64,128},{128,192},{192,0},{1,65},{65,129},{129,193},{193,1... | collective-permute-start | bytes 196616 | tf_op jit(solution)/shard_map/ppermute | solution.py:383
  73.7 9.6 %collective-permute-start.3 = (bf16[32,1024]{1,0:T(8,128)(2,1)}, bf16[32,1024]{1,0:T(8,128)(2,1)S(1)}, u32[]{:S(2)}, u32[]{:S(2)}) collective-permute-start(bf16[32,1024]{1,0:T(8,128)(2,1)} %get-tuple-element.53), channel_id=1, source_target_pairs={{0,128},{64,192},{128,0},{192,64},{1,129},{65,193},{129,1},{193,65... | collective-permute-start | bytes 196616 | tf_op jit(solution)/shard_map/ppermute | solution.py:383
  73.7 9.6 %collective-permute-start.4 = (bf16[32,1024]{1,0:T(8,128)(2,1)}, bf16[32,1024]{1,0:T(8,128)(2,1)S(1)}, u32[]{:S(2)}, u32[]{:S(2)}) collective-permute-start(bf16[32,1024]{1,0:T(8,128)(2,1)} %get-tuple-element.54), channel_id=1, source_target_pairs={{0,192},{64,0},{128,64},{192,128},{1,193},{65,1},{129,65},{193,129... | collective-permute-start | bytes 196616 | tf_op jit(solution)/shard_map/ppermute | solution.py:383
  83.3 0.6 copy-start.5
  83.3 0.6 copy-start.6
  83.3 0.6 copy-start.7
  85.8 0.8 copy-start.4
  89.1 3.7 %copy-start.8 = (bf16[8,32,128]{2,1,0:T(8,128)(2,1)S(1)}, bf16[8,32,128]{2,1,0:T(8,128)(2,1)}, u32[]{:S(2)}) copy-start(bf16[8,32,128]{2,1,0:T(8,128)(2,1)} %shard_map.125) | copy-start | bytes 196612
  89.1 28.6 %copy-start = (bf16[1024,1024]{1,0:T(8,128)(2,1)S(1)}, bf16[1024,1024]{1,0:T(8,128)(2,1)}, u32[]{:S(2)}) copy-start(bf16[1024,1024]{1,0:T(8,128)(2,1)} %refs_1_.1) | copy-start | bytes 6291460
  89.1 25.2 %all-to-all-start.3 = ((bf16[8,640,128]{2,1,0:T(8,128)(2,1)}), bf16[8,640,128]{2,1,0:T(8,128)(2,1)S(1)}, u32[]{:S(2)}, u32[]{:S(2)}) async-start(bf16[8,640,128]{2,1,0:T(8,128)(2,1)} %shard_map.124), calls=%async_computation.3 | async-start | bytes 2621440 | tf_op jit(solution)/shard_map/all_to_all | solution.py:337
  92.9 9.6 %collective-permute-start.5 = (bf16[8,32,128]{2,1,0:T(8,128)(2,1)S(1)}, bf16[8,32,128]{2,1,0:T(8,128)(2,1)}, u32[]{:S(2)}, u32[]{:S(2)}) collective-permute-start(bf16[8,32,128]{2,1,0:T(8,128)(2,1)S(1)} %copy-done.8), channel_id=1, source_target_pairs={{0,0},{1,32},{2,64},{3,96},{4,128},{5,160},{6,192},{7,224},{8,1},{... | collective-permute-start | bytes 196616 | tf_op jit(solution)/shard_map/ppermute | solution.py:397
  114.3 8.9 %all-to-all-start.4 = ((bf16[8,32,128]{2,1,0:T(8,128)(2,1)}), bf16[8,32,128]{2,1,0:T(8,128)(2,1)S(1)}, u32[]{:S(2)}, u32[]{:S(2)}) async-start(bf16[8,32,128]{2,1,0:T(8,128)(2,1)} %collective-permute-done.5), calls=%async_computation.4 | async-start | bytes 131072 | tf_op jit(solution)/shard_map/all_to_all | solution.py:337
Sparse Core Ops, SparseCore 0:
  9.9 29.3 all-gather.1

commit v9 on v8

--- a/solution.py
+++ b/solution.py
@@ -236,7 +236,7 @@
 
 
 def middle_body(
-    low_ref, who_ref, mixt, gd, stats, halo, recv, start, qt, cot, sent, dmix, dqt, back, own, far1, far2, far3, kt_ref, dk_ref, dv_ref, all_ref
+    low_ref, who_ref, mixt, gd, stats, halo, recv, start, qt, near, mate, sent, dmix, dqt, back, own, far1, far2, far3, kt_ref, dk_ref, dv_ref, all_ref
 ):
     finish(mixt.get(), gd.get(), stats.get(), sent.ref, dmix.ref)
     sent.send((), (slice(None), slice(0, 256)))
@@ -255,10 +255,12 @@
         back.ref[2 * j : 2 * j + 2, 0:128, :] = dk_ref[j].astype(BF16).reshape(2, 128, 128)
         back.ref[2 * j : 2 * j + 2, 128:256, :] = dv_ref[j].astype(BF16).reshape(2, 128, 128)
     back.send()
-    cot_ref = cot.get()
-    total = dot(sent.ref[0, 0:128, :], cot_ref[0])
-    for b in range(1, HEADS):
-        total = total + dot(sent.ref[b, 0:128, :], cot_ref[b])
+    near_ref, mate_ref = near.get(), mate.get()
+    total = jnp.zeros((128, 1024), F32)
+    for n in range(4):
+        first = 2 * jnp.bitwise_and(who_ref[2] + n, 3)
+        total = total + dot(sent.ref[first + who_ref[3], 0:128, :], near_ref[n])
+        total = total + dot(sent.ref[first + 1 - who_ref[3], 0:128, :], mate_ref[n])
     all_ref[...] = total
     for n, made in enumerate((own, far1, far2, far3)):
         block = jnp.bitwise_and(who_ref[0] + n, 3)
@@ -340,7 +342,6 @@
 def shards(sizes, queries, keys, values, gates, cotangent, segment, w_out):
     dp, planes = sizes
     q, k, v, gate, cot, seg = (a[0] for a in (queries, keys, values, gates, cotangent, segment))
-    cot_plane = lax.all_gather(cot, PLANE_AXES)
     rows = shape((TOK, 1024), BF16)
     head = shape((TILES, 128, TILE), F32)
     head16 = shape((TILES, 128, TILE), BF16)
@@ -353,7 +354,7 @@
     recv = plane_exchange(packed)
 
     replica, plane = lax.axis_index("dp"), lax.axis_index("z")
-    who = jnp.stack([replica, plane]).astype(jnp.int32)
+    who = jnp.stack([replica, plane, lax.axis_index("x"), lax.axis_index("c")]).astype(jnp.int32)
     place = plane * PLANE
     users = jnp.arange(USERS, dtype=jnp.int32)[:, None]
     first = jnp.sum((seg[None, :] < users).astype(jnp.int32), axis=1)
@@ -363,22 +364,27 @@
     start = start.reshape(8, 128)
     (gd,) = call(dgated_body, "hhh", [shape((8, 256, 128), BF16)], 1 << 28)(cot, gate, w_out)
 
-    pair, gd, start, low, who = lax.optimization_barrier((recv[:, 128:384], gd, start, low, who))
+    along = [lax.ppermute(cot, "x", [(i, (i - n) % 4) for i in range(4)]) for n in (1, 2, 3)]
+    pair, gd, start, low, who, *along = lax.optimization_barrier((recv[:, 128:384], gd, start, low, who, *along))
     halo = lax.ppermute(pair, "z", [(i, i + 1) for i in range(planes - 1)])
     gd_recv = plane_exchange(gd)
+    near = jnp.stack([cot, *along])
     part, qt = call(fwd_own_body, "shh", [head, head16], 1 << 29, [vt])(low, recv, start)
+    halo, gd_recv, near, part = lax.optimization_barrier((halo, gd_recv, near, part))
+    mate = lax.ppermute(near, "c", [(0, 1), (1, 0)])
     mixt, stats = call(fwd_halo_body, "shhhhh", [head, shape((8, 32, 128), F32)], 1 << 28, [vt], TIGHT, kept={1: (1, 32, 128)})(
         low, halo, start, qt, part, gd_recv
     )
+    stats, near, mate = lax.optimization_barrier((stats, near, mate))
     stats = plane_exchange(stats)
 
     only_q = {6: ((slice(None), slice(0, 128)), (8, 128, 128))}
     far = shape((32, 1024), BF16)
     sent, dmix, dqt, back, own, *fars = call(
-        middle_body, "sshhhhhhhh",
+        middle_body, "sshhhhhhhhh",
         [shape((8, 640, 128), BF16), head16, head, shape((8, 256, 128), BF16), shape((32, 1024), F32), far, far, far],
         1 << 29, [vt, acc, acc, pltpu.VMEM((128, 1024), F32)], kept={0: (8, 256, 128)}, held=only_q,
-    )(low, who, mixt, gd_recv, stats, halo, recv, start, qt, cot_plane)
+    )(low, who, mixt, gd_recv, stats, halo, recv, start, qt, near, mate)
     back = lax.ppermute(back, "z", [(i, i - 1) for i in range(1, planes)])
     fars = [lax.ppermute(x, "dp", [(i, (i + n + 1) % dp) for i in range(dp)]) for n, x in enumerate(fars)]
     moved = shape((8, 32, 128), BF16)

time: 133 us -> 124 us (0.932)
  between operations: 14.3 us -> 1.16 us
  Pallas kernels: 33.5 us -> 38.7 us
  waiting for transfers between devices: 35.7 us -> 34.1 us
    ppermute x0 -> x4, starting transfers between devices: none -> 5.82 us  [the longest x3 5.73 us: shards(): lax.ppermute(cot, 'x', [(i, (i - n) % 4) for i in range(4)])]
    pallas_call x10, Pallas kernels: 33.5 us -> 38.7 us  [build(): pl.pallas_call(whole, out_shape=outs, in_specs=[pl.BlockSpec(memory_space...]
    ppermute x1, starting transfers between devices: 8.32 us -> 4.13 us  [shards(): back = lax.ppermute(back, 'z', [(i, i - 1) for i in range(1, planes)])]
  transfers between devices with their start and end apart: 11 -> 14, of which waited for: 5 -> 5; matrix products, arithmetic and copies ran while one was open for 2% -> 3% of each run, Pallas kernels for 20% -> 23%
where the time goes in v9:
time: 124 us; the launch traced here: 123 us
  Pallas kernels  38.7 us (31%)
  waiting for transfers between devices  34.1 us (28%)
  starting transfers between devices  32.8 us (26%)
  blocking collectives  10.1 us (8%)
  local copies, waits for them, and re-layouts  3.38 us (3%)
  other arithmetic  2.67 us (2%)
    pallas_call x10, Pallas kernels, build(): pl.pallas_call(whole, out_shape=outs, in_specs=[pl.BlockSpec(memory_space...  38.7 us
    all_to_all x4, waiting for transfers between devices, plane_exchange(): return lax.all_to_all(blocks, PLANE_AXES, 0, 0, tiled=True)  26.4 us
    all_to_all x4, starting transfers between devices, plane_exchange(): return lax.all_to_all(blocks, PLANE_AXES, 0, 0, tiled=True)  14.2 us
    all_to_all x1, blocking collectives, plane_exchange(): return lax.all_to_all(blocks, PLANE_AXES, 0, 0, tiled=True)  10.1 us
    ppermute x1, waiting for transfers between devices, shards(): moved = lax.ppermute(moved, ('dp', 'z', 'x', 'c'), route)  7.68 us
    ppermute x3, starting transfers between devices, shards(): lax.ppermute(cot, 'x', [(i, (i - n) % 4) for i in range(4)])  5.73 us
    ppermute x1, starting transfers between devices, shards(): back = lax.ppermute(back, 'z', [(i, i - 1) for i in range(1, planes)])  4.13 us
    ppermute x3, starting transfers between devices, shards(): lax.ppermute(x, 'dp', [(i, (i + n + 1) % dp) for i in range(dp)])  3.67 us
  transfers between devices with their start and end apart: 14, of which 5 were waited for; matrix products, arithmetic and copies ran while one was open for 3% of the time, Pallas kernels for 23%

profile of v9, /device:TPU:128, one launch (start us, length us, event | category | flops | bytes accessed | tf_op | source)
XLA Modules:
  0.0 123.0 jit_solution(5444266038924775347)
XLA Ops:
  0.6 1.6 %collective-permute-start.2 = (bf16[128,1024]{1,0:T(8,128)(2,1)}, bf16[128,1024]{1,0:T(8,128)(2,1)S(1)}, u32[]{:S(2)}, u32[]{:S(2)}) collective-permute-start(bf16[128,1024]{1,0:T(8,128)(2,1)} %bitcast.21), channel_id=1, source_target_pairs={{0,2},{2,4},{4,6},{6,0},{1,3},{3,5},{5,7},{7,1},{8,10},{10,12},{12... | collective-permute-start | bytes 786440 | tf_op jit(solution)/shard_map/ppermute | solution.py:367
  2.2 2.7 %collective-permute-start.1 = (bf16[128,1024]{1,0:T(8,128)(2,1)}, bf16[128,1024]{1,0:T(8,128)(2,1)S(1)}, u32[]{:S(2)}, u32[]{:S(2)}) collective-permute-start(bf16[128,1024]{1,0:T(8,128)(2,1)} %bitcast.22), channel_id=1, source_target_pairs={{0,4},{2,6},{4,0},{6,2},{1,5},{3,7},{5,1},{7,3},{8,12},{10,14},{12... | collective-permute-start | bytes 786440 | tf_op jit(solution)/shard_map/ppermute | solution.py:367
  4.9 1.4 %collective-permute-start = (bf16[128,1024]{1,0:T(8,128)(2,1)}, bf16[128,1024]{1,0:T(8,128)(2,1)S(1)}, u32[]{:S(2)}, u32[]{:S(2)}) collective-permute-start(bf16[128,1024]{1,0:T(8,128)(2,1)} %bitcast.23), channel_id=1, source_target_pairs={{0,6},{2,0},{4,2},{6,4},{1,7},{3,1},{5,3},{7,5},{8,14},{10,8},{12,... | collective-permute-start | bytes 786440 | tf_op jit(solution)/shard_map/ppermute | solution.py:367
  6.4 2.1 %shard_map.118 = bf16[8,384,128]{2,1,0:T(8,128)(2,1)} custom-call(bf16[128,1024]{1,0:T(8,128)(2,1)} %bitcast.26, bf16[128,1024]{1,0:T(8,128)(2,1)} %bitcast.27, bf16[128,1024]{1,0:T(8,128)(2,1)} %bitcast.28), custom_call_target="tpu_custom_call" | custom-call | flops 65536 | bytes 1572864 | tf_op jit(solution)/shard_map/pallas_call | solution.py:93
  8.5 3.6 %all-to-all-start = ((bf16[8,384,128]{2,1,0:T(8,128)(2,1)}), bf16[8,384,128]{2,1,0:T(8,128)(2,1)S(1)}, u32[]{:S(2)}, u32[]{:S(2)}) async-start(bf16[8,384,128]{2,1,0:T(8,128)(2,1)} %shard_map.118), calls=%async_computation | async-start | bytes 1572864 | tf_op jit(solution)/shard_map/all_to_all | solution.py:339
  13.1 3.5 %shard_map.119 = bf16[8,256,128]{2,1,0:T(8,128)(2,1)} custom-call(bf16[128,1024]{1,0:T(8,128)(2,1)} %bitcast.24, bf16[128,1024]{1,0:T(8,128)(2,1)} %bitcast.25, bf16[1024,1024]{1,0:T(8,128)(2,1)} %refs_1_.1), custom_call_target="tpu_custom_call" | custom-call | flops 268435456 | bytes 3145728 | tf_op jit(solution)/shard_map/pallas_call | solution.py:93
  17.1 8.1 %all-to-all-done.refs_1_.refs_6_ = bf16[8,384,128]{2,1,0:T(8,128)(2,1)S(1)} async-done(((bf16[8,384,128]{2,1,0:T(8,128)(2,1)}), bf16[8,384,128]{2,1,0:T(8,128)(2,1)S(1)}, u32[]{:S(2)}, u32[]{:S(2)}) %all-to-all-start) | async-done | bytes 786464 | tf_op jit(solution)/shard_map/all_to_all | solution.py:339
  25.2 0.9 slice.8
  26.2 3.1 %collective-permute-start.3 = (bf16[8,256,128]{2,1,0:T(8,128)(2,1)}, bf16[8,256,128]{2,1,0:T(8,128)(2,1)S(1)}, u32[]{:S(2)}, u32[]{:S(2)}) collective-permute-start(bf16[8,256,128]{2,1,0:T(8,128)(2,1)} %slice.8), channel_id=1, source_target_pairs={{0,8},{8,16},{16,24},{24,32},{32,40},{40,48},{48,56},{1,9},{9,17},... | collective-permute-start | bytes 1572872 | tf_op jit(solution)/shard_map/ppermute | solution.py:369
  29.2 3.6 %all-to-all-start.1 = ((bf16[8,256,128]{2,1,0:T(8,128)(2,1)}), bf16[8,256,128]{2,1,0:T(8,128)(2,1)S(1)}, u32[]{:S(2)}, u32[]{:S(2)}) async-start(bf16[8,256,128]{2,1,0:T(8,128)(2,1)} %shard_map.119), calls=%async_computation.1 | async-start | bytes 1048576 | tf_op jit(solution)/shard_map/all_to_all | solution.py:339
  32.8 6.1 %shard_map.120 = (f32[4,128,256]{2,1,0:T(8,128)}, bf16[4,128,256]{2,1,0:T(8,128)(2,1)}) custom-call(s32[4]{0:T(128)} %get-tuple-element.45.refs_0_, bf16[8,384,128]{2,1,0:T(8,128)(2,1)} %copy-done.1, s32[8,128]{1,0:T(8,128)} %fusion.refs_2_.refs_7_), custom_call_target="tpu_custom_call" | custom-call | flops 536870912 | bytes 1576976 | tf_op jit(solution)/shard_map/pallas_call | solution.py:93
  38.9 1.2 pad_maximum_fusion.refs_9_
  40.1 3.1 %all-to-all-done.1.refs_5_.refs_3_ = bf16[8,256,128]{2,1,0:T(8,128)(2,1)S(1)} async-done(((bf16[8,256,128]{2,1,0:T(8,128)(2,1)}), bf16[8,256,128]{2,1,0:T(8,128)(2,1)S(1)}, u32[]{:S(2)}, u32[]{:S(2)}) %all-to-all-start.1) | async-done | bytes 524320 | tf_op jit(solution)/shard_map/all_to_all | solution.py:339
  43.3 0.7 copy-done.2
  44.2 5.6 %shard_map.121 = (f32[4,128,256]{2,1,0:T(8,128)}, f32[8,32,128]{2,1,0:T(8,128)}) custom-call(s32[4]{0:T(128)} %get-tuple-element.45.refs_0_, bf16[8,256,128]{2,1,0:T(8,128)(2,1)} %copy-done.4, s32[8,128]{1,0:T(8,128)} %fusion.refs_2_.refs_7_, bf16[4,128,256]{2,1,0:T(8,128)(2,1)} %get-tuple-element.47.refs_3_.refs_8_, ...), custom_call_target="tpu_custom_call" | custom-call | flops 268435456 | bytes 2494480 | tf_op jit(solution)/shard_map/pallas_call | solution.py:93
  49.8 10.1 %all_to_all.25.refs_4_ = f32[8,32,128]{2,1,0:T(8,128)} all-to-all(f32[8,32,128]{2,1,0:T(8,128)} %get-tuple-element.61), channel_id=1, replica_groups=mesh['dp'=4,'z'=8,'x'=4,'c'=2] {'x','c'}, dimensions={0} | all-to-all | bytes 262144 | tf_op jit(solution)/shard_map/all_to_all | solution.py:339
  60.0 7.0 %shard_map.122 = (bf16[8,640,128]{2,1,0:T(8,128)(2,1)}, bf16[4,128,256]{2,1,0:T(8,128)(2,1)}, f32[4,128,256]{2,1,0:T(8,128)}, bf16[8,256,128]{2,1,0:T(8,128)(2,1...) custom-call(s32[4]{0:T(128)} %get-tuple-element.45.refs_0_, ...), custom_call_target="tpu_custom_call" | custom-call | flops 536870912 | bytes 7802912 | tf_op jit(solution)/shard_map/pallas_call | solution.py:93
  66.9 4.1 %collective-permute-start.5 = (bf16[8,256,128]{2,1,0:T(8,128)(2,1)}, bf16[8,256,128]{2,1,0:T(8,128)(2,1)S(1)}, u32[]{:S(2)}, u32[]{:S(2)}) collective-permute-start(bf16[8,256,128]{2,1,0:T(8,128)(2,1)} %get-tuple-element.69), channel_id=1, source_target_pairs={{8,0},{16,8},{24,16},{32,24},{40,32},{48,40},{56,48},{9,1},{17,9},... | collective-permute-start | bytes 1572872 | tf_op jit(solution)/shard_map/ppermute | solution.py:388
  71.2 1.1 collective-permute-start.7
  72.2 2.5 %collective-permute-start.8 = (bf16[32,1024]{1,0:T(8,128)(2,1)}, bf16[32,1024]{1,0:T(8,128)(2,1)S(1)}, u32[]{:S(2)}, u32[]{:S(2)}) collective-permute-start(bf16[32,1024]{1,0:T(8,128)(2,1)} %get-tuple-element.74), channel_id=1, source_target_pairs={{0,192},{64,0},{128,64},{192,128},{1,193},{65,1},{129,65},{193,129... | collective-permute-start | bytes 196616 | tf_op jit(solution)/shard_map/ppermute | solution.py:389
  74.8 7.3 %shard_map.123 = (bf16[8,640,128]{2,1,0:T(8,128)(2,1)}, f32[4,256,128]{2,1,0:T(8,128)}, f32[4,256,128]{2,1,0:T(8,128)}) custom-call(s32[4]{0:T(128)} %get-tuple-element.45.refs_0_, bf16[8,384,128]{2,1,0:T(8,128)(2,1)} %copy-done.1, s32[8,128]{1,0:T(8,128)} %fusion.refs_2_.refs_7_, ...), custom_call_target="tpu_custom_call", output_to_operand_aliasing={{0}: (6, {})} | custom-call | flops 1073741824 | bytes 5509136 | tf_op jit(solution)/shard_map/pallas_call | solution.py:93
  82.8 1.8 %shard_map.125 = bf16[8,32,128]{2,1,0:T(8,128)(2,1)} custom-call(f32[32,1024]{1,0:T(8,128)} %get-tuple-element.71.refs_0_, bf16[32,1024]{1,0:T(8,128)(2,1)} %copy-done.10, bf16[32,1024]{1,0:T(8,128)(2,1)} %copy-done.11, bf16[32,1024]{1,0:T(8,128)(2,1)} %copy-done.12), custom_call_target="tpu_custom_call" | custom-call | flops 65536 | bytes 393216 | tf_op jit(solution)/shard_map/pallas_call | solution.py:93
  84.6 0.8 copy-done.7
  85.4 2.4 %shard_map.124 = bf16[8,640,128]{2,1,0:T(8,128)(2,1)} custom-call(f32[4,256,128]{2,1,0:T(8,128)} %get-tuple-element.67.refs_0_, f32[4,256,128]{2,1,0:T(8,128)} %get-tuple-element.68.refs_1_, bf16[8,256,128]{2,1,0:T(8,128)(2,1)} %copy-done.7, bf16[8,640,128]{2,1,0:T(8,128)(2,1)} %get-tuple-element.70.refs_3_), custom_call_target="tpu_custom_call", output_to_operand_aliasing={{}: (3, {})} | custom-call | flops 1048576 | bytes 4194304 | tf_op jit(solution)/shard_map/pallas_call | solution.py:93
  87.9 3.7 %all-to-all-start.3 = ((bf16[8,640,128]{2,1,0:T(8,128)(2,1)}), bf16[8,640,128]{2,1,0:T(8,128)(2,1)S(1)}, u32[]{:S(2)}, u32[]{:S(2)}) async-start(bf16[8,640,128]{2,1,0:T(8,128)(2,1)} %shard_map.124), calls=%async_computation.3 | async-start | bytes 2621440 | tf_op jit(solution)/shard_map/all_to_all | solution.py:339
  91.6 1.9 %collective-permute-start.9 = (bf16[8,32,128]{2,1,0:T(8,128)(2,1)S(1)}, bf16[8,32,128]{2,1,0:T(8,128)(2,1)}, u32[]{:S(2)}, u32[]{:S(2)}) collective-permute-start(bf16[8,32,128]{2,1,0:T(8,128)(2,1)S(1)} %copy-done.13), channel_id=1, source_target_pairs={{0,0},{1,32},{2,64},{3,96},{4,128},{5,160},{6,192},{7,224},{8,1},{... | collective-permute-start | bytes 196616 | tf_op jit(solution)/shard_map/ppermute | solution.py:403
  93.5 7.7 %collective-permute-done.9 = bf16[8,32,128]{2,1,0:T(8,128)(2,1)} collective-permute-done((bf16[8,32,128]{2,1,0:T(8,128)(2,1)S(1)}, bf16[8,32,128]{2,1,0:T(8,128)(2,1)}, u32[]{:S(2)}, u32[]{:S(2)}) %collective-permute-start.9) | collective-permute-done | bytes 65568 | tf_op jit(solution)/shard_map/ppermute | solution.py:403
  101.2 11.9 %all-to-all-done.3.refs_0_ = bf16[8,640,128]{2,1,0:T(8,128)(2,1)S(1)} async-done(((bf16[8,640,128]{2,1,0:T(8,128)(2,1)}), bf16[8,640,128]{2,1,0:T(8,128)(2,1)S(1)}, u32[]{:S(2)}, u32[]{:S(2)}) %all-to-all-start.3) | async-done | bytes 1310752 | tf_op jit(solution)/shard_map/all_to_all | solution.py:339
  113.1 3.3 %all-to-all-start.4 = ((bf16[8,32,128]{2,1,0:T(8,128)(2,1)}), bf16[8,32,128]{2,1,0:T(8,128)(2,1)S(1)}, u32[]{:S(2)}, u32[]{:S(2)}) async-start(bf16[8,32,128]{2,1,0:T(8,128)(2,1)} %collective-permute-done.9), calls=%async_computation.4 | async-start | bytes 131072 | tf_op jit(solution)/shard_map/all_to_all | solution.py:339
  116.4 2.1 %shard_map.126 = (bf16[128,1024]{1,0:T(8,128)(2,1)}, bf16[128,1024]{1,0:T(8,128)(2,1)}, bf16[128,1024]{1,0:T(8,128)(2,1)}, bf16[128,1024]{1,0:T(8,128)(2,1)}, bf16[128,1024]{1,0:T(8,128)(2,1)}) custom-call(bf16[8,640,128]{2,1,0:T(8,128)(2,1)S(1)} %all-to-all-done.3.refs_0_, bf16[1024,1024]{1,0:T(8,128)(2,1)S(1)} %copy-done), custom_call_target="tpu_custom_call" | custom-call | flops 268435456 | bytes 4718592 | tf_op jit(solution)/shard_map/pallas_call | solution.py:93
  118.6 3.4 %all-to-all-done.4.refs_0_ = bf16[8,32,128]{2,1,0:T(8,128)(2,1)S(1)} async-done(((bf16[8,32,128]{2,1,0:T(8,128)(2,1)}), bf16[8,32,128]{2,1,0:T(8,128)(2,1)S(1)}, u32[]{:S(2)}, u32[]{:S(2)}) %all-to-all-start.4) | async-done | bytes 65568 | tf_op jit(solution)/shard_map/all_to_all | solution.py:339
  122.0 0.8 shard_map.127
  (46 shorter events, 2.7 us)
Async XLA Ops:
  0.6 25.5 %collective-permute-start.2 = (bf16[128,1024]{1,0:T(8,128)(2,1)}, bf16[128,1024]{1,0:T(8,128)(2,1)S(1)}, u32[]{:S(2)}, u32[]{:S(2)}) collective-permute-start(bf16[128,1024]{1,0:T(8,128)(2,1)} %bitcast.21), channel_id=1, source_target_pairs={{0,2},{2,4},{4,6},{6,0},{1,3},{3,5},{5,7},{7,1},{8,10},{10,12},{12... | collective-permute-start | bytes 786440 | tf_op jit(solution)/shard_map/ppermute | solution.py:367
  2.2 23.9 %collective-permute-start.1 = (bf16[128,1024]{1,0:T(8,128)(2,1)}, bf16[128,1024]{1,0:T(8,128)(2,1)S(1)}, u32[]{:S(2)}, u32[]{:S(2)}) collective-permute-start(bf16[128,1024]{1,0:T(8,128)(2,1)} %bitcast.22), channel_id=1, source_target_pairs={{0,4},{2,6},{4,0},{6,2},{1,5},{3,7},{5,1},{7,3},{8,12},{10,14},{12... | collective-permute-start | bytes 786440 | tf_op jit(solution)/shard_map/ppermute | solution.py:367
  4.9 21.2 %collective-permute-start = (bf16[128,1024]{1,0:T(8,128)(2,1)}, bf16[128,1024]{1,0:T(8,128)(2,1)S(1)}, u32[]{:S(2)}, u32[]{:S(2)}) collective-permute-start(bf16[128,1024]{1,0:T(8,128)(2,1)} %bitcast.23), channel_id=1, source_target_pairs={{0,6},{2,0},{4,2},{6,4},{1,7},{3,1},{5,3},{7,5},{8,14},{10,8},{12,... | collective-permute-start | bytes 786440 | tf_op jit(solution)/shard_map/ppermute | solution.py:367
  6.4 5.7 %copy-start.14 = (s32[1,8192]{1,0:T(1,128)S(1)}, s32[1,8192]{1,0:T(1,128)}, u32[]{:S(2)}) copy-start(s32[1,8192]{1,0:T(1,128)} %param.12) | copy-start | bytes 98308
  8.5 16.7 %all-to-all-start = ((bf16[8,384,128]{2,1,0:T(8,128)(2,1)}), bf16[8,384,128]{2,1,0:T(8,128)(2,1)S(1)}, u32[]{:S(2)}, u32[]{:S(2)}) async-start(bf16[8,384,128]{2,1,0:T(8,128)(2,1)} %shard_map.118), calls=%async_computation | async-start | bytes 1572864 | tf_op jit(solution)/shard_map/all_to_all | solution.py:339
  25.2 7.6 %copy-start.1 = (bf16[8,384,128]{2,1,0:T(8,128)(2,1)}, bf16[8,384,128]{2,1,0:T(8,128)(2,1)S(1)}, u32[]{:S(2)}) copy-start(bf16[8,384,128]{2,1,0:T(8,128)(2,1)S(1)} %all-to-all-done.refs_1_.refs_6_) | copy-start | bytes 2359300
  26.1 12.8 %copy-start.8 = (bf16[128,1024]{1,0:T(8,128)(2,1)}, bf16[128,1024]{1,0:T(8,128)(2,1)S(1)}, u32[]{:S(2)}) copy-start(bf16[128,1024]{1,0:T(8,128)(2,1)S(1)} %collective-permute-done.1) | copy-start | bytes 786436
  26.1 12.8 %copy-start.9 = (bf16[128,1024]{1,0:T(8,128)(2,1)}, bf16[128,1024]{1,0:T(8,128)(2,1)S(1)}, u32[]{:S(2)}) copy-start(bf16[128,1024]{1,0:T(8,128)(2,1)S(1)} %collective-permute-done) | copy-start | bytes 786436
  26.2 12.8 %copy-start.6 = (bf16[1,128,1024]{2,1,0:T(8,128)(2,1)S(1)}, bf16[1,128,1024]{2,1,0:T(8,128)(2,1)}, u32[]{:S(2)}) copy-start(bf16[1,128,1024]{2,1,0:T(8,128)(2,1)} %param.11) | copy-start | bytes 786436
  26.2 17.0 %collective-permute-start.3 = (bf16[8,256,128]{2,1,0:T(8,128)(2,1)}, bf16[8,256,128]{2,1,0:T(8,128)(2,1)S(1)}, u32[]{:S(2)}, u32[]{:S(2)}) collective-permute-start(bf16[8,256,128]{2,1,0:T(8,128)(2,1)} %slice.8), channel_id=1, source_target_pairs={{0,8},{8,16},{16,24},{24,32},{32,40},{40,48},{48,56},{1,9},{9,17},... | collective-permute-start | bytes 1572872 | tf_op jit(solution)/shard_map/ppermute | solution.py:369
  29.2 13.9 %all-to-all-start.1 = ((bf16[8,256,128]{2,1,0:T(8,128)(2,1)}), bf16[8,256,128]{2,1,0:T(8,128)(2,1)S(1)}, u32[]{:S(2)}, u32[]{:S(2)}) async-start(bf16[8,256,128]{2,1,0:T(8,128)(2,1)} %shard_map.119), calls=%async_computation.1 | async-start | bytes 1048576 | tf_op jit(solution)/shard_map/all_to_all | solution.py:339
  40.1 19.9 %copy-start.3 = (bf16[4,128,1024]{2,1,0:T(8,128)(2,1)}, bf16[4,128,1024]{2,1,0:T(8,128)(2,1)S(1)}, u32[]{:S(2)}) copy-start(bf16[4,128,1024]{2,1,0:T(8,128)(2,1)S(1)} %pad_maximum_fusion.refs_9_) | copy-start | bytes 3145732
  43.2 0.8 copy-start.2
  43.2 1.0 copy-start.4
  43.2 6.6 %collective-permute-start.4 = (bf16[4,128,1024]{2,1,0:T(8,128)(2,1)S(1)}, bf16[4,128,1024]{2,1,0:T(8,128)(2,1)S(1)}, u32[]{:S(2)}, u32[]{:S(2)}) collective-permute-start(bf16[4,128,1024]{2,1,0:T(8,128)(2,1)S(1)} %pad_maximum_fusion.refs_9_), channel_id=1, source_target_pairs={{0,1},{1,0},{2,3},{3,2},{4,5},{5,4},{6,7},{7,6},{8,9},{9,8},{10,11... | collective-permute-start | bytes 3145736 | tf_op jit(solution)/shard_map/ppermute | solution.py:374
  49.8 10.1 %copy-start.5 = (bf16[4,128,1024]{2,1,0:T(8,128)(2,1)}, bf16[4,128,1024]{2,1,0:T(8,128)(2,1)S(1)}, u32[]{:S(2)}) copy-start(bf16[4,128,1024]{2,1,0:T(8,128)(2,1)S(1)} %collective-permute-done.4.refs_10_) | copy-start | bytes 3145732
  66.9 17.7 %collective-permute-start.5 = (bf16[8,256,128]{2,1,0:T(8,128)(2,1)}, bf16[8,256,128]{2,1,0:T(8,128)(2,1)S(1)}, u32[]{:S(2)}, u32[]{:S(2)}) collective-permute-start(bf16[8,256,128]{2,1,0:T(8,128)(2,1)} %get-tuple-element.69), channel_id=1, source_target_pairs={{8,0},{16,8},{24,16},{32,24},{40,32},{48,40},{56,48},{9,1},{17,9},... | collective-permute-start | bytes 1572872 | tf_op jit(solution)/shard_map/ppermute | solution.py:388
  71.1 11.0 %collective-permute-start.6 = (bf16[32,1024]{1,0:T(8,128)(2,1)}, bf16[32,1024]{1,0:T(8,128)(2,1)S(1)}, u32[]{:S(2)}, u32[]{:S(2)}) collective-permute-start(bf16[32,1024]{1,0:T(8,128)(2,1)} %get-tuple-element.72), channel_id=1, source_target_pairs={{0,64},{64,128},{128,192},{192,0},{1,65},{65,129},{129,193},{193,1... | collective-permute-start | bytes 196616 | tf_op jit(solution)/shard_map/ppermute | solution.py:389
  71.2 10.9 %collective-permute-start.7 = (bf16[32,1024]{1,0:T(8,128)(2,1)}, bf16[32,1024]{1,0:T(8,128)(2,1)S(1)}, u32[]{:S(2)}, u32[]{:S(2)}) collective-permute-start(bf16[32,1024]{1,0:T(8,128)(2,1)} %get-tuple-element.73), channel_id=1, source_target_pairs={{0,128},{64,192},{128,0},{192,64},{1,129},{65,193},{129,1},{193,65... | collective-permute-start | bytes 196616 | tf_op jit(solution)/shard_map/ppermute | solution.py:389
  72.2 9.9 %collective-permute-start.8 = (bf16[32,1024]{1,0:T(8,128)(2,1)}, bf16[32,1024]{1,0:T(8,128)(2,1)S(1)}, u32[]{:S(2)}, u32[]{:S(2)}) collective-permute-start(bf16[32,1024]{1,0:T(8,128)(2,1)} %get-tuple-element.74), channel_id=1, source_target_pairs={{0,192},{64,0},{128,64},{192,128},{1,193},{65,1},{129,65},{193,129... | collective-permute-start | bytes 196616 | tf_op jit(solution)/shard_map/ppermute | solution.py:389
  82.1 0.6 copy-start.10
  82.1 0.6 copy-start.11
  82.1 0.6 copy-start.12
  84.6 0.8 copy-start.7
  87.8 3.7 %copy-start.13 = (bf16[8,32,128]{2,1,0:T(8,128)(2,1)S(1)}, bf16[8,32,128]{2,1,0:T(8,128)(2,1)}, u32[]{:S(2)}) copy-start(bf16[8,32,128]{2,1,0:T(8,128)(2,1)} %shard_map.125) | copy-start | bytes 196612
  87.8 28.6 %copy-start = (bf16[1024,1024]{1,0:T(8,128)(2,1)S(1)}, bf16[1024,1024]{1,0:T(8,128)(2,1)}, u32[]{:S(2)}) copy-start(bf16[1024,1024]{1,0:T(8,128)(2,1)} %refs_1_.1) | copy-start | bytes 6291460
  87.9 25.2 %all-to-all-start.3 = ((bf16[8,640,128]{2,1,0:T(8,128)(2,1)}), bf16[8,640,128]{2,1,0:T(8,128)(2,1)S(1)}, u32[]{:S(2)}, u32[]{:S(2)}) async-start(bf16[8,640,128]{2,1,0:T(8,128)(2,1)} %shard_map.124), calls=%async_computation.3 | async-start | bytes 2621440 | tf_op jit(solution)/shard_map/all_to_all | solution.py:339
  91.6 9.6 %collective-permute-start.9 = (bf16[8,32,128]{2,1,0:T(8,128)(2,1)S(1)}, bf16[8,32,128]{2,1,0:T(8,128)(2,1)}, u32[]{:S(2)}, u32[]{:S(2)}) collective-permute-start(bf16[8,32,128]{2,1,0:T(8,128)(2,1)S(1)} %copy-done.13), channel_id=1, source_target_pairs={{0,0},{1,32},{2,64},{3,96},{4,128},{5,160},{6,192},{7,224},{8,1},{... | collective-permute-start | bytes 196616 | tf_op jit(solution)/shard_map/ppermute | solution.py:403
  113.1 8.9 %all-to-all-start.4 = ((bf16[8,32,128]{2,1,0:T(8,128)(2,1)}), bf16[8,32,128]{2,1,0:T(8,128)(2,1)S(1)}, u32[]{:S(2)}, u32[]{:S(2)}) async-start(bf16[8,32,128]{2,1,0:T(8,128)(2,1)} %collective-permute-done.9), calls=%async_computation.4 | async-start | bytes 131072 | tf_op jit(solution)/shard_map/all_to_all | solution.py:339

commit v10 on v9

--- a/solution.py
+++ b/solution.py
@@ -364,7 +364,8 @@
     start = start.reshape(8, 128)
     (gd,) = call(dgated_body, "hhh", [shape((8, 256, 128), BF16)], 1 << 28)(cot, gate, w_out)
 
-    along = [lax.ppermute(cot, "x", [(i, (i - n) % 4) for i in range(4)]) for n in (1, 2, 3)]
+    low, cot_later = lax.optimization_barrier((low, cot))
+    along = [lax.ppermute(cot_later, "x", [(i, (i - n) % 4) for i in range(4)]) for n in (1, 2, 3)]
     pair, gd, start, low, who, *along = lax.optimization_barrier((recv[:, 128:384], gd, start, low, who, *along))
     halo = lax.ppermute(pair, "z", [(i, i + 1) for i in range(planes - 1)])
     gd_recv = plane_exchange(gd)

time: 124 us -> 130 us (1.048)
  starting transfers between devices: 32.8 us -> 38.9 us
  Pallas kernels: 38.7 us -> 34.3 us
  waiting for transfers between devices: 34.1 us -> 38.3 us
    ppermute x3, waiting for transfers between devices: 0.01 us -> 10.7 us  [shards(): lax.ppermute(cot_later, 'x', [(i, (i - n) % 4) for i in range(4)])]
    all_to_all x4, waiting for transfers between devices: 26.4 us -> 19.9 us  [plane_exchange(): return lax.all_to_all(blocks, PLANE_AXES, 0, 0, tiled=True)]
    ppermute x3, starting transfers between devices: 3.67 us -> 8.77 us  [shards(): lax.ppermute(x, 'dp', [(i, (i + n + 1) % dp) for i in range(dp)])]
    pallas_call x10, Pallas kernels: 38.7 us -> 34.3 us  [build(): pl.pallas_call(whole, out_shape=outs, in_specs=[pl.BlockSpec(memory_space...]
  transfers between devices with their start and end apart: 14 -> 14, of which waited for: 5 -> 7; matrix products, arithmetic and copies ran while one was open for 3% -> 3% of each run, Pallas kernels for 23% -> 19%
where the time goes in v10:
time: 130 us; the launch traced here: 129 us
  starting transfers between devices  38.9 us (30%)
  waiting for transfers between devices  38.3 us (29%)
  Pallas kernels  34.3 us (26%)
  blocking collectives  10.1 us (8%)
  other arithmetic  3.48 us (3%)
  local copies, waits for them, and re-layouts  2.48 us (2%)
    pallas_call x10, Pallas kernels, build(): pl.pallas_call(whole, out_shape=outs, in_specs=[pl.BlockSpec(memory_space...  34.3 us
    all_to_all x4, waiting for transfers between devices, plane_exchange(): return lax.all_to_all(blocks, PLANE_AXES, 0, 0, tiled=True)  19.9 us
    all_to_all x4, starting transfers between devices, plane_exchange(): return lax.all_to_all(blocks, PLANE_AXES, 0, 0, tiled=True)  14.9 us
    ppermute x3, waiting for transfers between devices, shards(): lax.ppermute(cot_later, 'x', [(i, (i - n) % 4) for i in range(4)])  10.7 us
    all_to_all x1, blocking collectives, plane_exchange(): return lax.all_to_all(blocks, PLANE_AXES, 0, 0, tiled=True)  10.1 us
    ppermute x3, starting transfers between devices, shards(): lax.ppermute(x, 'dp', [(i, (i + n + 1) % dp) for i in range(dp)])  8.77 us
    ppermute x1, waiting for transfers between devices, shards(): moved = lax.ppermute(moved, ('dp', 'z', 'x', 'c'), route)  7.68 us
    ppermute x3, starting transfers between devices, shards(): lax.ppermute(cot_later, 'x', [(i, (i - n) % 4) for i in range(4)])  6.15 us
  transfers between devices with their start and end apart: 14, of which 7 were waited for; matrix products, arithmetic and copies ran while one was open for 3% of the time, Pallas kernels for 19%

profile of v10, /device:TPU:128, one launch (start us, length us, event | category | flops | bytes accessed | tf_op | source)
XLA Modules:
  0.0 128.7 jit_solution(15183512815399791395)
XLA Ops:
  0.6 2.1 %shard_map.118 = bf16[8,384,128]{2,1,0:T(8,128)(2,1)} custom-call(bf16[128,1024]{1,0:T(8,128)(2,1)} %bitcast.22, bf16[128,1024]{1,0:T(8,128)(2,1)} %bitcast.23, bf16[128,1024]{1,0:T(8,128)(2,1)} %bitcast.24), custom_call_target="tpu_custom_call" | custom-call | flops 65536 | bytes 1572864 | tf_op jit(solution)/shard_map/pallas_call | solution.py:93
  2.7 4.3 %all-to-all-start = ((bf16[8,384,128]{2,1,0:T(8,128)(2,1)}), bf16[8,384,128]{2,1,0:T(8,128)(2,1)S(1)}, u32[]{:S(2)}, u32[]{:S(2)}) async-start(bf16[8,384,128]{2,1,0:T(8,128)(2,1)} %shard_map.118), calls=%async_computation | async-start | bytes 1572864 | tf_op jit(solution)/shard_map/all_to_all | solution.py:339
  8.1 2.0 %collective-permute-start.2 = (bf16[128,1024]{1,0:T(8,128)(2,1)}, bf16[128,1024]{1,0:T(8,128)(2,1)S(1)}, u32[]{:S(2)}, u32[]{:S(2)}) collective-permute-start(bf16[128,1024]{1,0:T(8,128)(2,1)} %bitcast.3.refs_0_), channel_id=1, source_target_pairs={{0,2},{2,4},{4,6},{6,0},{1,3},{3,5},{5,7},{7,1},{8,10},{10,12},{12... | collective-permute-start | bytes 786440 | tf_op jit(solution)/shard_map/ppermute | solution.py:368
  10.1 2.7 %collective-permute-start.1 = (bf16[128,1024]{1,0:T(8,128)(2,1)}, bf16[128,1024]{1,0:T(8,128)(2,1)S(1)}, u32[]{:S(2)}, u32[]{:S(2)}) collective-permute-start(bf16[128,1024]{1,0:T(8,128)(2,1)} %bitcast.3.refs_0_), channel_id=1, source_target_pairs={{0,4},{2,6},{4,0},{6,2},{1,5},{3,7},{5,1},{7,3},{8,12},{10,14},{12... | collective-permute-start | bytes 786440 | tf_op jit(solution)/shard_map/ppermute | solution.py:368
  12.8 1.5 %collective-permute-start = (bf16[128,1024]{1,0:T(8,128)(2,1)}, bf16[128,1024]{1,0:T(8,128)(2,1)S(1)}, u32[]{:S(2)}, u32[]{:S(2)}) collective-permute-start(bf16[128,1024]{1,0:T(8,128)(2,1)} %bitcast.3.refs_0_), channel_id=1, source_target_pairs={{0,6},{2,0},{4,2},{6,4},{1,7},{3,1},{5,3},{7,5},{8,14},{10,8},{12,... | collective-permute-start | bytes 786440 | tf_op jit(solution)/shard_map/ppermute | solution.py:368
  14.9 3.5 %shard_map.119 = bf16[8,256,128]{2,1,0:T(8,128)(2,1)} custom-call(bf16[128,1024]{1,0:T(8,128)(2,1)} %bitcast.3.refs_0_, bf16[128,1024]{1,0:T(8,128)(2,1)} %bitcast.21, bf16[1024,1024]{1,0:T(8,128)(2,1)} %refs_1_.1), custom_call_target="tpu_custom_call" | custom-call | flops 268435456 | bytes 3145728 | tf_op jit(solution)/shard_map/pallas_call | solution.py:93
  19.0 1.8 %all-to-all-done.refs_1_.refs_6_ = bf16[8,384,128]{2,1,0:T(8,128)(2,1)S(1)} async-done(((bf16[8,384,128]{2,1,0:T(8,128)(2,1)}), bf16[8,384,128]{2,1,0:T(8,128)(2,1)S(1)}, u32[]{:S(2)}, u32[]{:S(2)}) %all-to-all-start) | async-done | bytes 786464 | tf_op jit(solution)/shard_map/all_to_all | solution.py:339
  20.8 4.9 %collective-permute-done.2 = bf16[128,1024]{1,0:T(8,128)(2,1)S(1)} collective-permute-done((bf16[128,1024]{1,0:T(8,128)(2,1)}, bf16[128,1024]{1,0:T(8,128)(2,1)S(1)}, u32[]{:S(2)}, u32[]{:S(2)}) %collective-permute-start.2) | collective-permute-done | bytes 262176 | tf_op jit(solution)/shard_map/ppermute | solution.py:368
  25.7 5.8 %collective-permute-done.1 = bf16[128,1024]{1,0:T(8,128)(2,1)S(1)} collective-permute-done((bf16[128,1024]{1,0:T(8,128)(2,1)}, bf16[128,1024]{1,0:T(8,128)(2,1)S(1)}, u32[]{:S(2)}, u32[]{:S(2)}) %collective-permute-start.1) | collective-permute-done | bytes 262176 | tf_op jit(solution)/shard_map/ppermute | solution.py:368
  31.5 2.9 %collective-permute-start.3 = (bf16[8,256,128]{2,1,0:T(8,128)(2,1)S(1)}, bf16[8,256,128]{2,1,0:T(8,128)(2,1)S(1)}, u32[]{:S(2)}, u32[]{:S(2)}) collective-permute-start(bf16[8,256,128]{2,1,0:T(8,128)(2,1)S(1)} %slice.8), channel_id=1, source_target_pairs={{0,8},{8,16},{16,24},{24,32},{32,40},{40,48},{48,56},{1,9},{9,17},... | collective-permute-start | bytes 1572872 | tf_op jit(solution)/shard_map/ppermute | solution.py:370
  34.4 3.5 %all-to-all-start.1 = ((bf16[8,256,128]{2,1,0:T(8,128)(2,1)}), bf16[8,256,128]{2,1,0:T(8,128)(2,1)S(1)}, u32[]{:S(2)}, u32[]{:S(2)}) async-start(bf16[8,256,128]{2,1,0:T(8,128)(2,1)} %shard_map.119), calls=%async_computation.1 | async-start | bytes 1048576 | tf_op jit(solution)/shard_map/all_to_all | solution.py:339
  38.0 6.0 %shard_map.120 = (f32[4,128,256]{2,1,0:T(8,128)}, bf16[4,128,256]{2,1,0:T(8,128)(2,1)}) custom-call(s32[4]{0:T(128)} %and_select_fusion.refs_0_, bf16[8,384,128]{2,1,0:T(8,128)(2,1)} %copy-done.1, s32[8,128]{1,0:T(8,128)} %fusion.refs_2_.refs_7_), custom_call_target="tpu_custom_call" | custom-call | flops 536870912 | bytes 1576976 | tf_op jit(solution)/shard_map/pallas_call | solution.py:93
  44.0 1.3 %pad_maximum_fusion.refs_9_ = bf16[4,128,1024]{2,1,0:T(8,128)(2,1)S(1)} fusion(bf16[1,128,1024]{2,1,0:T(8,128)(2,1)} %bitcast.25, bf16[1,128,1024]{2,1,0:T(8,128)(2,1)} %bitcast.26, bf16[1,128,1024]{2,1,0:T(8,128)(2,1)} %bitcast.27, bf16[1,128,1024]{2,1,0:T(8,128)(2,1)} %param.11), kind=kLoop, calls=%fused_computation | loop fusion | flops 1572864 | bytes 2097152 | tf_op jit(solution)/shard_map/stack | solution.py:372
  45.4 2.8 %all-to-all-done.1.refs_5_.refs_3_ = bf16[8,256,128]{2,1,0:T(8,128)(2,1)S(1)} async-done(((bf16[8,256,128]{2,1,0:T(8,128)(2,1)}), bf16[8,256,128]{2,1,0:T(8,128)(2,1)S(1)}, u32[]{:S(2)}, u32[]{:S(2)}) %all-to-all-start.1) | async-done | bytes 524320 | tf_op jit(solution)/shard_map/all_to_all | solution.py:339
  49.2 3.6 %shard_map.121 = (f32[4,128,256]{2,1,0:T(8,128)}, f32[8,32,128]{2,1,0:T(8,128)}) custom-call(s32[4]{0:T(128)} %and_select_fusion.refs_0_, bf16[8,256,128]{2,1,0:T(8,128)(2,1)} %copy-done.4, s32[8,128]{1,0:T(8,128)} %fusion.refs_2_.refs_7_, bf16[4,128,256]{2,1,0:T(8,128)(2,1)} %get-tuple-element.51.refs_3_.refs_8_, f32[4,128,256]{2,1,0:T(8,128)} %get-tuple-element.60.refs_4_, ...), custom_call_target="tpu_custom_call" | custom-call | flops 268435456 | bytes 2494480 | tf_op jit(solution)/shard_map/pallas_call | solution.py:93
  52.9 10.1 %all_to_all.25.refs_4_ = f32[8,32,128]{2,1,0:T(8,128)} all-to-all(f32[8,32,128]{2,1,0:T(8,128)} %get-tuple-element.65), channel_id=1, replica_groups=mesh['dp'=4,'z'=8,'x'=4,'c'=2] {'x','c'}, dimensions={0} | all-to-all | bytes 262144 | tf_op jit(solution)/shard_map/all_to_all | solution.py:339
  63.0 4.6 %shard_map.122 = (bf16[8,640,128]{2,1,0:T(8,128)(2,1)}, bf16[4,128,256]{2,1,0:T(8,128)(2,1)}, f32[4,128,256]{2,1,0:T(8,128)}, bf16[8,256,128]{2,1,0:T(8,128)(2,1...) custom-call(s32[4]{0:T(128)} %and_select_fusion.refs_0_, ...), custom_call_target="tpu_custom_call" | custom-call | flops 536870912 | bytes 7802912 | tf_op jit(solution)/shard_map/pallas_call | solution.py:93
  67.6 4.1 %collective-permute-start.5 = (bf16[8,256,128]{2,1,0:T(8,128)(2,1)}, bf16[8,256,128]{2,1,0:T(8,128)(2,1)S(1)}, u32[]{:S(2)}, u32[]{:S(2)}) collective-permute-start(bf16[8,256,128]{2,1,0:T(8,128)(2,1)} %get-tuple-element.73), channel_id=1, source_target_pairs={{8,0},{16,8},{24,16},{32,24},{40,32},{48,40},{56,48},{9,1},{17,9},... | collective-permute-start | bytes 1572872 | tf_op jit(solution)/shard_map/ppermute | solution.py:389
  71.7 6.0 %collective-permute-start.6 = (bf16[32,1024]{1,0:T(8,128)(2,1)}, bf16[32,1024]{1,0:T(8,128)(2,1)S(1)}, u32[]{:S(2)}, u32[]{:S(2)}) collective-permute-start(bf16[32,1024]{1,0:T(8,128)(2,1)} %get-tuple-element.76), channel_id=1, source_target_pairs={{0,64},{64,128},{128,192},{192,0},{1,65},{65,129},{129,193},{193,1... | collective-permute-start | bytes 196616 | tf_op jit(solution)/shard_map/ppermute | solution.py:390
  77.7 1.2 collective-permute-start.7
  78.9 1.6 %collective-permute-start.8 = (bf16[32,1024]{1,0:T(8,128)(2,1)}, bf16[32,1024]{1,0:T(8,128)(2,1)S(1)}, u32[]{:S(2)}, u32[]{:S(2)}) collective-permute-start(bf16[32,1024]{1,0:T(8,128)(2,1)} %get-tuple-element.78), channel_id=1, source_target_pairs={{0,192},{64,0},{128,64},{192,128},{1,193},{65,1},{129,65},{193,129... | collective-permute-start | bytes 196616 | tf_op jit(solution)/shard_map/ppermute | solution.py:390
  80.5 7.3 %shard_map.123 = (bf16[8,640,128]{2,1,0:T(8,128)(2,1)}, f32[4,256,128]{2,1,0:T(8,128)}, f32[4,256,128]{2,1,0:T(8,128)}) custom-call(s32[4]{0:T(128)} %and_select_fusion.refs_0_, bf16[8,384,128]{2,1,0:T(8,128)(2,1)} %copy-done.1, s32[8,128]{1,0:T(8,128)} %fusion.refs_2_.refs_7_, ...), custom_call_target="tpu_custom_call", output_to_operand_aliasing={{0}: (6, {})} | custom-call | flops 1073741824 | bytes 5509136 | tf_op jit(solution)/shard_map/pallas_call | solution.py:93
  88.5 1.8 %shard_map.125 = bf16[8,32,128]{2,1,0:T(8,128)(2,1)} custom-call(f32[32,1024]{1,0:T(8,128)} %get-tuple-element.75.refs_0_, bf16[32,1024]{1,0:T(8,128)(2,1)} %copy-done.10, bf16[32,1024]{1,0:T(8,128)(2,1)} %copy-done.11, bf16[32,1024]{1,0:T(8,128)(2,1)} %copy-done.12), custom_call_target="tpu_custom_call" | custom-call | flops 65536 | bytes 393216 | tf_op jit(solution)/shard_map/pallas_call | solution.py:93
  91.1 2.4 %shard_map.124 = bf16[8,640,128]{2,1,0:T(8,128)(2,1)} custom-call(f32[4,256,128]{2,1,0:T(8,128)} %get-tuple-element.71.refs_0_, f32[4,256,128]{2,1,0:T(8,128)} %get-tuple-element.72.refs_1_, bf16[8,256,128]{2,1,0:T(8,128)(2,1)} %copy-done.6, bf16[8,640,128]{2,1,0:T(8,128)(2,1)} %get-tuple-element.74.refs_3_), custom_call_target="tpu_custom_call", output_to_operand_aliasing={{}: (3, {})} | custom-call | flops 1048576 | bytes 4194304 | tf_op jit(solution)/shard_map/pallas_call | solution.py:93
  93.6 3.7 %all-to-all-start.3 = ((bf16[8,640,128]{2,1,0:T(8,128)(2,1)}), bf16[8,640,128]{2,1,0:T(8,128)(2,1)S(1)}, u32[]{:S(2)}, u32[]{:S(2)}) async-start(bf16[8,640,128]{2,1,0:T(8,128)(2,1)} %shard_map.124), calls=%async_computation.3 | async-start | bytes 2621440 | tf_op jit(solution)/shard_map/all_to_all | solution.py:339
  97.3 1.9 %collective-permute-start.9 = (bf16[8,32,128]{2,1,0:T(8,128)(2,1)S(1)}, bf16[8,32,128]{2,1,0:T(8,128)(2,1)}, u32[]{:S(2)}, u32[]{:S(2)}) collective-permute-start(bf16[8,32,128]{2,1,0:T(8,128)(2,1)S(1)} %copy-done.13), channel_id=1, source_target_pairs={{0,0},{1,32},{2,64},{3,96},{4,128},{5,160},{6,192},{7,224},{8,1},{... | collective-permute-start | bytes 196616 | tf_op jit(solution)/shard_map/ppermute | solution.py:404
  99.2 7.7 %collective-permute-done.9 = bf16[8,32,128]{2,1,0:T(8,128)(2,1)} collective-permute-done((bf16[8,32,128]{2,1,0:T(8,128)(2,1)S(1)}, bf16[8,32,128]{2,1,0:T(8,128)(2,1)}, u32[]{:S(2)}, u32[]{:S(2)}) %collective-permute-start.9) | collective-permute-done | bytes 65568 | tf_op jit(solution)/shard_map/ppermute | solution.py:404
  106.9 11.9 %all-to-all-done.3.refs_0_ = bf16[8,640,128]{2,1,0:T(8,128)(2,1)S(1)} async-done(((bf16[8,640,128]{2,1,0:T(8,128)(2,1)}), bf16[8,640,128]{2,1,0:T(8,128)(2,1)S(1)}, u32[]{:S(2)}, u32[]{:S(2)}) %all-to-all-start.3) | async-done | bytes 1310752 | tf_op jit(solution)/shard_map/all_to_all | solution.py:339
  118.8 3.3 %all-to-all-start.4 = ((bf16[8,32,128]{2,1,0:T(8,128)(2,1)}), bf16[8,32,128]{2,1,0:T(8,128)(2,1)S(1)}, u32[]{:S(2)}, u32[]{:S(2)}) async-start(bf16[8,32,128]{2,1,0:T(8,128)(2,1)} %collective-permute-done.9), calls=%async_computation.4 | async-start | bytes 131072 | tf_op jit(solution)/shard_map/all_to_all | solution.py:339
  122.2 2.1 %shard_map.126 = (bf16[128,1024]{1,0:T(8,128)(2,1)}, bf16[128,1024]{1,0:T(8,128)(2,1)}, bf16[128,1024]{1,0:T(8,128)(2,1)}, bf16[128,1024]{1,0:T(8,128)(2,1)}, bf16[128,1024]{1,0:T(8,128)(2,1)}) custom-call(bf16[8,640,128]{2,1,0:T(8,128)(2,1)S(1)} %all-to-all-done.3.refs_0_, bf16[1024,1024]{1,0:T(8,128)(2,1)S(1)} %copy-done), custom_call_target="tpu_custom_call" | custom-call | flops 268435456 | bytes 4718592 | tf_op jit(solution)/shard_map/pallas_call | solution.py:93
  124.3 3.4 %all-to-all-done.4.refs_0_ = bf16[8,32,128]{2,1,0:T(8,128)(2,1)S(1)} async-done(((bf16[8,32,128]{2,1,0:T(8,128)(2,1)}), bf16[8,32,128]{2,1,0:T(8,128)(2,1)S(1)}, u32[]{:S(2)}, u32[]{:S(2)}) %all-to-all-start.4) | async-done | bytes 65568 | tf_op jit(solution)/shard_map/all_to_all | solution.py:339
  127.7 0.8 shard_map.127
  (47 shorter events, 4.7 us)
Async XLA Ops:
  0.6 6.4 %copy-start.14 = (s32[1,8192]{1,0:T(1,128)S(1)}, s32[1,8192]{1,0:T(1,128)}, u32[]{:S(2)}) copy-start(s32[1,8192]{1,0:T(1,128)} %param.12) | copy-start | bytes 98308
  2.7 18.0 %all-to-all-start = ((bf16[8,384,128]{2,1,0:T(8,128)(2,1)}), bf16[8,384,128]{2,1,0:T(8,128)(2,1)S(1)}, u32[]{:S(2)}, u32[]{:S(2)}) async-start(bf16[8,384,128]{2,1,0:T(8,128)(2,1)} %shard_map.118), calls=%async_computation | async-start | bytes 1572864 | tf_op jit(solution)/shard_map/all_to_all | solution.py:339
  8.1 17.6 %collective-permute-start.2 = (bf16[128,1024]{1,0:T(8,128)(2,1)}, bf16[128,1024]{1,0:T(8,128)(2,1)S(1)}, u32[]{:S(2)}, u32[]{:S(2)}) collective-permute-start(bf16[128,1024]{1,0:T(8,128)(2,1)} %bitcast.3.refs_0_), channel_id=1, source_target_pairs={{0,2},{2,4},{4,6},{6,0},{1,3},{3,5},{5,7},{7,1},{8,10},{10,12},{12... | collective-permute-start | bytes 786440 | tf_op jit(solution)/shard_map/ppermute | solution.py:368
  10.1 21.4 %collective-permute-start.1 = (bf16[128,1024]{1,0:T(8,128)(2,1)}, bf16[128,1024]{1,0:T(8,128)(2,1)S(1)}, u32[]{:S(2)}, u32[]{:S(2)}) collective-permute-start(bf16[128,1024]{1,0:T(8,128)(2,1)} %bitcast.3.refs_0_), channel_id=1, source_target_pairs={{0,4},{2,6},{4,0},{6,2},{1,5},{3,7},{5,1},{7,3},{8,12},{10,14},{12... | collective-permute-start | bytes 786440 | tf_op jit(solution)/shard_map/ppermute | solution.py:368
  12.8 18.7 %collective-permute-start = (bf16[128,1024]{1,0:T(8,128)(2,1)}, bf16[128,1024]{1,0:T(8,128)(2,1)S(1)}, u32[]{:S(2)}, u32[]{:S(2)}) collective-permute-start(bf16[128,1024]{1,0:T(8,128)(2,1)} %bitcast.3.refs_0_), channel_id=1, source_target_pairs={{0,6},{2,0},{4,2},{6,4},{1,7},{3,1},{5,3},{7,5},{8,14},{10,8},{12,... | collective-permute-start | bytes 786440 | tf_op jit(solution)/shard_map/ppermute | solution.py:368
  20.7 17.2 %copy-start.1 = (bf16[8,384,128]{2,1,0:T(8,128)(2,1)}, bf16[8,384,128]{2,1,0:T(8,128)(2,1)S(1)}, u32[]{:S(2)}) copy-start(bf16[8,384,128]{2,1,0:T(8,128)(2,1)S(1)} %all-to-all-done.refs_1_.refs_6_) | copy-start | bytes 2359300
  25.7 18.3 %copy-start.7 = (bf16[128,1024]{1,0:T(8,128)(2,1)}, bf16[128,1024]{1,0:T(8,128)(2,1)S(1)}, u32[]{:S(2)}) copy-start(bf16[128,1024]{1,0:T(8,128)(2,1)S(1)} %collective-permute-done.2) | copy-start | bytes 786436
  31.5 12.5 %copy-start.8 = (bf16[128,1024]{1,0:T(8,128)(2,1)}, bf16[128,1024]{1,0:T(8,128)(2,1)S(1)}, u32[]{:S(2)}) copy-start(bf16[128,1024]{1,0:T(8,128)(2,1)S(1)} %collective-permute-done.1) | copy-start | bytes 786436
  31.5 12.5 %copy-start.9 = (bf16[128,1024]{1,0:T(8,128)(2,1)}, bf16[128,1024]{1,0:T(8,128)(2,1)S(1)}, u32[]{:S(2)}) copy-start(bf16[128,1024]{1,0:T(8,128)(2,1)S(1)} %collective-permute-done) | copy-start | bytes 786436
  31.5 16.7 %collective-permute-start.3 = (bf16[8,256,128]{2,1,0:T(8,128)(2,1)S(1)}, bf16[8,256,128]{2,1,0:T(8,128)(2,1)S(1)}, u32[]{:S(2)}, u32[]{:S(2)}) collective-permute-start(bf16[8,256,128]{2,1,0:T(8,128)(2,1)S(1)} %slice.8), channel_id=1, source_target_pairs={{0,8},{8,16},{16,24},{24,32},{32,40},{40,48},{48,56},{1,9},{9,17},... | collective-permute-start | bytes 1572872 | tf_op jit(solution)/shard_map/ppermute | solution.py:370
  34.4 13.8 %all-to-all-start.1 = ((bf16[8,256,128]{2,1,0:T(8,128)(2,1)}), bf16[8,256,128]{2,1,0:T(8,128)(2,1)S(1)}, u32[]{:S(2)}, u32[]{:S(2)}) async-start(bf16[8,256,128]{2,1,0:T(8,128)(2,1)} %shard_map.119), calls=%async_computation.1 | async-start | bytes 1048576 | tf_op jit(solution)/shard_map/all_to_all | solution.py:339
  45.4 17.6 %copy-start.3 = (bf16[4,128,1024]{2,1,0:T(8,128)(2,1)}, bf16[4,128,1024]{2,1,0:T(8,128)(2,1)S(1)}, u32[]{:S(2)}) copy-start(bf16[4,128,1024]{2,1,0:T(8,128)(2,1)S(1)} %pad_maximum_fusion.refs_9_) | copy-start | bytes 3145732
  48.2 0.8 copy-start.2
  48.2 1.0 copy-start.4
  48.2 4.6 %collective-permute-start.4 = (bf16[4,128,1024]{2,1,0:T(8,128)(2,1)S(1)}, bf16[4,128,1024]{2,1,0:T(8,128)(2,1)S(1)}, u32[]{:S(2)}, u32[]{:S(2)}) collective-permute-start(bf16[4,128,1024]{2,1,0:T(8,128)(2,1)S(1)} %pad_maximum_fusion.refs_9_), channel_id=1, source_target_pairs={{0,1},{1,0},{2,3},{3,2},{4,5},{5,4},{6,7},{7,6},{8,9},{9,8},{10,11... | collective-permute-start | bytes 3145736 | tf_op jit(solution)/shard_map/ppermute | solution.py:375
  52.9 10.1 %copy-start.5 = (bf16[4,128,1024]{2,1,0:T(8,128)(2,1)}, bf16[4,128,1024]{2,1,0:T(8,128)(2,1)S(1)}, u32[]{:S(2)}) copy-start(bf16[4,128,1024]{2,1,0:T(8,128)(2,1)S(1)} %collective-permute-done.4.refs_10_) | copy-start | bytes 3145732
  67.6 22.7 %collective-permute-start.5 = (bf16[8,256,128]{2,1,0:T(8,128)(2,1)}, bf16[8,256,128]{2,1,0:T(8,128)(2,1)S(1)}, u32[]{:S(2)}, u32[]{:S(2)}) collective-permute-start(bf16[8,256,128]{2,1,0:T(8,128)(2,1)} %get-tuple-element.73), channel_id=1, source_target_pairs={{8,0},{16,8},{24,16},{32,24},{40,32},{48,40},{56,48},{9,1},{17,9},... | collective-permute-start | bytes 1572872 | tf_op jit(solution)/shard_map/ppermute | solution.py:389
  71.7 16.1 %collective-permute-start.6 = (bf16[32,1024]{1,0:T(8,128)(2,1)}, bf16[32,1024]{1,0:T(8,128)(2,1)S(1)}, u32[]{:S(2)}, u32[]{:S(2)}) collective-permute-start(bf16[32,1024]{1,0:T(8,128)(2,1)} %get-tuple-element.76), channel_id=1, source_target_pairs={{0,64},{64,128},{128,192},{192,0},{1,65},{65,129},{129,193},{193,1... | collective-permute-start | bytes 196616 | tf_op jit(solution)/shard_map/ppermute | solution.py:390
  77.7 10.1 %collective-permute-start.7 = (bf16[32,1024]{1,0:T(8,128)(2,1)}, bf16[32,1024]{1,0:T(8,128)(2,1)S(1)}, u32[]{:S(2)}, u32[]{:S(2)}) collective-permute-start(bf16[32,1024]{1,0:T(8,128)(2,1)} %get-tuple-element.77), channel_id=1, source_target_pairs={{0,128},{64,192},{128,0},{192,64},{1,129},{65,193},{129,1},{193,65... | collective-permute-start | bytes 196616 | tf_op jit(solution)/shard_map/ppermute | solution.py:390
  78.9 8.9 %collective-permute-start.8 = (bf16[32,1024]{1,0:T(8,128)(2,1)}, bf16[32,1024]{1,0:T(8,128)(2,1)S(1)}, u32[]{:S(2)}, u32[]{:S(2)}) collective-permute-start(bf16[32,1024]{1,0:T(8,128)(2,1)} %get-tuple-element.78), channel_id=1, source_target_pairs={{0,192},{64,0},{128,64},{192,128},{1,193},{65,1},{129,65},{193,129... | collective-permute-start | bytes 196616 | tf_op jit(solution)/shard_map/ppermute | solution.py:390
  87.8 0.6 copy-start.10
  87.8 0.6 copy-start.11
  87.9 0.6 copy-start.12
  90.3 0.8 copy-start.6
  93.6 3.7 %copy-start.13 = (bf16[8,32,128]{2,1,0:T(8,128)(2,1)S(1)}, bf16[8,32,128]{2,1,0:T(8,128)(2,1)}, u32[]{:S(2)}) copy-start(bf16[8,32,128]{2,1,0:T(8,128)(2,1)} %shard_map.125) | copy-start | bytes 196612
  93.6 28.6 %copy-start = (bf16[1024,1024]{1,0:T(8,128)(2,1)S(1)}, bf16[1024,1024]{1,0:T(8,128)(2,1)}, u32[]{:S(2)}) copy-start(bf16[1024,1024]{1,0:T(8,128)(2,1)} %refs_1_.1) | copy-start | bytes 6291460
  93.6 25.2 %all-to-all-start.3 = ((bf16[8,640,128]{2,1,0:T(8,128)(2,1)}), bf16[8,640,128]{2,1,0:T(8,128)(2,1)S(1)}, u32[]{:S(2)}, u32[]{:S(2)}) async-start(bf16[8,640,128]{2,1,0:T(8,128)(2,1)} %shard_map.124), calls=%async_computation.3 | async-start | bytes 2621440 | tf_op jit(solution)/shard_map/all_to_all | solution.py:339
  97.3 9.6 %collective-permute-start.9 = (bf16[8,32,128]{2,1,0:T(8,128)(2,1)S(1)}, bf16[8,32,128]{2,1,0:T(8,128)(2,1)}, u32[]{:S(2)}, u32[]{:S(2)}) collective-permute-start(bf16[8,32,128]{2,1,0:T(8,128)(2,1)S(1)} %copy-done.13), channel_id=1, source_target_pairs={{0,0},{1,32},{2,64},{3,96},{4,128},{5,160},{6,192},{7,224},{8,1},{... | collective-permute-start | bytes 196616 | tf_op jit(solution)/shard_map/ppermute | solution.py:404
  118.8 8.9 %all-to-all-start.4 = ((bf16[8,32,128]{2,1,0:T(8,128)(2,1)}), bf16[8,32,128]{2,1,0:T(8,128)(2,1)S(1)}, u32[]{:S(2)}, u32[]{:S(2)}) async-start(bf16[8,32,128]{2,1,0:T(8,128)(2,1)} %collective-permute-done.9), calls=%async_computation.4 | async-start | bytes 131072 | tf_op jit(solution)/shard_map/all_to_all | solution.py:339

commit v11 on v10

--- a/solution.py
+++ b/solution.py
@@ -366,11 +366,12 @@
 
     low, cot_later = lax.optimization_barrier((low, cot))
     along = [lax.ppermute(cot_later, "x", [(i, (i - n) % 4) for i in range(4)]) for n in (1, 2, 3)]
-    pair, gd, start, low, who, *along = lax.optimization_barrier((recv[:, 128:384], gd, start, low, who, *along))
+    pair, gd, start, low, who = lax.optimization_barrier((recv[:, 128:384], gd, start, low, who))
     halo = lax.ppermute(pair, "z", [(i, i + 1) for i in range(planes - 1)])
     gd_recv = plane_exchange(gd)
+    part, qt = call(fwd_own_body, "shh", [head, head16], 1 << 29, [vt])(low, recv, start)
+    part, *along = lax.optimization_barrier((part, *along))
     near = jnp.stack([cot, *along])
-    part, qt = call(fwd_own_body, "shh", [head, head16], 1 << 29, [vt])(low, recv, start)
     halo, gd_recv, near, part = lax.optimization_barrier((halo, gd_recv, near, part))
     mate = lax.ppermute(near, "c", [(0, 1), (1, 0)])
     mixt, stats = call(fwd_halo_body, "shhhhh", [head, shape((8, 32, 128), F32)], 1 << 28, [vt], TIGHT, kept={1: (1, 32, 128)})(

time: 130 us -> 130 us (level)
  starting transfers between devices: 38.9 us -> 34.6 us
  Pallas kernels: 34.3 us -> 37.8 us
  waiting for transfers between devices: 38.3 us -> 40.3 us
  other arithmetic: 3.48 us -> 2.15 us
    pallas_call x10, Pallas kernels: 34.3 us -> 37.8 us  [build(): pl.pallas_call(whole, out_shape=outs, in_specs=[pl.BlockSpec(memory_space...]
    all_to_all x4, waiting for transfers between devices: 19.9 us -> 22.8 us  [plane_exchange(): return lax.all_to_all(blocks, PLANE_AXES, 0, 0, tiled=True)]
    ppermute x1, starting transfers between devices: 4.13 us -> 1.92 us  [shards(): back = lax.ppermute(back, 'z', [(i, i - 1) for i in range(1, planes)])]
    ppermute x3, starting transfers between devices: 8.77 us -> 6.76 us  [shards(): lax.ppermute(x, 'dp', [(i, (i + n + 1) % dp) for i in range(dp)])]
  transfers between devices with their start and end apart: 14 -> 14, of which waited for: 7 -> 6; matrix products, arithmetic and copies ran while one was open for 3% -> 2% of each run, Pallas kernels for 19% -> 20%
where the time goes in v11:
time: 130 us; the launch traced here: 129 us
  waiting for transfers between devices  40.3 us (31%)
  Pallas kernels  37.8 us (29%)
  starting transfers between devices  34.6 us (27%)
  blocking collectives  10.1 us (8%)
  local copies, waits for them, and re-layouts  3.36 us (3%)
  other arithmetic  2.15 us (2%)
    pallas_call x10, Pallas kernels, build(): pl.pallas_call(whole, out_shape=outs, in_specs=[pl.BlockSpec(memory_space...  37.8 us
    all_to_all x4, waiting for transfers between devices, plane_exchange(): return lax.all_to_all(blocks, PLANE_AXES, 0, 0, tiled=True)  22.8 us
    all_to_all x4, starting transfers between devices, plane_exchange(): return lax.all_to_all(blocks, PLANE_AXES, 0, 0, tiled=True)  14.9 us
    all_to_all x1, blocking collectives, plane_exchange(): return lax.all_to_all(blocks, PLANE_AXES, 0, 0, tiled=True)  10.1 us
    ppermute x3, waiting for transfers between devices, shards(): lax.ppermute(cot_later, 'x', [(i, (i - n) % 4) for i in range(4)])  9.81 us
    ppermute x1, waiting for transfers between devices, shards(): moved = lax.ppermute(moved, ('dp', 'z', 'x', 'c'), route)  7.68 us
    ppermute x3, starting transfers between devices, shards(): lax.ppermute(x, 'dp', [(i, (i + n + 1) % dp) for i in range(dp)])  6.76 us
    ppermute x3, starting transfers between devices, shards(): lax.ppermute(cot_later, 'x', [(i, (i - n) % 4) for i in range(4)])  6.07 us
  transfers between devices with their start and end apart: 14, of which 6 were waited for; matrix products, arithmetic and copies ran while one was open for 2% of the time, Pallas kernels for 20%

profile of v11, /device:TPU:128, one launch (start us, length us, event | category | flops | bytes accessed | tf_op | source)
XLA Modules:
  0.0 129.5 jit_solution(4733864631234515374)
XLA Ops:
  0.6 2.1 %shard_map.118 = bf16[8,384,128]{2,1,0:T(8,128)(2,1)} custom-call(bf16[128,1024]{1,0:T(8,128)(2,1)} %bitcast.26, bf16[128,1024]{1,0:T(8,128)(2,1)} %bitcast.27, bf16[128,1024]{1,0:T(8,128)(2,1)} %bitcast.28), custom_call_target="tpu_custom_call" | custom-call | flops 65536 | bytes 1572864 | tf_op jit(solution)/shard_map/pallas_call | solution.py:93
  2.8 4.3 %all-to-all-start = ((bf16[8,384,128]{2,1,0:T(8,128)(2,1)}), bf16[8,384,128]{2,1,0:T(8,128)(2,1)S(1)}, u32[]{:S(2)}, u32[]{:S(2)}) async-start(bf16[8,384,128]{2,1,0:T(8,128)(2,1)} %shard_map.118), calls=%async_computation | async-start | bytes 1572864 | tf_op jit(solution)/shard_map/all_to_all | solution.py:339
  8.1 3.5 %shard_map.119 = bf16[8,256,128]{2,1,0:T(8,128)(2,1)} custom-call(bf16[128,1024]{1,0:T(8,128)(2,1)} %bitcast.21, bf16[128,1024]{1,0:T(8,128)(2,1)} %bitcast.25, bf16[1024,1024]{1,0:T(8,128)(2,1)} %refs_1_.1), custom_call_target="tpu_custom_call" | custom-call | flops 268435456 | bytes 3145728 | tf_op jit(solution)/shard_map/pallas_call | solution.py:93
  12.7 7.5 %all-to-all-done.refs_1_.refs_6_ = bf16[8,384,128]{2,1,0:T(8,128)(2,1)S(1)} async-done(((bf16[8,384,128]{2,1,0:T(8,128)(2,1)}), bf16[8,384,128]{2,1,0:T(8,128)(2,1)S(1)}, u32[]{:S(2)}, u32[]{:S(2)}) %all-to-all-start) | async-done | bytes 786464 | tf_op jit(solution)/shard_map/all_to_all | solution.py:339
  20.3 0.9 slice.8
  21.2 2.9 %collective-permute-start = (bf16[8,256,128]{2,1,0:T(8,128)(2,1)}, bf16[8,256,128]{2,1,0:T(8,128)(2,1)S(1)}, u32[]{:S(2)}, u32[]{:S(2)}) collective-permute-start(bf16[8,256,128]{2,1,0:T(8,128)(2,1)} %slice.8), channel_id=1, source_target_pairs={{0,8},{8,16},{16,24},{24,32},{32,40},{40,48},{48,56},{1,9},{9,17},... | collective-permute-start | bytes 1572872 | tf_op jit(solution)/shard_map/ppermute | solution.py:370
  24.1 3.5 %all-to-all-start.1 = ((bf16[8,256,128]{2,1,0:T(8,128)(2,1)}), bf16[8,256,128]{2,1,0:T(8,128)(2,1)S(1)}, u32[]{:S(2)}, u32[]{:S(2)}) async-start(bf16[8,256,128]{2,1,0:T(8,128)(2,1)} %shard_map.119), calls=%async_computation.1 | async-start | bytes 1048576 | tf_op jit(solution)/shard_map/all_to_all | solution.py:339
  27.6 1.9 %collective-permute-start.3 = (bf16[128,1024]{1,0:T(8,128)(2,1)S(1)}, bf16[128,1024]{1,0:T(8,128)(2,1)S(1)}, u32[]{:S(2)}, u32[]{:S(2)}) collective-permute-start(bf16[128,1024]{1,0:T(8,128)(2,1)S(1)} %bitcast.22), channel_id=1, source_target_pairs={{0,2},{2,4},{4,6},{6,0},{1,3},{3,5},{5,7},{7,1},{8,10},{10,12},{12... | collective-permute-start | bytes 786440 | tf_op jit(solution)/shard_map/ppermute | solution.py:368
  29.5 2.7 %collective-permute-start.2 = (bf16[128,1024]{1,0:T(8,128)(2,1)S(1)}, bf16[128,1024]{1,0:T(8,128)(2,1)S(1)}, u32[]{:S(2)}, u32[]{:S(2)}) collective-permute-start(bf16[128,1024]{1,0:T(8,128)(2,1)S(1)} %bitcast.23), channel_id=1, source_target_pairs={{0,4},{2,6},{4,0},{6,2},{1,5},{3,7},{5,1},{7,3},{8,12},{10,14},{12... | collective-permute-start | bytes 786440 | tf_op jit(solution)/shard_map/ppermute | solution.py:368
  32.2 1.4 %collective-permute-start.1 = (bf16[128,1024]{1,0:T(8,128)(2,1)S(1)}, bf16[128,1024]{1,0:T(8,128)(2,1)S(1)}, u32[]{:S(2)}, u32[]{:S(2)}) collective-permute-start(bf16[128,1024]{1,0:T(8,128)(2,1)S(1)} %bitcast.24), channel_id=1, source_target_pairs={{0,6},{2,0},{4,2},{6,4},{1,7},{3,1},{5,3},{7,5},{8,14},{10,8},{12,... | collective-permute-start | bytes 786440 | tf_op jit(solution)/shard_map/ppermute | solution.py:368
  33.7 5.7 %shard_map.120 = (f32[4,128,256]{2,1,0:T(8,128)}, bf16[4,128,256]{2,1,0:T(8,128)(2,1)}) custom-call(s32[4]{0:T(128)} %and_select_fusion.refs_0_, bf16[8,384,128]{2,1,0:T(8,128)(2,1)} %copy-done.1, s32[8,128]{1,0:T(8,128)} %fusion.refs_2_.refs_7_), custom_call_target="tpu_custom_call" | custom-call | flops 536870912 | bytes 1576976 | tf_op jit(solution)/shard_map/pallas_call | solution.py:93
  39.3 4.0 %collective-permute-done.3 = bf16[128,1024]{1,0:T(8,128)(2,1)S(1)} collective-permute-done((bf16[128,1024]{1,0:T(8,128)(2,1)S(1)}, bf16[128,1024]{1,0:T(8,128)(2,1)S(1)}, u32[]{:S(2)}, u32[]{:S(2)}) %collective-permute-start.3) | collective-permute-done | bytes 262176 | tf_op jit(solution)/shard_map/ppermute | solution.py:368
  43.3 5.8 %collective-permute-done.2 = bf16[128,1024]{1,0:T(8,128)(2,1)S(1)} collective-permute-done((bf16[128,1024]{1,0:T(8,128)(2,1)S(1)}, bf16[128,1024]{1,0:T(8,128)(2,1)S(1)}, u32[]{:S(2)}, u32[]{:S(2)}) %collective-permute-start.2) | collective-permute-done | bytes 262176 | tf_op jit(solution)/shard_map/ppermute | solution.py:368
  49.4 0.7 copy-done.2
  50.3 5.6 %shard_map.121 = (f32[4,128,256]{2,1,0:T(8,128)}, f32[8,32,128]{2,1,0:T(8,128)}) custom-call(s32[4]{0:T(128)} %and_select_fusion.refs_0_, bf16[8,256,128]{2,1,0:T(8,128)(2,1)} %copy-done.4, s32[8,128]{1,0:T(8,128)} %fusion.refs_2_.refs_7_, bf16[4,128,256]{2,1,0:T(8,128)(2,1)} %get-tuple-element.51.refs_3_.refs_8_, f32[4,128,256]{2,1,0:T(8,128)} %get-tuple-element.62.refs_4_, ...), custom_call_target="tpu_custom_call" | custom-call | flops 268435456 | bytes 2494480 | tf_op jit(solution)/shard_map/pallas_call | solution.py:93
  56.0 10.1 %all_to_all.25.refs_4_ = f32[8,32,128]{2,1,0:T(8,128)} all-to-all(f32[8,32,128]{2,1,0:T(8,128)} %get-tuple-element.67), channel_id=1, replica_groups=mesh['dp'=4,'z'=8,'x'=4,'c'=2] {'x','c'}, dimensions={0} | all-to-all | bytes 262144 | tf_op jit(solution)/shard_map/all_to_all | solution.py:339
  66.1 7.0 %shard_map.122 = (bf16[8,640,128]{2,1,0:T(8,128)(2,1)}, bf16[4,128,256]{2,1,0:T(8,128)(2,1)}, f32[4,128,256]{2,1,0:T(8,128)}, bf16[8,256,128]{2,1,0:T(8,128)(2,1...) custom-call(s32[4]{0:T(128)} %and_select_fusion.refs_0_, ...), custom_call_target="tpu_custom_call" | custom-call | flops 536870912 | bytes 7802912 | tf_op jit(solution)/shard_map/pallas_call | solution.py:93
  73.1 1.9 %collective-permute-start.5 = (bf16[8,256,128]{2,1,0:T(8,128)(2,1)}, bf16[8,256,128]{2,1,0:T(8,128)(2,1)S(1)}, u32[]{:S(2)}, u32[]{:S(2)}) collective-permute-start(bf16[8,256,128]{2,1,0:T(8,128)(2,1)} %get-tuple-element.75), channel_id=1, source_target_pairs={{8,0},{16,8},{24,16},{32,24},{40,32},{48,40},{56,48},{9,1},{17,9},... | collective-permute-start | bytes 1572872 | tf_op jit(solution)/shard_map/ppermute | solution.py:390
  75.0 2.1 %collective-permute-start.6 = (bf16[32,1024]{1,0:T(8,128)(2,1)}, bf16[32,1024]{1,0:T(8,128)(2,1)S(1)}, u32[]{:S(2)}, u32[]{:S(2)}) collective-permute-start(bf16[32,1024]{1,0:T(8,128)(2,1)} %get-tuple-element.78), channel_id=1, source_target_pairs={{0,64},{64,128},{128,192},{192,0},{1,65},{65,129},{129,193},{193,1... | collective-permute-start | bytes 196616 | tf_op jit(solution)/shard_map/ppermute | solution.py:391
  77.2 4.6 %collective-permute-start.7 = (bf16[32,1024]{1,0:T(8,128)(2,1)}, bf16[32,1024]{1,0:T(8,128)(2,1)S(1)}, u32[]{:S(2)}, u32[]{:S(2)}) collective-permute-start(bf16[32,1024]{1,0:T(8,128)(2,1)} %get-tuple-element.79), channel_id=1, source_target_pairs={{0,128},{64,192},{128,0},{192,64},{1,129},{65,193},{129,1},{193,65... | collective-permute-start | bytes 196616 | tf_op jit(solution)/shard_map/ppermute | solution.py:391
  81.8 6.8 %shard_map.123 = (bf16[8,640,128]{2,1,0:T(8,128)(2,1)}, f32[4,256,128]{2,1,0:T(8,128)}, f32[4,256,128]{2,1,0:T(8,128)}) custom-call(s32[4]{0:T(128)} %and_select_fusion.refs_0_, bf16[8,384,128]{2,1,0:T(8,128)(2,1)} %copy-done.1, s32[8,128]{1,0:T(8,128)} %fusion.refs_2_.refs_7_, ...), custom_call_target="tpu_custom_call", output_to_operand_aliasing={{0}: (6, {})} | custom-call | flops 1073741824 | bytes 5509136 | tf_op jit(solution)/shard_map/pallas_call | solution.py:93
  89.3 1.8 %shard_map.125 = bf16[8,32,128]{2,1,0:T(8,128)(2,1)} custom-call(f32[32,1024]{1,0:T(8,128)} %get-tuple-element.77.refs_0_, bf16[32,1024]{1,0:T(8,128)(2,1)} %copy-done.8, bf16[32,1024]{1,0:T(8,128)(2,1)} %copy-done.9, bf16[32,1024]{1,0:T(8,128)(2,1)} %copy-done.10), custom_call_target="tpu_custom_call" | custom-call | flops 65536 | bytes 393216 | tf_op jit(solution)/shard_map/pallas_call | solution.py:93
  91.1 0.8 copy-done.7
  91.9 2.4 %shard_map.124 = bf16[8,640,128]{2,1,0:T(8,128)(2,1)} custom-call(f32[4,256,128]{2,1,0:T(8,128)} %get-tuple-element.73.refs_0_, f32[4,256,128]{2,1,0:T(8,128)} %get-tuple-element.74.refs_1_, bf16[8,256,128]{2,1,0:T(8,128)(2,1)} %copy-done.7, bf16[8,640,128]{2,1,0:T(8,128)(2,1)} %get-tuple-element.76.refs_3_), custom_call_target="tpu_custom_call", output_to_operand_aliasing={{}: (3, {})} | custom-call | flops 1048576 | bytes 4194304 | tf_op jit(solution)/shard_map/pallas_call | solution.py:93
  94.4 3.7 %all-to-all-start.3 = ((bf16[8,640,128]{2,1,0:T(8,128)(2,1)}), bf16[8,640,128]{2,1,0:T(8,128)(2,1)S(1)}, u32[]{:S(2)}, u32[]{:S(2)}) async-start(bf16[8,640,128]{2,1,0:T(8,128)(2,1)} %shard_map.124), calls=%async_computation.3 | async-start | bytes 2621440 | tf_op jit(solution)/shard_map/all_to_all | solution.py:339
  98.1 1.9 %collective-permute-start.9 = (bf16[8,32,128]{2,1,0:T(8,128)(2,1)S(1)}, bf16[8,32,128]{2,1,0:T(8,128)(2,1)}, u32[]{:S(2)}, u32[]{:S(2)}) collective-permute-start(bf16[8,32,128]{2,1,0:T(8,128)(2,1)S(1)} %copy-done.11), channel_id=1, source_target_pairs={{0,0},{1,32},{2,64},{3,96},{4,128},{5,160},{6,192},{7,224},{8,1},{... | collective-permute-start | bytes 196616 | tf_op jit(solution)/shard_map/ppermute | solution.py:405
  100.0 7.7 %collective-permute-done.9 = bf16[8,32,128]{2,1,0:T(8,128)(2,1)} collective-permute-done((bf16[8,32,128]{2,1,0:T(8,128)(2,1)S(1)}, bf16[8,32,128]{2,1,0:T(8,128)(2,1)}, u32[]{:S(2)}, u32[]{:S(2)}) %collective-permute-start.9) | collective-permute-done | bytes 65568 | tf_op jit(solution)/shard_map/ppermute | solution.py:405
  107.7 11.9 %all-to-all-done.3.refs_0_ = bf16[8,640,128]{2,1,0:T(8,128)(2,1)S(1)} async-done(((bf16[8,640,128]{2,1,0:T(8,128)(2,1)}), bf16[8,640,128]{2,1,0:T(8,128)(2,1)S(1)}, u32[]{:S(2)}, u32[]{:S(2)}) %all-to-all-start.3) | async-done | bytes 1310752 | tf_op jit(solution)/shard_map/all_to_all | solution.py:339
  119.6 3.3 %all-to-all-start.4 = ((bf16[8,32,128]{2,1,0:T(8,128)(2,1)}), bf16[8,32,128]{2,1,0:T(8,128)(2,1)S(1)}, u32[]{:S(2)}, u32[]{:S(2)}) async-start(bf16[8,32,128]{2,1,0:T(8,128)(2,1)} %collective-permute-done.9), calls=%async_computation.4 | async-start | bytes 131072 | tf_op jit(solution)/shard_map/all_to_all | solution.py:339
  123.0 2.1 %shard_map.126 = (bf16[128,1024]{1,0:T(8,128)(2,1)}, bf16[128,1024]{1,0:T(8,128)(2,1)}, bf16[128,1024]{1,0:T(8,128)(2,1)}, bf16[128,1024]{1,0:T(8,128)(2,1)}, bf16[128,1024]{1,0:T(8,128)(2,1)}) custom-call(bf16[8,640,128]{2,1,0:T(8,128)(2,1)S(1)} %all-to-all-done.3.refs_0_, bf16[1024,1024]{1,0:T(8,128)(2,1)S(1)} %copy-done), custom_call_target="tpu_custom_call" | custom-call | flops 268435456 | bytes 4718592 | tf_op jit(solution)/shard_map/pallas_call | solution.py:93
  125.1 3.4 %all-to-all-done.4.refs_0_ = bf16[8,32,128]{2,1,0:T(8,128)(2,1)S(1)} async-done(((bf16[8,32,128]{2,1,0:T(8,128)(2,1)}), bf16[8,32,128]{2,1,0:T(8,128)(2,1)S(1)}, u32[]{:S(2)}, u32[]{:S(2)}) %all-to-all-start.4) | async-done | bytes 65568 | tf_op jit(solution)/shard_map/all_to_all | solution.py:339
  128.5 0.8 shard_map.127
  (43 shorter events, 3.2 us)
Async XLA Ops:
  0.6 6.5 %copy-start.12 = (s32[1,8192]{1,0:T(1,128)S(1)}, s32[1,8192]{1,0:T(1,128)}, u32[]{:S(2)}) copy-start(s32[1,8192]{1,0:T(1,128)} %param.12) | copy-start | bytes 98308
  2.8 17.5 %all-to-all-start = ((bf16[8,384,128]{2,1,0:T(8,128)(2,1)}), bf16[8,384,128]{2,1,0:T(8,128)(2,1)S(1)}, u32[]{:S(2)}, u32[]{:S(2)}) async-start(bf16[8,384,128]{2,1,0:T(8,128)(2,1)} %shard_map.118), calls=%async_computation | async-start | bytes 1572864 | tf_op jit(solution)/shard_map/all_to_all | solution.py:339
  11.6 16.0 %copy-start.6 = (bf16[1,128,1024]{2,1,0:T(8,128)(2,1)S(1)}, bf16[1,128,1024]{2,1,0:T(8,128)(2,1)}, u32[]{:S(2)}) copy-start(bf16[1,128,1024]{2,1,0:T(8,128)(2,1)} %param.11) | copy-start | bytes 786436
  20.2 13.4 %copy-start.1 = (bf16[8,384,128]{2,1,0:T(8,128)(2,1)}, bf16[8,384,128]{2,1,0:T(8,128)(2,1)S(1)}, u32[]{:S(2)}) copy-start(bf16[8,384,128]{2,1,0:T(8,128)(2,1)S(1)} %all-to-all-done.refs_1_.refs_6_) | copy-start | bytes 2359300
  21.2 28.2 %collective-permute-start = (bf16[8,256,128]{2,1,0:T(8,128)(2,1)}, bf16[8,256,128]{2,1,0:T(8,128)(2,1)S(1)}, u32[]{:S(2)}, u32[]{:S(2)}) collective-permute-start(bf16[8,256,128]{2,1,0:T(8,128)(2,1)} %slice.8), channel_id=1, source_target_pairs={{0,8},{8,16},{16,24},{24,32},{32,40},{40,48},{48,56},{1,9},{9,17},... | collective-permute-start | bytes 1572872 | tf_op jit(solution)/shard_map/ppermute | solution.py:370
  24.1 25.2 %all-to-all-start.1 = ((bf16[8,256,128]{2,1,0:T(8,128)(2,1)}), bf16[8,256,128]{2,1,0:T(8,128)(2,1)S(1)}, u32[]{:S(2)}, u32[]{:S(2)}) async-start(bf16[8,256,128]{2,1,0:T(8,128)(2,1)} %shard_map.119), calls=%async_computation.1 | async-start | bytes 1048576 | tf_op jit(solution)/shard_map/all_to_all | solution.py:339
  27.6 15.7 %collective-permute-start.3 = (bf16[128,1024]{1,0:T(8,128)(2,1)S(1)}, bf16[128,1024]{1,0:T(8,128)(2,1)S(1)}, u32[]{:S(2)}, u32[]{:S(2)}) collective-permute-start(bf16[128,1024]{1,0:T(8,128)(2,1)S(1)} %bitcast.22), channel_id=1, source_target_pairs={{0,2},{2,4},{4,6},{6,0},{1,3},{3,5},{5,7},{7,1},{8,10},{10,12},{12... | collective-permute-start | bytes 786440 | tf_op jit(solution)/shard_map/ppermute | solution.py:368
  29.5 19.6 %collective-permute-start.2 = (bf16[128,1024]{1,0:T(8,128)(2,1)S(1)}, bf16[128,1024]{1,0:T(8,128)(2,1)S(1)}, u32[]{:S(2)}, u32[]{:S(2)}) collective-permute-start(bf16[128,1024]{1,0:T(8,128)(2,1)S(1)} %bitcast.23), channel_id=1, source_target_pairs={{0,4},{2,6},{4,0},{6,2},{1,5},{3,7},{5,1},{7,3},{8,12},{10,14},{12... | collective-permute-start | bytes 786440 | tf_op jit(solution)/shard_map/ppermute | solution.py:368
  32.2 16.9 %collective-permute-start.1 = (bf16[128,1024]{1,0:T(8,128)(2,1)S(1)}, bf16[128,1024]{1,0:T(8,128)(2,1)S(1)}, u32[]{:S(2)}, u32[]{:S(2)}) collective-permute-start(bf16[128,1024]{1,0:T(8,128)(2,1)S(1)} %bitcast.24), channel_id=1, source_target_pairs={{0,6},{2,0},{4,2},{6,4},{1,7},{3,1},{5,3},{7,5},{8,14},{10,8},{12,... | collective-permute-start | bytes 786440 | tf_op jit(solution)/shard_map/ppermute | solution.py:368
  49.3 16.8 %copy-start.3 = (bf16[4,128,1024]{2,1,0:T(8,128)(2,1)}, bf16[4,128,1024]{2,1,0:T(8,128)(2,1)S(1)}, u32[]{:S(2)}) copy-start(bf16[4,128,1024]{2,1,0:T(8,128)(2,1)S(1)} %pad_maximum_fusion.refs_9_) | copy-start | bytes 3145732
  49.3 0.8 copy-start.2
  49.3 1.0 copy-start.4
  49.3 6.6 %collective-permute-start.4 = (bf16[4,128,1024]{2,1,0:T(8,128)(2,1)S(1)}, bf16[4,128,1024]{2,1,0:T(8,128)(2,1)S(1)}, u32[]{:S(2)}, u32[]{:S(2)}) collective-permute-start(bf16[4,128,1024]{2,1,0:T(8,128)(2,1)S(1)} %pad_maximum_fusion.refs_9_), channel_id=1, source_target_pairs={{0,1},{1,0},{2,3},{3,2},{4,5},{5,4},{6,7},{7,6},{8,9},{9,8},{10,11... | collective-permute-start | bytes 3145736 | tf_op jit(solution)/shard_map/ppermute | solution.py:376
  56.0 10.1 %copy-start.5 = (bf16[4,128,1024]{2,1,0:T(8,128)(2,1)}, bf16[4,128,1024]{2,1,0:T(8,128)(2,1)S(1)}, u32[]{:S(2)}) copy-start(bf16[4,128,1024]{2,1,0:T(8,128)(2,1)S(1)} %collective-permute-done.4.refs_10_) | copy-start | bytes 3145732
  73.1 18.0 %collective-permute-start.5 = (bf16[8,256,128]{2,1,0:T(8,128)(2,1)}, bf16[8,256,128]{2,1,0:T(8,128)(2,1)S(1)}, u32[]{:S(2)}, u32[]{:S(2)}) collective-permute-start(bf16[8,256,128]{2,1,0:T(8,128)(2,1)} %get-tuple-element.75), channel_id=1, source_target_pairs={{8,0},{16,8},{24,16},{32,24},{40,32},{48,40},{56,48},{9,1},{17,9},... | collective-permute-start | bytes 1572872 | tf_op jit(solution)/shard_map/ppermute | solution.py:390
  75.0 13.6 %collective-permute-start.6 = (bf16[32,1024]{1,0:T(8,128)(2,1)}, bf16[32,1024]{1,0:T(8,128)(2,1)S(1)}, u32[]{:S(2)}, u32[]{:S(2)}) collective-permute-start(bf16[32,1024]{1,0:T(8,128)(2,1)} %get-tuple-element.78), channel_id=1, source_target_pairs={{0,64},{64,128},{128,192},{192,0},{1,65},{65,129},{129,193},{193,1... | collective-permute-start | bytes 196616 | tf_op jit(solution)/shard_map/ppermute | solution.py:391
  77.2 11.4 %collective-permute-start.7 = (bf16[32,1024]{1,0:T(8,128)(2,1)}, bf16[32,1024]{1,0:T(8,128)(2,1)S(1)}, u32[]{:S(2)}, u32[]{:S(2)}) collective-permute-start(bf16[32,1024]{1,0:T(8,128)(2,1)} %get-tuple-element.79), channel_id=1, source_target_pairs={{0,128},{64,192},{128,0},{192,64},{1,129},{65,193},{129,1},{193,65... | collective-permute-start | bytes 196616 | tf_op jit(solution)/shard_map/ppermute | solution.py:391
  81.8 6.8 %collective-permute-start.8 = (bf16[32,1024]{1,0:T(8,128)(2,1)}, bf16[32,1024]{1,0:T(8,128)(2,1)S(1)}, u32[]{:S(2)}, u32[]{:S(2)}) collective-permute-start(bf16[32,1024]{1,0:T(8,128)(2,1)} %get-tuple-element.80), channel_id=1, source_target_pairs={{0,192},{64,0},{128,64},{192,128},{1,193},{65,1},{129,65},{193,129... | collective-permute-start | bytes 196616 | tf_op jit(solution)/shard_map/ppermute | solution.py:391
  88.6 0.6 copy-start.8
  88.6 0.6 copy-start.9
  88.6 0.6 copy-start.10
  91.1 0.8 copy-start.7
  94.4 3.7 %copy-start.11 = (bf16[8,32,128]{2,1,0:T(8,128)(2,1)S(1)}, bf16[8,32,128]{2,1,0:T(8,128)(2,1)}, u32[]{:S(2)}) copy-start(bf16[8,32,128]{2,1,0:T(8,128)(2,1)} %shard_map.125) | copy-start | bytes 196612
  94.4 28.6 %copy-start = (bf16[1024,1024]{1,0:T(8,128)(2,1)S(1)}, bf16[1024,1024]{1,0:T(8,128)(2,1)}, u32[]{:S(2)}) copy-start(bf16[1024,1024]{1,0:T(8,128)(2,1)} %refs_1_.1) | copy-start | bytes 6291460
  94.4 25.2 %all-to-all-start.3 = ((bf16[8,640,128]{2,1,0:T(8,128)(2,1)}), bf16[8,640,128]{2,1,0:T(8,128)(2,1)S(1)}, u32[]{:S(2)}, u32[]{:S(2)}) async-start(bf16[8,640,128]{2,1,0:T(8,128)(2,1)} %shard_map.124), calls=%async_computation.3 | async-start | bytes 2621440 | tf_op jit(solution)/shard_map/all_to_all | solution.py:339
  98.1 9.6 %collective-permute-start.9 = (bf16[8,32,128]{2,1,0:T(8,128)(2,1)S(1)}, bf16[8,32,128]{2,1,0:T(8,128)(2,1)}, u32[]{:S(2)}, u32[]{:S(2)}) collective-permute-start(bf16[8,32,128]{2,1,0:T(8,128)(2,1)S(1)} %copy-done.11), channel_id=1, source_target_pairs={{0,0},{1,32},{2,64},{3,96},{4,128},{5,160},{6,192},{7,224},{8,1},{... | collective-permute-start | bytes 196616 | tf_op jit(solution)/shard_map/ppermute | solution.py:405
  119.6 8.9 %all-to-all-start.4 = ((bf16[8,32,128]{2,1,0:T(8,128)(2,1)}), bf16[8,32,128]{2,1,0:T(8,128)(2,1)S(1)}, u32[]{:S(2)}, u32[]{:S(2)}) async-start(bf16[8,32,128]{2,1,0:T(8,128)(2,1)} %collective-permute-done.9), calls=%async_computation.4 | async-start | bytes 131072 | tf_op jit(solution)/shard_map/all_to_all | solution.py:339
